TPU v7x, 32 devices: a whole 2x2x4 slice. The times are simulated.
32 devices in a mesh: pair: 2 (over y), fsdp: 4 (over x, core), rep: 4 (over z).
Axes of the slice: x: 2, y: 2, z: 4, core: 2. Of those that a mesh axis runs over, the one named last changes fastest.
Arguments:
- tokens: bfloat16 [4096, 2048], P(('pair', 'fsdp', 'rep')), may hold values from -6 to 6
- cotangent: bfloat16 [4096, 2048], P(('pair', 'fsdp', 'rep')), may hold values from -6 to 6
- segment_ids: int32 [4096], P(('pair', 'fsdp', 'rep')), may hold values from 0 to 2, as said below
- positions: int32 [4096], P(('pair', 'fsdp', 'rep')), may hold values from 0 to 381, as said below
- q_weight: bfloat16 [2048, 2048], P('fsdp'), may hold values from -0.4375 to 0.4375
- k_weight: bfloat16 [2048, 512], P('fsdp'), may hold values from -0.4375 to 0.4375
- v_weight: bfloat16 [2048, 512], P('fsdp'), may hold values from -0.5 to 0.5
- o_weight: bfloat16 [2048, 2048], P('fsdp'), may hold values from -1 to 1
- attn_gain: bfloat16 [2048], P('fsdp'), may hold values from 0.5 to 1.5
- gate_up_weight: bfloat16 [2048, 16384], P('fsdp'), may hold values from -0.25 to 0.25
- down_weight: bfloat16 [8192, 2048], P('fsdp'), may hold values from -0.1875 to 0.1875
- mlp_gain: bfloat16 [2048], P('fsdp'), may hold values from 0.5 to 1.5
Outputs:
- out: bfloat16 [4096, 2048], P(('pair', 'fsdp', 'rep'))
- input_grad: bfloat16 [4096, 2048], P(('pair', 'fsdp', 'rep'))
- q_update: float32 [2048, 2048], P(('pair', 'fsdp'))
- k_update: float32 [2048, 512], P(('pair', 'fsdp'))
- v_grad: float32 [2048, 512], P(('pair', 'fsdp'))
- o_grad: float32 [2048, 2048], P(('pair', 'fsdp'))
- attn_gain_grad: float32 [2048], P(('pair', 'fsdp'))
- gate_up_grad: float32 [2048, 16384], P(('pair', 'fsdp'))
- down_grad: float32 [8192, 2048], P(('pair', 'fsdp'))
- mlp_gain_grad: float32 [2048], P(('pair', 'fsdp'))
Inputs may be any that keep to these rules, and one draw needn't show every extreme that they name: `segment_ids`: in each group the 128 prompt tokens have segment 0; the 128 continuation tokens fill aligned windows of 128 tokens, each split into two continuations of one token or more, numbered 1 to 2 in order. A group's prompt has consecutive positions from a start below 128; each continuation's positions run consecutively from the prompt's last position plus one.
All inputs are finite; a program needn't handle non-finite values.
Results may differ from a plain program's by a relative error of at most 0.022.
Values may be sent and summed in bfloat16 or wider, within the bound.
No kernel may reach another device: no remote copies, remote signals or barrier semaphores. Data moves between devices by JAX's collectives and lax.ppermute only.
A program may use at most 512 MiB of HBM per device.

v0:
```python
import jax
import jax.numpy as jnp
from jax import lax
from jax.sharding import PartitionSpec as P

D = 2048
FF = 8192
HEADS = 32
KV_HEADS = 8
HEAD = 64


EPS = 1e-05
THETA = 10000000.0
SCALE = 0.015625
RESID = 0.22
TAU = 3.0


def shifted(x, axis, by):
    devices = lax.axis_size(axis)
    pairs = [(i, i + by) for i in range(devices) if 0 <= i + by < devices]
    return lax.ppermute(x, axis, pairs)


def rope_tables(positions, half):
    inverse = THETA ** (-(jnp.arange(half, dtype=jnp.float32) * 2.0 / (2 * half)))
    angle = positions.astype(jnp.float32)[:, None] * inverse[None, :]
    return (jnp.cos(angle), jnp.sin(angle))


def rotate(vectors, cosine, sine, sign):
    half = vectors.shape[-1] // 2
    first = vectors[..., :half]
    second = vectors[..., half:]
    cos_b = cosine[:, None, :]
    sin_b = sign * sine[:, None, :]
    return jnp.concatenate(
        [first * cos_b - second * sin_b, second * cos_b + first * sin_b], axis=-1
    )


def outer(left, right):
    return lax.dot_general(
        left, right, (((0,), (0,)), ((), ())), preferred_element_type=jnp.float32
    )


def times_t(left, right):
    return lax.dot_general(
        left, right, (((1,), (1,)), ((), ())), preferred_element_type=jnp.float32
    )


def norm_back(grad_normed, unit, inv_scale, gain):
    scaled = grad_normed * gain
    grad_in = inv_scale * (scaled - unit * jnp.mean(scaled * unit, axis=-1, keepdims=True))
    return (grad_in, jnp.sum(grad_normed * unit, axis=0))


def replicas(parts):
    return (
        lax.psum(parts[0].astype(jnp.bfloat16), "rep").astype(jnp.float32),
        lax.psum(parts[1].astype(jnp.bfloat16), "rep").astype(jnp.float32),
        lax.psum(parts[2].astype(jnp.bfloat16), "rep").astype(jnp.float32),
        lax.psum(parts[3].astype(jnp.bfloat16), "rep").astype(jnp.float32),
        lax.psum(parts[4].astype(jnp.bfloat16), "rep").astype(jnp.float32),
        lax.psum(parts[5].astype(jnp.bfloat16), "rep").astype(jnp.float32),
        lax.psum(parts[6].astype(jnp.bfloat16), "rep").astype(jnp.float32),
        lax.psum(parts[7].astype(jnp.bfloat16), "rep").astype(jnp.float32),
    )


def on_device(
    tokens,
    cotangent,
    segment_ids,
    positions,
    q_weight,
    k_weight,
    v_weight,
    o_weight,
    attn_gain,
    gate_up_weight,
    down_weight,
    mlp_gain,
):
    tok_rows = tokens.shape[0]
    kv_width = KV_HEADS * HEAD
    group_size = HEADS // KV_HEADS
    inputs = tokens.astype(jnp.float32)
    w_query, w_key, w_value, w_out, gain_attn = (
        lax.all_gather(q_weight, "fsdp", axis=0, tiled=True),
        lax.all_gather(k_weight, "fsdp", axis=0, tiled=True),
        lax.all_gather(v_weight, "fsdp", axis=0, tiled=True),
        lax.all_gather(o_weight, "fsdp", axis=0, tiled=True),
        lax.all_gather(attn_gain, "fsdp", axis=0, tiled=True),
    )
    gain_one = gain_attn.astype(jnp.float32)
    inv_one = lax.rsqrt(jnp.mean(inputs * inputs, axis=-1, keepdims=True) + EPS)
    unit_one = inputs * inv_one
    normed = (unit_one * gain_one).astype(jnp.bfloat16)
    query_lin = jnp.dot(normed, w_query, preferred_element_type=jnp.float32)
    key_lin = jnp.dot(normed, w_key, preferred_element_type=jnp.float32)
    value_tok = jnp.dot(normed, w_value, preferred_element_type=jnp.float32).astype(jnp.bfloat16)
    cosine, sine = rope_tables(positions, HEAD // 2)
    query_rot = (
        rotate(query_lin.reshape(tok_rows, HEADS, HEAD), cosine, sine, 1.0)
        .astype(jnp.bfloat16)
        .reshape(tok_rows, KV_HEADS, group_size, HEAD)
    )
    key_rot = (
        rotate(key_lin.reshape(tok_rows, KV_HEADS, HEAD), cosine, sine, 1.0)
        .astype(jnp.bfloat16)
        .reshape(tok_rows, kv_width)
    )
    remote = shifted(jnp.concatenate([key_rot, value_tok], axis=1), "pair", 1)
    all_keys = jnp.concatenate([remote[:, :kv_width], key_rot], axis=0).reshape(
        2 * tok_rows, KV_HEADS, HEAD
    )
    all_values = jnp.concatenate([remote[:, kv_width:], value_tok], axis=0).reshape(
        2 * tok_rows, KV_HEADS, HEAD
    )
    partner = lax.axis_index("pair") == 1
    same_doc = (segment_ids[None, :] == 0) | (segment_ids[None, :] == segment_ids[:, None])
    local_vis = same_doc & (positions[None, :] <= positions[:, None])
    visible = jnp.concatenate([jnp.broadcast_to(partner, (tok_rows, tok_rows)), local_vis], axis=1)
    scores = (
        jnp.einsum("qgjd,kgd->gjqk", query_rot, all_keys, preferred_element_type=jnp.float32)
        * SCALE
    )
    masked = jnp.where(visible[None, None], scores, -jnp.inf)
    peak = jnp.max(masked, axis=3, keepdims=True)
    exp_scores = jnp.exp(masked - peak)
    row_total = jnp.sum(exp_scores, axis=3, keepdims=True)
    log_total = peak + jnp.log(row_total)
    probs_low = (exp_scores / row_total).astype(jnp.bfloat16)
    top_local = jnp.max(peak, axis=(2, 3)).reshape(HEADS)
    attended = (
        jnp.einsum("gjqk,kgd->qgjd", probs_low, all_values, preferred_element_type=jnp.float32)
        .reshape(tok_rows, D)
        .astype(jnp.bfloat16)
    )
    middle = inputs + RESID * jnp.dot(attended, w_out, preferred_element_type=jnp.float32)
    w_gate_up, w_down, gain_mlp = (
        lax.all_gather(gate_up_weight, "fsdp", axis=0, tiled=True),
        lax.all_gather(down_weight, "fsdp", axis=0, tiled=True),
        lax.all_gather(mlp_gain, "fsdp", axis=0, tiled=True),
    )
    gain_two = gain_mlp.astype(jnp.float32)
    inv_two = lax.rsqrt(jnp.mean(middle * middle, axis=-1, keepdims=True) + EPS)
    unit_two = middle * inv_two
    normed_mlp = (unit_two * gain_two).astype(jnp.bfloat16)
    gate_up = jnp.dot(normed_mlp, w_gate_up, preferred_element_type=jnp.float32)
    gate = gate_up[:, :FF]
    up_part = gate_up[:, FF:]
    sigma = jax.nn.sigmoid(gate)
    silu_gate = gate * sigma
    hidden = (silu_gate * up_part).astype(jnp.bfloat16)
    result = (middle + RESID * jnp.dot(hidden, w_down, preferred_element_type=jnp.float32)).astype(
        jnp.bfloat16
    )
    peaks = lax.pmax(top_local, ("pair", "fsdp", "rep"))
    grad_out = cotangent.astype(jnp.float32)
    grad_branch = (RESID * grad_out).astype(jnp.bfloat16)
    grad_hidden = times_t(grad_branch, w_down)
    grad_gate_up = jnp.concatenate(
        [grad_hidden * up_part * sigma * (1.0 + gate * (1.0 - sigma)), grad_hidden * silu_gate],
        axis=1,
    ).astype(jnp.bfloat16)
    grad_normed_mlp = times_t(grad_gate_up, w_gate_up)
    grad_mid_norm, gain_two_grad = norm_back(grad_normed_mlp, unit_two, inv_two, gain_two)
    grad_middle = grad_out + grad_mid_norm
    grad_attn_branch = (RESID * grad_middle).astype(jnp.bfloat16)
    grad_attended = (
        times_t(grad_attn_branch, w_out)
        .astype(jnp.bfloat16)
        .reshape(tok_rows, KV_HEADS, group_size, HEAD)
    )
    scores_again = (
        jnp.einsum("qgjd,kgd->gjqk", query_rot, all_keys, preferred_element_type=jnp.float32)
        * SCALE
    )
    probs_full = jnp.where(visible[None, None], jnp.exp(scores_again - log_total), 0.0)
    grad_probs = jnp.einsum(
        "qgjd,kgd->gjqk", grad_attended, all_values, preferred_element_type=jnp.float32
    )
    delta = jnp.sum(probs_full * grad_probs, axis=3, keepdims=True)
    grad_scores = (probs_full * (grad_probs - delta) * SCALE).astype(jnp.bfloat16)
    grad_query = jnp.einsum(
        "gjqk,kgd->qgjd", grad_scores, all_keys, preferred_element_type=jnp.float32
    ).reshape(tok_rows, HEADS, HEAD)
    grad_keys = jnp.einsum(
        "gjqk,qgjd->kgd", grad_scores, query_rot, preferred_element_type=jnp.float32
    ).reshape(2 * tok_rows, kv_width)
    grad_values = jnp.einsum(
        "gjqk,qgjd->kgd", probs_low, grad_attended, preferred_element_type=jnp.float32
    ).reshape(2 * tok_rows, kv_width)
    returned = shifted(
        jnp.concatenate([grad_keys[:tok_rows], grad_values[:tok_rows]], axis=1).astype(
            jnp.bfloat16
        ),
        "pair",
        -1,
    ).astype(jnp.float32)
    grad_key_rot = grad_keys[tok_rows:] + returned[:, :kv_width]
    grad_value = (grad_values[tok_rows:] + returned[:, kv_width:]).astype(jnp.bfloat16)
    grad_query_lin = (
        rotate(grad_query, cosine, sine, -1.0).reshape(tok_rows, D).astype(jnp.bfloat16)
    )
    grad_key_lin = (
        rotate(grad_key_rot.reshape(tok_rows, KV_HEADS, HEAD), cosine, sine, -1.0)
        .reshape(tok_rows, kv_width)
        .astype(jnp.bfloat16)
    )
    grad_normed = (
        times_t(grad_query_lin, w_query)
        + times_t(grad_key_lin, w_key)
        + times_t(grad_value, w_value)
    )
    grad_in_norm, gain_one_grad = norm_back(grad_normed, unit_one, inv_one, gain_one)
    input_grad = (grad_middle + grad_in_norm).astype(jnp.bfloat16)
    down_part = lax.psum_scatter(
        outer(hidden, grad_branch).astype(jnp.bfloat16),
        ("pair", "fsdp"),
        scatter_dimension=0,
        tiled=True,
    ).astype(jnp.float32)
    gate_up_part = lax.psum_scatter(
        outer(normed_mlp, grad_gate_up).astype(jnp.bfloat16),
        ("pair", "fsdp"),
        scatter_dimension=0,
        tiled=True,
    ).astype(jnp.float32)
    query_grad = outer(normed, grad_query_lin)
    key_grad = outer(normed, grad_key_lin)
    value_grad = outer(normed, grad_value)
    out_grad_term = outer(attended, grad_attn_branch)
    attn_parts = (
        lax.psum_scatter(
            query_grad.astype(jnp.bfloat16), ("pair", "fsdp"), scatter_dimension=0, tiled=True
        ).astype(jnp.float32),
        lax.psum_scatter(
            key_grad.astype(jnp.bfloat16), ("pair", "fsdp"), scatter_dimension=0, tiled=True
        ).astype(jnp.float32),
        lax.psum_scatter(
            value_grad.astype(jnp.bfloat16), ("pair", "fsdp"), scatter_dimension=0, tiled=True
        ).astype(jnp.float32),
        lax.psum_scatter(
            out_grad_term.astype(jnp.bfloat16), ("pair", "fsdp"), scatter_dimension=0, tiled=True
        ).astype(jnp.float32),
        lax.psum_scatter(
            gain_one_grad.astype(jnp.bfloat16), ("pair", "fsdp"), scatter_dimension=0, tiled=True
        ).astype(jnp.float32),
        lax.psum_scatter(
            gain_two_grad.astype(jnp.bfloat16), ("pair", "fsdp"), scatter_dimension=0, tiled=True
        ).astype(jnp.float32),
    )
    summed = replicas(
        (
            attn_parts[0],
            attn_parts[1],
            attn_parts[2],
            attn_parts[3],
            attn_parts[4],
            attn_parts[5],
            down_part,
            gate_up_part,
        )
    )
    query_sum, key_sum, value_sum, out_sum, gain_one_sum, gain_two_sum, down_sum, gate_up_sum = (
        summed
    )
    factor = TAU / jnp.maximum(peaks, TAU)
    q_update = query_sum * jnp.repeat(factor, HEAD)[None, :]
    k_update = (
        key_sum * jnp.repeat(jnp.min(factor.reshape(KV_HEADS, group_size), axis=1), HEAD)[None, :]
    )
    return (
        result,
        input_grad,
        q_update,
        k_update,
        value_sum,
        out_sum,
        gain_one_sum,
        gate_up_sum,
        down_sum,
        gain_two_sum,
    )


def solution(mesh):
    return jax.shard_map(
        on_device,
        mesh=mesh,
        in_specs=(
            P(("pair", "fsdp", "rep"), None),
            P(("pair", "fsdp", "rep"), None),
            P(("pair", "fsdp", "rep")),
            P(("pair", "fsdp", "rep")),
            P("fsdp", None),
            P("fsdp", None),
            P("fsdp", None),
            P("fsdp", None),
            P("fsdp"),
            P("fsdp", None),
            P("fsdp", None),
            P("fsdp"),
        ),
        out_specs=(
            P(("pair", "fsdp", "rep"), None),
            P(("pair", "fsdp", "rep"), None),
            P(("pair", "fsdp"), None),
            P(("pair", "fsdp"), None),
            P(("pair", "fsdp"), None),
            P(("pair", "fsdp"), None),
            P(("pair", "fsdp")),
            P(("pair", "fsdp"), None),
            P(("pair", "fsdp"), None),
            P(("pair", "fsdp")),
        ),
        check_vma=False,
    )
```

profile of v0, /device:TPU:0, one launch (start us, length us, event | category | flops | bytes accessed | tf_op | source)
XLA Modules:
  0.0 2249.1 jit_solution(9477198817957616256)
XLA Ops:
  18.4 16.4 all-gather.9.cloned.1.call-done
  37.6 21.4 all-gather.11.cloned.1.call-done
  70.8 48.1 %all-gather.13.cloned.1.call-done = bf16[2048,2048]{1,0:T(8,128)(2,1)} async-done(((bf16[512,2048]{1,0:T(8,128)(2,1)}), bf16[2048,2048]{1,0:T(8,128)(2,1)}) %all-gather.13.cloned.1.call-update) | async-done | bytes 8388624 | tf_op jit(solution)/shard_map/all_gather | solution.py:93
  131.4 47.1 %all-gather.15.cloned.1.call-done = bf16[2048,2048]{1,0:T(8,128)(2,1)} async-done(((bf16[512,2048]{1,0:T(8,128)(2,1)}), bf16[2048,2048]{1,0:T(8,128)(2,1)}) %all-gather.15.cloned.1.call-update) | async-done | bytes 8388624 | tf_op jit(solution)/shard_map/all_gather | solution.py:96
  184.0 388.7 %all-gather.17.cloned.1.call-done = bf16[2048,16384]{1,0:T(8,128)(2,1)} async-done(((bf16[512,16384]{1,0:T(8,128)(2,1)}), bf16[2048,16384]{1,0:T(8,128)(2,1)}) %all-gather.17.cloned.1.call-update) | async-done | bytes 67108880 | tf_op jit(solution)/shard_map/all_gather | solution.py:146
  572.7 37.7 %fusion.65 = f32[128,16384]{1,0:T(8,128)} fusion(bf16[2048,16384]{1,0:T(8,128)(2,1)} %all-gather.17.cloned.1.call-done, f32[128,2048]{1,0:T(8,128)S(1)} %get-tuple-element.47, f32[2048]{0:T(1024)S(1)} %bitcast.144, f32[128]{0:T(128)S(1)} %add_rsqrt_fusion), kind=kOutput, calls=%fused_computation.121 | convolution fusion | flops 8590721024 | bytes 76554752 | tf_op jit(solution)/shard_map/dot_general | solution.py:154
  610.5 165.2 %all-gather.19.cloned.1.call-done = bf16[8192,2048]{1,0:T(8,128)(2,1)} async-done(((bf16[2048,2048]{1,0:T(8,128)(2,1)}), bf16[8192,2048]{1,0:T(8,128)(2,1)}) %all-gather.19.cloned.1.call-update) | async-done | bytes 33554448 | tf_op jit(solution)/shard_map/all_gather | solution.py:147
  775.7 21.0 multiply_convert_fusion.1
  796.7 30.7 %multiply_reduce_fusion = (bf16[2048]{0:T(1024)(128)(2,1)}, f32[128]{0:T(128)S(1)}, f32[128,2048]{1,0:T(8,128)}) fusion(f32[128,2048]{1,0:T(8,128)S(1)} %get-tuple-element.47, f32[128]{0:T(128)S(1)} %add_rsqrt_fusion, f32[2048]{0:T(1024)S(1)} %bitcast.145, bf16[2048,16384]{1,0:T(8,128)(2,1)} %all-gather.17.cloned.1.call-done, ...), kind=kOutput, calls=%fused_computation.67 | convolution fusion | flops 8599894016 | bytes 73413632 | tf_op jit(solution)/shard_map/dot_general | solution.py:50
  844.8 9.4 fusion.33
  879.8 9.4 fusion.16
  897.2 15.7 convolution_convert_fusion.1
  913.6 27.8 %convolution_convert_fusion = bf16[2048,16384]{1,0:T(8,128)(2,1)} fusion(bf16[128,8192]{1,0:T(8,128)(2,1)} %get-tuple-element.27, bf16[128,8192]{1,0:T(8,128)(2,1)} %get-tuple-element.26, f32[128,2048]{1,0:T(8,128)S(1)} %get-tuple-element.47, f32[2048]{0:T(1024)S(1)} %bitcast.147, f32[128]{0:T(128)S(1)} %copy-done.15), kind=kOutput, calls=%fused_computation.1 | convolution fusion | flops 8632664064 | bytes 72360448 | tf_op jit(solution)/shard_map/dot_general | solution.py:44
  941.5 12.6 reduce-scatter.9.cloned.1.call-done
  954.0 75.6 %reduce-scatter.13.cloned.1.call-done = bf16[256,2048]{1,0:T(8,128)(2,1)} async-done(((bf16[2048,2048]{1,0:T(8,128)(2,1)}), bf16[256,2048]{1,0:T(8,128)(2,1)}) %reduce-scatter.13.cloned.1.call-update) | async-done | bytes 1048592 | tf_op jit(solution)/shard_map/reduce_scatter | solution.py:249
  1029.6 75.4 %reduce-scatter.7.cloned.1.call-done = bf16[256,2048]{1,0:T(8,128)(2,1)} async-done(((bf16[2048,2048]{1,0:T(8,128)(2,1)}), bf16[256,2048]{1,0:T(8,128)(2,1)}) %reduce-scatter.7.cloned.1.call-update) | async-done | bytes 1048592 | tf_op jit(solution)/shard_map/reduce_scatter | solution.py:240
  1105.0 209.1 %reduce-scatter.17.cloned.1.call-done = bf16[1024,2048]{1,0:T(8,128)(2,1)} async-done(((bf16[8192,2048]{1,0:T(8,128)(2,1)}), bf16[1024,2048]{1,0:T(8,128)(2,1)}) %reduce-scatter.17.cloned.1.call-update) | async-done | bytes 4194320 | tf_op jit(solution)/shard_map/reduce_scatter | solution.py:223
  1314.1 387.4 %reduce-scatter.15.cloned.1.call-done = bf16[256,16384]{1,0:T(8,128)(2,1)} async-done(((bf16[2048,16384]{1,0:T(8,128)(2,1)}), bf16[256,16384]{1,0:T(8,128)(2,1)}) %reduce-scatter.15.cloned.1.call-update) | async-done | bytes 8388624 | tf_op jit(solution)/shard_map/reduce_scatter | solution.py:229
  1703.5 45.5 %pmax.7 = f32[32]{0:T(128)S(1)} all-reduce(f32[32]{0:T(128)S(1)} %reshape.194), channel_id=1, replica_groups=mesh['pair'=2,'fsdp'=4,'rep'=4] {'pair','fsdp','rep'}, use_global_device_ids=true, to_apply=%region_10.11 | all-reduce | flops 32 | bytes 256 | tf_op jit(solution)/shard_map/pmax | solution.py:163
  1756.0 14.2 fusion.13
  1772.8 13.8 all-reduce.3
  1786.7 15.5 all-reduce.4
  1804.5 412.3 %all-reduce.8.cloned.1.call-done = (bf16[256,2048]{1,0:T(8,128)(2,1)}, bf16[256,512]{1,0:T(8,128)(2,1)}, bf16[256,512]{1,0:T(8,128)(2,1)}, bf16[256,2048]{1,0:T(...) async-done(((bf16[256,2048]{1,0:T(8,128)(2,1)}, bf16[256,512]{1,0:T(8,128)(2,1)}, bf16[256,512]{1,0:T(8,128)(2,1)}, bf16[256,2048]{1,0:T(8,128)(2,1)}, ...) | async-done | bytes 15204368 | tf_op jit(solution)/shard_map/psum | solution.py:63
  2228.1 11.6 convert_element_type.183
  (175 shorter events, 121.8 us)
Async XLA Ops:
  7.2 27.7 %all-gather.9.cloned.1.call-start = ((), (), s32[]{:S(2)}) async-start(), calls=%async_computation.6 | async-start | bytes 2621440 | tf_op jit(solution)/shard_map/all_gather | solution.py:94
  7.9 51.1 %all-gather.11.cloned.1.call-start = ((), (), s32[]{:S(2)}) async-start(), calls=%async_computation.7 | async-start | bytes 2621440 | tf_op jit(solution)/shard_map/all_gather | solution.py:95
  8.7 110.2 %all-gather.13.cloned.1.call-start = ((), (), s32[]{:S(2)}) async-start(), calls=%async_computation.8 | async-start | bytes 10485760 | tf_op jit(solution)/shard_map/all_gather | solution.py:93
  9.4 169.2 %all-gather.15.cloned.1.call-start = ((), (), s32[]{:S(2)}) async-start(), calls=%async_computation.9 | async-start | bytes 10485760 | tf_op jit(solution)/shard_map/all_gather | solution.py:96
  10.0 562.8 %all-gather.17.cloned.1.call-start = ((), (), s32[]{:S(2)}) async-start(), calls=%async_computation.10 | async-start | bytes 83886080 | tf_op jit(solution)/shard_map/all_gather | solution.py:146
  10.6 765.1 %all-gather.19.cloned.1.call-start = ((), (), s32[]{:S(2)}) async-start(), calls=%async_computation.11 | async-start | bytes 41943040 | tf_op jit(solution)/shard_map/all_gather | solution.py:147
  11.2 53.4 %copy-start.29 = (s32[128]{0:T(128)S(1)}, s32[128]{0:T(128)}, u32[]{:S(2)}) copy-start(s32[128]{0:T(128)} %param.14) | copy-start | bytes 1540
  11.2 53.4 %copy-start.31 = (bf16[512]{0:T(512)(128)(2,1)S(1)}, bf16[512]{0:T(512)(128)(2,1)}, u32[]{:S(2)}) copy-start(bf16[512]{0:T(512)(128)(2,1)} %param.23) | copy-start | bytes 3076
  11.2 930.3 %reduce-scatter.11.cloned.1.call-start = ((), (), s32[]{:S(2)}) async-start(), calls=%async_computation.14 | async-start | bytes 2359296 | tf_op jit(solution)/shard_map/reduce_scatter | solution.py:246
  17.7 101.2 %copy-start.23 = (f32[128]{0:T(128)}, f32[128]{0:T(128)S(1)}, u32[]{:S(2)}) copy-start(f32[128]{0:T(128)S(1)} %add_rsqrt_fusion.1) | copy-start | bytes 1540
  18.4 107.2 %copy-start.12 = (f32[128,32]{0,1:T(8,128)}, f32[128,32]{0,1:T(8,128)S(1)}, u32[]{:S(2)}) copy-start(f32[128,32]{0,1:T(8,128)S(1)} %get-tuple-element.43) | copy-start | bytes 49156
  37.5 88.4 %copy-start.10 = (bf16[128,8,64]{0,2,1:T(8,128)(2,1)}, bf16[128,8,64]{0,2,1:T(8,128)(2,1)S(1)}, u32[]{:S(2)}) copy-start(bf16[128,8,64]{0,2,1:T(8,128)(2,1)S(1)} %maximum_convert_fusion) | copy-start | bytes 393220
  61.1 9.3 collective-permute-start
  69.9 58.7 %copy-start.16 = (pred[128,256]{0,1:T(8,128)(4,1)}, pred[128,256]{0,1:T(8,128)(4,1)S(1)}, u32[]{:S(2)}) copy-start(pred[128,256]{0,1:T(8,128)(4,1)S(1)} %concatenate.46) | copy-start | bytes 98308
  70.6 55.3 %copy-start.21 = (bf16[128,512]{0,1:T(8,128)(2,1)}, bf16[128,512]{0,1:T(8,128)(2,1)S(1)}, u32[]{:S(2)}) copy-start(bf16[128,512]{0,1:T(8,128)(2,1)S(1)} %copy.54) | copy-start | bytes 393220
  183.4 644.1 %copy-start.14 = (f32[128]{0:T(128)}, f32[128]{0:T(128)S(1)}, u32[]{:S(2)}) copy-start(f32[128]{0:T(128)S(1)} %add_rsqrt_fusion) | copy-start | bytes 1540
  572.7 203.0 %copy-start.6 = (bf16[128,2048]{1,0:T(8,128)(2,1)S(1)}, bf16[128,2048]{1,0:T(8,128)(2,1)}, u32[]{:S(2)}) copy-start(bf16[128,2048]{1,0:T(8,128)(2,1)} %param.13) | copy-start | bytes 1572868
  855.3 10.4 collective-permute-start.1
  869.3 84.7 %reduce-scatter.9.cloned.1.call-start = ((), (), s32[]{:S(2)}) async-start(), calls=%async_computation.13 | async-start | bytes 2359296 | tf_op jit(solution)/shard_map/reduce_scatter | solution.py:243
  873.0 156.6 %reduce-scatter.13.cloned.1.call-start = ((), (), s32[]{:S(2)}) async-start(), calls=%async_computation.15 | async-start | bytes 9437184 | tf_op jit(solution)/shard_map/reduce_scatter | solution.py:249
  878.8 226.2 %reduce-scatter.7.cloned.1.call-start = ((), (), s32[]{:S(2)}) async-start(), calls=%async_computation.12 | async-start | bytes 9437184 | tf_op jit(solution)/shard_map/reduce_scatter | solution.py:240
  897.2 416.9 %reduce-scatter.17.cloned.1.call-start = ((), (), s32[]{:S(2)}) async-start(), calls=%async_computation.17 | async-start | bytes 37748736 | tf_op jit(solution)/shard_map/reduce_scatter | solution.py:223
  913.0 788.5 %reduce-scatter.15.cloned.1.call-start = ((), (), s32[]{:S(2)}) async-start(), calls=%async_computation.16 | async-start | bytes 75497472 | tf_op jit(solution)/shard_map/reduce_scatter | solution.py:229
  941.4 1275.4 %all-reduce.8.cloned.1.call-start = ((), (), s32[]{:S(2)}) async-start(), calls=%async_computation.18 | async-start | bytes 30408704 | tf_op jit(solution)/shard_map/psum | solution.py:63
  (25 other events, 122.8 us)
Sparse Core Ops, SparseCore 0:
  9.5 25.2 all-gather.8
  36.4 22.5 all-gather.10
  60.6 58.2 all-gather.12
  120.3 58.2 all-gather.14
  180.0 392.6 all-gather.16
  574.2 201.4 all-gather.18
  869.4 40.1 reduce-scatter.10
  912.9 41.0 reduce-scatter.8
  958.1 71.4 reduce-scatter.12
  1033.5 71.4 reduce-scatter.6
  1108.6 205.4 reduce-scatter.16
  1317.5 383.9 reduce-scatter.14
  1704.8 512.0 all-reduce.7
where the time goes:
time: 2260 us; the launch traced here: 2250 us
  waiting for transfers between devices  1870 us (83%)
  matrix products  223 us (10%)
  blocking collectives  86.2 us (4%)
  other arithmetic  37.4 us (2%)
    psum x1, waiting for transfers between devices, replicas(): lax.psum(parts[0].astype(jnp.bfloat16), 'rep').astype(jnp.float32)  412 us
    all_gather x1, waiting for transfers between devices, on_device(): lax.all_gather(gate_up_weight, 'fsdp', axis=0, tiled=True)  389 us
    reduce_scatter x1, waiting for transfers between devices, on_device(): lax.psum_scatter(outer(normed_mlp, grad_gate_up).astype(jnp.bfloat16), ('...  387 us
    reduce_scatter x1, waiting for transfers between devices, on_device(): lax.psum_scatter(outer(hidden, grad_branch).astype(jnp.bfloat16), ('pair'...  209 us
    all_gather x1, waiting for transfers between devices, on_device(): lax.all_gather(down_weight, 'fsdp', axis=0, tiled=True)  165 us
    reduce_scatter x1, waiting for transfers between devices, on_device(): lax.psum_scatter(out_grad_term.astype(jnp.bfloat16), ('pair', 'fsdp'), sc...  75.6 us
    reduce_scatter x1, waiting for transfers between devices, on_device(): lax.psum_scatter(query_grad.astype(jnp.bfloat16), ('pair', 'fsdp'), scatt...  75.4 us
    dot_general x6, matrix products, times_t(): lax.dot_general(left, right, (((1,), (1,)), ((), ())), preferred_element_...  67.1 us
  transfers between devices with their start and end apart: 15, of which 14 were waited for; matrix products, arithmetic and copies ran while one was open for 7% of the time, Pallas kernels for 0%

commit v1 on v0

v1 whole, which is shorter than its diff:
```python
import jax
import jax.numpy as jnp
from jax import lax
from jax.sharding import PartitionSpec as P

D = 2048
FF = 8192
HEADS = 32
KV_HEADS = 8
HEAD = 64
GROUP = HEADS // KV_HEADS

EPS = 1e-05
THETA = 10000000.0
SCALE = 0.015625
RESID = 0.22
TAU = 3.0

PLANE = ("pair", "fsdp")
F32 = jnp.float32
BF16 = jnp.bfloat16
ORDER = (0, 4, 2, 6, 1, 5, 3, 7)


def dot(left, right):
    return jnp.dot(left, right, preferred_element_type=F32)


def outer(left, right):
    return lax.dot_general(left, right, (((0,), (0,)), ((), ())), preferred_element_type=F32)


def times_t(left, right):
    return lax.dot_general(left, right, (((1,), (1,)), ((), ())), preferred_element_type=F32)


def swap(x, mask, devices=8):
    return lax.ppermute(x, PLANE, [(i, i ^ mask) for i in range(devices)])


def rope_tables(positions, half):
    inverse = THETA ** (-(jnp.arange(half, dtype=F32) * 2.0 / (2 * half)))
    angle = positions.astype(F32)[..., None] * inverse
    return (jnp.cos(angle), jnp.sin(angle))


def rotate(vectors, cosine, sine, sign):
    half = vectors.shape[-1] // 2
    first = vectors[..., :half]
    second = vectors[..., half:]
    cos_b = cosine[..., None, :]
    sin_b = sign * sine[..., None, :]
    return jnp.concatenate(
        [first * cos_b - second * sin_b, second * cos_b + first * sin_b], axis=-1
    )


class Plane:
    def __init__(self):
        self.np = lax.axis_size("pair")
        self.nf = lax.axis_size("fsdp")
        self.nr = lax.axis_size("rep")
        self.n = self.np * self.nf
        self.p = lax.axis_index("pair")
        self.f = lax.axis_index("fsdp")
        self.unit = self.np * self.f + self.p
        self.cube = self.np == 2 and self.nf == 4

    def gather(self, x):
        if not self.cube:
            return lax.all_gather(x, PLANE, axis=0, tiled=True)
        near = [x] + [swap(x, m) for m in ORDER[1:4]]
        far = [swap(piece, 1) for piece in near]
        return jnp.concatenate(near + far, axis=0)

    def scatter(self, left, right, product):
        rows = left.shape[0]
        if not self.cube:
            whole = product(left, right).astype(BF16)
            return lax.psum_scatter(whole, PLANE, scatter_dimension=0, tiled=True).astype(F32)
        half = rows // 2
        far = swap(product(left[half:], right).astype(BF16), 1)
        near = product(left[:half], right) + far.astype(F32)
        size = half // 4
        total = near[:size]
        for i in (1, 2, 3):
            piece = near[i * size : (i + 1) * size].astype(BF16)
            total = total + swap(piece, ORDER[i]).astype(F32)
        return total

    def groups(self, x):
        if self.cube:
            return x.reshape((self.nf, -1) + x.shape[1:])
        y = x.reshape((self.np, self.nf, -1) + x.shape[1:])
        return jnp.swapaxes(y, 0, 1).reshape((self.nf, -1) + x.shape[1:])

    def rows(self, x):
        if self.cube:
            return x.reshape((-1,) + x.shape[2:])
        y = x.reshape((self.nf, self.np, -1) + x.shape[2:])
        return jnp.swapaxes(y, 0, 1).reshape((-1,) + x.shape[2:])

    def reshard(self, columns):
        if not self.cube:
            parts = jnp.stack([columns(self.np * i + self.p) for i in range(self.nf)])
            got = lax.all_to_all(parts, "fsdp", 0, 0, tiled=True)
            return got.reshape((-1,) + got.shape[2:])
        own = columns(self.unit)
        rows = own.shape[0]
        out = jnp.zeros((self.nf * rows,) + own.shape[1:], own.dtype)
        out = lax.dynamic_update_slice(out, own, (self.f * rows, 0))
        for k in (1, 2, 3):
            other = self.f ^ k
            got = swap(columns(self.np * other + self.p), k)
            out = lax.dynamic_update_slice(out, got, (other * rows, 0))
        return out

    def by_unit(self, x, axis):
        shape = x.shape
        y = x.reshape(shape[:axis] + (self.np, self.nf) + shape[axis + 1 :])
        return jnp.swapaxes(y, axis, axis + 1).reshape(shape)

    def sum_rows(self, term):
        rows, width = term.shape
        each = rows // (self.n * self.nr)
        split = term.astype(BF16).reshape(self.n, self.nr, each, width)
        mine = lax.psum_scatter(jnp.swapaxes(split, 0, 1), "rep", scatter_dimension=0)
        moved = lax.all_to_all(mine, PLANE, 0, 0, tiled=True)
        full = lax.all_gather(moved, "rep", axis=0)
        return jnp.swapaxes(self.by_unit(full, 1), 1, 2)

    def sum_units(self, term):
        mine = lax.psum_scatter(term.astype(BF16), "rep", scatter_dimension=0, tiled=True)
        pairs = []
        for p in range(self.np):
            for f in range(self.nf):
                pairs.append((p * self.nf + f, self.np * f + p))
        moved = lax.ppermute(mine, PLANE, pairs)
        return lax.all_gather(moved, "rep", axis=0, tiled=True).astype(F32)


def norm_back(grad_normed, unit, inv_scale, gain):
    scaled = grad_normed * gain
    grad_in = inv_scale * (scaled - unit * jnp.mean(scaled * unit, axis=-1, keepdims=True))
    return (grad_in, jnp.sum(grad_normed * unit, axis=0))


def on_device(
    tokens,
    cotangent,
    segment_ids,
    positions,
    q_weight,
    k_weight,
    v_weight,
    o_weight,
    attn_gain,
    gate_up_weight,
    down_weight,
    mlp_gain,
):
    plane = Plane()
    unit, n = plane.unit, plane.n
    heads = HEADS // n
    share = max(1, n // KV_HEADS)
    q_cols = heads * HEAD
    ff = FF // n
    kv_head = unit // share

    def qkv_columns(u):
        rows = q_weight.shape[0]
        return jnp.concatenate(
            [
                lax.dynamic_slice(q_weight, (0, u * q_cols), (rows, q_cols)),
                lax.dynamic_slice(k_weight, (0, (u // share) * HEAD), (rows, HEAD)),
                lax.dynamic_slice(v_weight, (0, (u // share) * HEAD), (rows, HEAD)),
            ],
            axis=1,
        )

    def mlp_columns(u):
        rows = gate_up_weight.shape[0]
        return jnp.concatenate(
            [
                lax.dynamic_slice(gate_up_weight, (0, u * ff), (rows, ff)),
                lax.dynamic_slice(gate_up_weight, (0, FF + u * ff), (rows, ff)),
            ],
            axis=1,
        )

    tokens_all = plane.gather(tokens)
    w_qkv = plane.reshard(qkv_columns)
    gains = lax.all_gather(jnp.stack([attn_gain, mlp_gain]), "fsdp", axis=1, tiled=True)
    gain_one = gains[0].astype(F32)
    gain_two = gains[1].astype(F32)
    segments = plane.groups(plane.gather(segment_ids))
    places = plane.groups(plane.gather(positions))
    w_out = lax.dynamic_slice(o_weight, (plane.p * q_cols, 0), (q_cols, D))
    w_down = lax.dynamic_slice(down_weight, (plane.p * ff, 0), (ff, D))

    inputs_all = tokens_all.astype(F32)
    inv_all = lax.rsqrt(jnp.mean(inputs_all * inputs_all, axis=-1, keepdims=True) + EPS)
    normed = (inputs_all * inv_all * gain_one).astype(BF16)
    lin = dot(normed, w_qkv)
    lin = plane.groups(lin)
    groups, length = lin.shape[:2]
    cosine, sine = rope_tables(places, HEAD // 2)
    query = rotate(lin[..., :q_cols].reshape(groups, length, heads, HEAD), cosine, sine, 1.0)
    query = query.astype(BF16)
    key = rotate(lin[..., None, q_cols : q_cols + HEAD], cosine, sine, 1.0)[:, :, 0].astype(BF16)
    value = lin[..., q_cols + HEAD :].astype(BF16)
    visible = (
        (segments[:, None, :] == 0) | (segments[:, None, :] == segments[:, :, None])
    ) & (places[:, None, :] <= places[:, :, None])
    scores = jnp.einsum("gqjd,gkd->gjqk", query, key, preferred_element_type=F32) * SCALE
    masked = jnp.where(visible[:, None], scores, -jnp.inf)
    peak = jnp.max(masked, axis=3, keepdims=True)
    exp_scores = jnp.exp(masked - peak)
    probs = exp_scores / jnp.sum(exp_scores, axis=3, keepdims=True)
    probs_low = probs.astype(BF16)
    top_local = jnp.max(peak, axis=(0, 2, 3))
    attended = jnp.einsum("gjqk,gkd->gqjd", probs_low, value, preferred_element_type=F32)
    attended = plane.rows(attended.astype(BF16).reshape(groups, length, q_cols))

    inputs = tokens.astype(F32)
    middle = inputs + RESID * plane.scatter(attended, w_out, dot)
    inv_two = lax.rsqrt(jnp.mean(middle * middle, axis=-1, keepdims=True) + EPS)
    unit_two = middle * inv_two
    normed_mlp = plane.gather((unit_two * gain_two).astype(BF16))
    grad_out = cotangent.astype(F32)
    grad_branch = plane.gather((RESID * grad_out).astype(BF16))
    w_gate_up = plane.reshard(mlp_columns)

    gate_up = dot(normed_mlp, w_gate_up)
    gate = gate_up[:, :ff]
    up_part = gate_up[:, ff:]
    sigma = jax.nn.sigmoid(gate)
    silu_gate = gate * sigma
    hidden = (silu_gate * up_part).astype(BF16)
    grad_hidden = times_t(grad_branch, w_down)
    grad_gate_up = jnp.concatenate(
        [grad_hidden * up_part * sigma * (1.0 + gate * (1.0 - sigma)), grad_hidden * silu_gate],
        axis=1,
    ).astype(BF16)
    down_grad = plane.sum_units(outer(hidden, grad_branch))
    grad_normed_mlp = plane.scatter(grad_gate_up, w_gate_up, times_t)
    gate_up_rows = plane.sum_rows(outer(normed_mlp, grad_gate_up))
    owned = gate_up_rows.shape[0] * gate_up_rows.shape[1]
    gate_up_rows = gate_up_rows.reshape(owned, n, 2, ff)
    gate_up_grad = jnp.swapaxes(gate_up_rows, 1, 2).reshape(owned, 2 * FF).astype(F32)
    result = (middle + RESID * plane.scatter(hidden, w_down, dot)).astype(BF16)

    grad_mid_norm, gain_two_grad = norm_back(grad_normed_mlp, unit_two, inv_two, gain_two)
    grad_middle = grad_out + grad_mid_norm
    grad_attn_branch = plane.gather((RESID * grad_middle).astype(BF16))
    grad_attended = times_t(grad_attn_branch, w_out).astype(BF16)
    o_grad = plane.sum_units(outer(attended, grad_attn_branch))
    grad_attended = plane.groups(grad_attended).reshape(groups, length, heads, HEAD)
    grad_probs = jnp.einsum("gqjd,gkd->gjqk", grad_attended, value, preferred_element_type=F32)
    delta = jnp.sum(probs * grad_probs, axis=3, keepdims=True)
    grad_scores = (probs * (grad_probs - delta) * SCALE).astype(BF16)
    grad_query = jnp.einsum("gjqk,gkd->gqjd", grad_scores, key, preferred_element_type=F32)
    grad_key = jnp.einsum("gjqk,gqjd->gkd", grad_scores, query, preferred_element_type=F32)
    grad_value = jnp.einsum("gjqk,gqjd->gkd", probs_low, grad_attended, preferred_element_type=F32)
    grad_query = rotate(grad_query, cosine, sine, -1.0).reshape(groups, length, q_cols)
    grad_key = rotate(grad_key[:, :, None], cosine, sine, -1.0)[:, :, 0]
    grad_lin = plane.rows(
        jnp.concatenate([grad_query, grad_key, grad_value], axis=-1).astype(BF16)
    )
    grad_normed = plane.scatter(grad_lin, w_qkv, times_t)
    lin_rows = plane.sum_rows(outer(normed, grad_lin)).astype(F32)
    inv_one = lax.rsqrt(jnp.mean(inputs * inputs, axis=-1, keepdims=True) + EPS)
    grad_in_norm, gain_one_grad = norm_back(grad_normed, inputs * inv_one, inv_one, gain_one)
    input_grad = (grad_middle + grad_in_norm).astype(BF16)

    lin_rows = lin_rows.reshape((-1,) + lin_rows.shape[2:])
    rows = lin_rows.shape[0]
    tops = jnp.full((HEADS,), -jnp.inf, F32)
    tops = lax.dynamic_update_slice(tops, top_local, (unit * heads,))
    tops = lax.pmax(tops, ("pair", "fsdp", "rep"))
    factor = TAU / jnp.maximum(tops, TAU)
    k_factor = jnp.repeat(jnp.min(factor.reshape(KV_HEADS, GROUP), axis=1), HEAD)
    q_update = lin_rows[..., :q_cols].reshape(rows, D) * jnp.repeat(factor, HEAD)[None, :]
    kv = lin_rows[..., q_cols:].reshape(rows, n // share, share, 2 * HEAD).sum(axis=2)
    k_update = kv[..., :HEAD].reshape(rows, -1) * k_factor[None, :]
    v_grad = kv[..., HEAD:].reshape(rows, -1)
    gain_grads = lax.psum(jnp.stack([gain_one_grad, gain_two_grad]), ("pair", "fsdp", "rep"))
    place = plane.p * plane.nf + plane.f
    gain_grads = lax.dynamic_slice(gain_grads, (0, place * (D // n)), (2, D // n))
    return (
        result,
        input_grad,
        q_update,
        k_update,
        v_grad,
        o_grad,
        gain_grads[0],
        gate_up_grad,
        down_grad,
        gain_grads[1],
    )


def solution(mesh):
    tokens = P(("pair", "fsdp", "rep"))
    shard = P("fsdp")
    owned = P(("pair", "fsdp"))
    return jax.shard_map(
        on_device,
        mesh=mesh,
        in_specs=(tokens,) * 4 + (shard,) * 8,
        out_specs=(tokens, tokens) + (owned,) * 8,
        check_vma=False,
    )
```

time: 2260 us -> 1090 us (0.48)
  waiting for transfers between devices: 1870 us -> 486 us
  local copies, waits for them, and re-layouts: 9.67 us -> 183 us
  matrix products: 223 us -> 131 us
  blocking collectives: 86.2 us -> 149 us
  starting transfers between devices: 5.41 us -> 52.8 us
  other arithmetic: 37.4 us -> 61.2 us
    all_gather x6 -> x4, waiting for transfers between devices: 687 us -> 78.7 us  [the longest x2 78.6 us: sum_rows(): full = lax.all_gather(moved, 'rep', axis=0)]
    reduce_scatter x6 -> x4, waiting for transfers between devices: 760 us -> 213 us  [the longest x2 150 us: sum_rows(): lax.psum_scatter(jnp.swapaxes(split, 0, 1), 'rep', scatter_dimension=0)]
    psum x1 -> x0, waiting for transfers between devices: 412 us -> none  [replicas(): lax.psum(parts[0].astype(jnp.bfloat16), 'rep').astype(jnp.float32)]
    ppermute x2 -> x66, waiting for transfers between devices: 8.59 us -> 195 us  [the longest x64 195 us: swap(): return lax.ppermute(x, PLANE, [(i, i ^ mask) for i in range(devices)])]
    convert_element_type x2 -> x5, local copies, waits for them, and re-layouts: 2.15 us -> 65.9 us  [the longest x4 65.5 us: on_device(): jnp.swapaxes(gate_up_rows, 1, 2).reshape(owned, 2 * FF).astype(F32)]
    unnamed x71 -> x178, local copies, waits for them, and re-layouts: 4.82 us -> 54.6 us
    ppermute x2 -> x66, starting transfers between devices: 4.68 us -> 52.5 us  [the longest x64 49 us: swap(): return lax.ppermute(x, PLANE, [(i, i ^ mask) for i in range(devices)])]
    all_to_all x0 -> x2, blocking collectives: none -> 45.5 us  [sum_rows(): moved = lax.all_to_all(mine, PLANE, 0, 0, tiled=True)]
  transfers between devices with their start and end apart: 15 -> 74, of which waited for: 14 -> 28; matrix products, arithmetic and copies ran while one was open for 7% -> 20% of each run, Pallas kernels for 0% -> 0%
where the time goes in v1:
time: 1090 us; the launch traced here: 1080 us
  waiting for transfers between devices  486 us (45%)
  local copies, waits for them, and re-layouts  183 us (17%)
  blocking collectives  149 us (14%)
  matrix products  131 us (12%)
  other arithmetic  61.2 us (6%)
  starting transfers between devices  52.8 us (5%)
  between operations  16.1 us (1%)
    ppermute x64, waiting for transfers between devices, swap(): return lax.ppermute(x, PLANE, [(i, i ^ mask) for i in range(devices)])  195 us
    reduce_scatter x2, waiting for transfers between devices, sum_rows(): lax.psum_scatter(jnp.swapaxes(split, 0, 1), 'rep', scatter_dimension=0)  150 us
    all_gather x2, waiting for transfers between devices, sum_rows(): full = lax.all_gather(moved, 'rep', axis=0)  78.6 us
    convert_element_type x4, local copies, waits for them, and re-layouts, on_device(): jnp.swapaxes(gate_up_rows, 1, 2).reshape(owned, 2 * FF).astype(F32)  65.5 us
    reduce_scatter x2, waiting for transfers between devices, sum_units(): lax.psum_scatter(term.astype(BF16), 'rep', scatter_dimension=0, tiled=True)  63.3 us
    psum x1, blocking collectives, on_device(): lax.psum(jnp.stack([gain_one_grad, gain_two_grad]), ('pair', 'fsdp', 'rep'))  57.6 us
    unnamed x178, local copies, waits for them, and re-layouts  54.6 us
    ppermute x64, starting transfers between devices, swap(): return lax.ppermute(x, PLANE, [(i, i ^ mask) for i in range(devices)])  49 us
  transfers between devices with their start and end apart: 74, of which 28 were waited for; matrix products, arithmetic and copies ran while one was open for 20% of the time, Pallas kernels for 0%

profile of v1, /device:TPU:0, one launch (start us, length us, event | category | flops | bytes accessed | tf_op | source)
XLA Modules:
  0.0 1079.8 jit_solution(31448939773249350)
XLA Ops:
  142.7 91.0 %collective-permute-done.27 = bf16[128,2048]{1,0:T(8,128)(2,1)S(1)} collective-permute-done((bf16[128,2048]{1,0:T(8,128)(2,1)S(1)}, bf16[128,2048]{1,0:T(8,128)(2,1)S(1)}, u32[]{:S(2)}, u32[]{:S(2)}) %collective-permute-start.27) | collective-permute-done | bytes 524320 | tf_op jit(solution)/shard_map/ppermute | solution.py:38
  233.7 9.0 collective-permute-done.26
  274.0 13.4 %fusion.138 = f32[1024,2048]{1,0:T(8,128)} fusion(bf16[1024,2048]{1,0:T(8,128)(2,1)S(1)} %constant_dynamic-update-slice_fusion.10, bf16[2048,2048]{1,0:T(8,128)(2,1)} %constant_dynamic-update-slice_fusion.48), kind=kOutput, calls=%fused_computation.283 | convolution fusion | flops 8589934592 | bytes 20971520 | tf_op jit(solution)/shard_map/dot_general | solution.py:26
  287.4 10.1 multiply_convert_fusion
  297.4 9.0 convolution_convert_fusion.4
  321.8 12.2 %collective-permute-done.52 = bf16[128,2048]{1,0:T(8,128)(2,1)S(1)} collective-permute-done((bf16[128,2048]{1,0:T(8,128)(2,1)S(1)}, bf16[128,2048]{1,0:T(8,128)(2,1)S(1)}, u32[]{:S(2)}, u32[]{:S(2)}) %collective-permute-start.52) | collective-permute-done | bytes 524320 | tf_op jit(solution)/shard_map/ppermute | solution.py:38
  334.0 10.6 collective-permute-done.51
  351.1 9.1 collective-permute-done.53
  362.5 9.8 collective-permute-done.55
  412.5 9.5 convolution_convert_fusion.1
  422.0 14.5 %convolution_convert_fusion = bf16[2048,2048]{1,0:T(8,128)(2,1)} fusion(bf16[1024,2048]{1,0:T(8,128)(2,1)} %copy-done.35, bf16[1024,1024]{1,0:T(8,128)(2,1)} %copy-done.58, bf16[1024,1024]{1,0:T(8,128)(2,1)} %get-tuple-element.61), kind=kOutput, calls=%fused_computation.9 | convolution fusion | flops 8602517504 | bytes 16777216 | tf_op jit(solution)/shard_map/dot_general | solution.py:30
  452.1 14.6 %all_to_all.10 = bf16[8,64,384]{2,1,0:T(8,128)(2,1)} all-to-all(bf16[8,64,384]{2,1,0:T(8,128)(2,1)} %bitcast.206), channel_id=1, replica_groups=mesh['pair'=2,'fsdp'=4,'rep'=4] {'pair','fsdp'}, dimensions={0} | all-to-all | bytes 786432 | tf_op jit(solution)/shard_map/all_to_all | solution.py:128
  466.9 63.2 %reduce-scatter.11.cloned.1.call-done = bf16[256,2048]{1,0:T(8,128)(2,1)} async-done(((bf16[1024,2048]{1,0:T(8,128)(2,1)}), bf16[256,2048]{1,0:T(8,128)(2,1)}) %reduce-scatter.11.cloned.1.call-update) | async-done | bytes 1048592 | tf_op jit(solution)/shard_map/reduce_scatter | solution.py:133
  533.0 145.0 %reduce-scatter.9.cloned.1.call-done = bf16[1,8,64,2048]{3,2,1,0:T(8,128)(2,1)} async-done(((bf16[4,8,64,2048]{3,2,1,0:T(8,128)(2,1)}), bf16[1,8,64,2048]{3,2,1,0:T(8,128)(2,1)}) %reduce-scatter.9.cloned.1.call-update) | async-done | bytes 2097168 | tf_op jit(solution)/shard_map/reduce_scatter | solution.py:127
  678.1 30.9 %all_to_all.11 = bf16[8,64,2048]{2,1,0:T(8,128)(2,1)} all-to-all(bf16[8,64,2048]{2,1,0:T(8,128)(2,1)} %bitcast.190), channel_id=1, replica_groups=mesh['pair'=2,'fsdp'=4,'rep'=4] {'pair','fsdp'}, dimensions={0} | all-to-all | bytes 4194304 | tf_op jit(solution)/shard_map/all_to_all | solution.py:128
  724.9 40.8 %pmax.7 = f32[32]{0:T(128)} all-reduce(f32[32]{0:T(128)} %dynamic_update_slice.35), channel_id=1, replica_groups=mesh['pair'=2,'fsdp'=4,'rep'=4] {'pair','fsdp','rep'}, use_global_device_ids=true, to_apply=%region_10.11 | all-reduce | flops 32 | bytes 256 | tf_op jit(solution)/shard_map/pmax | solution.py:280
  798.8 9.8 collective-permute-done.62
  810.0 57.6 %psum.7 = f32[2,2048]{1,0:T(2,128)S(1)} all-reduce(f32[2,2048]{1,0:T(2,128)S(1)} %pad_maximum_fusion.15), channel_id=1, replica_groups=mesh['pair'=2,'fsdp'=4,'rep'=4] {'pair','fsdp','rep'}, use_global_device_ids=true, to_apply=%region_15.16 | all-reduce | flops 4096 | bytes 32768 | tf_op jit(solution)/shard_map/psum | solution.py:287
  899.3 78.6 %all-gather.13.cloned.1.call-done = bf16[32,64,2048]{2,1,0:T(8,128)(2,1)} async-done(((bf16[8,64,2048]{2,1,0:T(8,128)(2,1)}), bf16[32,64,2048]{2,1,0:T(8,128)(2,1)}) %all-gather.13.cloned.1.call-update) | async-done | bytes 8388624 | tf_op jit(solution)/shard_map/all_gather | solution.py:129
  977.9 11.7 %convert_bitcast_fusion = f32[4,4,2,64,2048]{4,3,1,2,0:T(8,128)} fusion(bf16[4,2,4,64,2048]{4,3,2,1,0:T(8,128)(2,1)} %bitcast.179), kind=kLoop, calls=%fused_computation.2 | loop fusion | flops 4194304 | bytes 25165824 | tf_op jit(solution)/shard_map/convert_element_type | solution.py:250
  996.1 12.0 %copy.119 = f32[4,64,8,2048]{3,2,1,0:T(8,128)} copy(f32[4,64,8,2048]{3,1,2,0:T(8,128)S(1)} %bitcast.172) | data formatting | bytes 33554432 | tf_op jit(solution)/shard_map/convert_element_type | solution.py:250
  1008.1 22.1 %reshape.187 = f32[256,8,2,1024]{3,2,1,0:T(2,128)} reshape(f32[4,64,8,2048]{3,2,1,0:T(8,128)} %copy.119) | data formatting | bytes 33554432 | tf_op jit(solution)/shard_map/convert_element_type | solution.py:250
  1030.2 24.9 %copy.120 = f32[256,2,8,1024]{0,3,2,1:T(8,128)} copy(f32[256,2,8,1024]{3,1,2,0:T(2,128)} %bitcast.173) | data formatting | bytes 33554432 | tf_op jit(solution)/shard_map/convert_element_type | solution.py:250
  1055.1 17.6 %copy.123 = f32[256,16384]{1,0:T(8,128)} copy(f32[256,16384]{0,1:T(8,128)} %bitcast.174) | data formatting | bytes 33554432
  (449 shorter events, 336.8 us)
Async XLA Ops:
  7.2 437.9 %reduce-scatter.7.cloned.1.call-start = ((), (), s32[]{:S(2)}) async-start(), calls=%async_computation.7 | async-start | bytes 1310720 | tf_op jit(solution)/shard_map/reduce_scatter | solution.py:133
  7.3 63.8 %collective-permute-start = (bf16[128,2048]{1,0:T(8,128)(2,1)}, bf16[128,2048]{1,0:T(8,128)(2,1)}, u32[]{:S(2)}, u32[]{:S(2)}) collective-permute-start(bf16[128,2048]{1,0:T(8,128)(2,1)} %param.12), channel_id=1, source_target_pairs={{0,16},{4,20},{8,24},{12,28},{16,0},{20,4},{24,8},{28,12},{1,17},{... | collective-permute-start | bytes 1572872 | tf_op jit(solution)/shard_map/ppermute | solution.py:38
  10.3 63.2 %collective-permute-start.1 = (bf16[128,2048]{1,0:T(8,128)(2,1)}, bf16[128,2048]{1,0:T(8,128)(2,1)}, u32[]{:S(2)}, u32[]{:S(2)}) collective-permute-start(bf16[128,2048]{1,0:T(8,128)(2,1)} %param.12), channel_id=1, source_target_pairs={{0,8},{4,12},{8,0},{12,4},{16,24},{20,28},{24,16},{28,20},{1,9},{5... | collective-permute-start | bytes 1572872 | tf_op jit(solution)/shard_map/ppermute | solution.py:38
  67.7 55.5 %collective-permute-start.42 = (bf16[128,2048]{1,0:T(8,128)(2,1)}, bf16[128,2048]{1,0:T(8,128)(2,1)}, u32[]{:S(2)}, u32[]{:S(2)}) collective-permute-start(bf16[128,2048]{1,0:T(8,128)(2,1)} %fusion.42), channel_id=1, source_target_pairs={{0,16},{4,20},{8,24},{12,28},{16,0},{20,4},{24,8},{28,12},{1,17},{... | collective-permute-start | bytes 1572872 | tf_op jit(solution)/shard_map/ppermute | solution.py:38
  71.0 54.1 %collective-permute-start.43 = (bf16[128,2048]{1,0:T(8,128)(2,1)}, bf16[128,2048]{1,0:T(8,128)(2,1)}, u32[]{:S(2)}, u32[]{:S(2)}) collective-permute-start(bf16[128,2048]{1,0:T(8,128)(2,1)} %fusion.42), channel_id=1, source_target_pairs={{0,8},{4,12},{8,0},{12,4},{16,24},{20,28},{24,16},{28,20},{1,9},{5... | collective-permute-start | bytes 1572872 | tf_op jit(solution)/shard_map/ppermute | solution.py:38
  82.8 44.7 %collective-permute-start.44 = (bf16[128,2048]{1,0:T(8,128)(2,1)}, bf16[128,2048]{1,0:T(8,128)(2,1)}, u32[]{:S(2)}, u32[]{:S(2)}) collective-permute-start(bf16[128,2048]{1,0:T(8,128)(2,1)} %fusion.42), channel_id=1, source_target_pairs={{0,24},{4,28},{8,16},{12,20},{16,8},{20,12},{24,0},{28,4},{1,25},{... | collective-permute-start | bytes 1572872 | tf_op jit(solution)/shard_map/ppermute | solution.py:38
  83.9 47.3 %collective-permute-start.45 = (bf16[128,2048]{1,0:T(8,128)(2,1)}, bf16[128,2048]{1,0:T(8,128)(2,1)}, u32[]{:S(2)}, u32[]{:S(2)}) collective-permute-start(bf16[128,2048]{1,0:T(8,128)(2,1)} %fusion.42), channel_id=1, source_target_pairs={{0,4},{4,0},{8,12},{12,8},{16,20},{20,16},{24,28},{28,24},{1,5},{5... | collective-permute-start | bytes 1572872 | tf_op jit(solution)/shard_map/ppermute | solution.py:38
  127.5 120.3 %collective-permute-start.36 = (bf16[512,2048]{1,0:T(8,128)(2,1)}, bf16[512,2048]{1,0:T(8,128)(2,1)S(1)}, u32[]{:S(2)}, u32[]{:S(2)}) collective-permute-start(bf16[512,2048]{1,0:T(8,128)(2,1)} %pad_maximum_fusion.3), channel_id=1, source_target_pairs={{0,8},{4,12},{8,0},{12,4},{16,24},{20,28},{24,16},{28,20},{1,9},{5... | collective-permute-start | bytes 6291464 | tf_op jit(solution)/shard_map/ppermute | solution.py:38
  131.2 118.3 %collective-permute-start.37 = (bf16[512,2048]{1,0:T(8,128)(2,1)}, bf16[512,2048]{1,0:T(8,128)(2,1)S(1)}, u32[]{:S(2)}, u32[]{:S(2)}) collective-permute-start(bf16[512,2048]{1,0:T(8,128)(2,1)} %pad_maximum_fusion.4), channel_id=1, source_target_pairs={{0,12},{4,8},{8,4},{12,0},{16,28},{20,24},{24,20},{28,16},{1,13},{... | collective-permute-start | bytes 6291464 | tf_op jit(solution)/shard_map/ppermute | solution.py:38
  137.5 96.2 %collective-permute-start.27 = (bf16[128,2048]{1,0:T(8,128)(2,1)S(1)}, bf16[128,2048]{1,0:T(8,128)(2,1)S(1)}, u32[]{:S(2)}, u32[]{:S(2)}) collective-permute-start(bf16[128,2048]{1,0:T(8,128)(2,1)S(1)} %get-tuple-element.75), channel_id=1, source_target_pairs={{0,24},{4,28},{8,16},{12,20},{16,8},{20,12},{24,0},{28,4},{1,25},{... | collective-permute-start | bytes 1572872 | tf_op jit(solution)/shard_map/ppermute | solution.py:38
  140.1 102.6 %collective-permute-start.26 = (bf16[128,2048]{1,0:T(8,128)(2,1)S(1)}, bf16[128,2048]{1,0:T(8,128)(2,1)S(1)}, u32[]{:S(2)}, u32[]{:S(2)}) collective-permute-start(bf16[128,2048]{1,0:T(8,128)(2,1)S(1)} %get-tuple-element.76), channel_id=1, source_target_pairs={{0,8},{4,12},{8,0},{12,4},{16,24},{20,28},{24,16},{28,20},{1,9},{5... | collective-permute-start | bytes 1572872 | tf_op jit(solution)/shard_map/ppermute | solution.py:38
  140.7 102.0 %collective-permute-start.25 = (bf16[128,2048]{1,0:T(8,128)(2,1)S(1)}, bf16[128,2048]{1,0:T(8,128)(2,1)S(1)}, u32[]{:S(2)}, u32[]{:S(2)}) collective-permute-start(bf16[128,2048]{1,0:T(8,128)(2,1)S(1)} %get-tuple-element.74), channel_id=1, source_target_pairs={{0,16},{4,20},{8,24},{12,28},{16,0},{20,4},{24,8},{28,12},{1,17},{... | collective-permute-start | bytes 1572872 | tf_op jit(solution)/shard_map/ppermute | solution.py:38
  387.0 65.1 %reduce-scatter.5.cloned.1.call-start = ((), (), s32[]{:S(2)}) async-start(), calls=%async_computation.6 | async-start | bytes 1966080 | tf_op jit(solution)/shard_map/reduce_scatter | solution.py:127
  412.4 117.6 %reduce-scatter.11.cloned.1.call-start = ((), (), s32[]{:S(2)}) async-start(), calls=%async_computation.10 | async-start | bytes 5242880 | tf_op jit(solution)/shard_map/reduce_scatter | solution.py:133
  422.0 256.1 %reduce-scatter.9.cloned.1.call-start = ((), (), s32[]{:S(2)}) async-start(), calls=%async_computation.9 | async-start | bytes 10485760 | tf_op jit(solution)/shard_map/reduce_scatter | solution.py:127
  445.1 427.2 %all-gather.7.cloned.1.call-start = ((), (), s32[]{:S(2)}) async-start(), calls=%async_computation.8 | async-start | bytes 1310720 | tf_op jit(solution)/shard_map/all_gather | solution.py:139
  447.5 427.5 %all-gather.11.cloned.1.call-start = ((), (), s32[]{:S(2)}) async-start(), calls=%async_computation.12 | async-start | bytes 1966080 | tf_op jit(solution)/shard_map/all_gather | solution.py:129
  466.8 425.8 %all-gather.9.cloned.1.call-start = ((), (), s32[]{:S(2)}) async-start(), calls=%async_computation.11 | async-start | bytes 5242880 | tf_op jit(solution)/shard_map/all_gather | solution.py:139
  533.0 444.9 %all-gather.13.cloned.1.call-start = ((), (), s32[]{:S(2)}) async-start(), calls=%async_computation.13 | async-start | bytes 10485760 | tf_op jit(solution)/shard_map/all_gather | solution.py:129
  714.0 61.5 %collective-permute-start.60 = (bf16[512,2048]{1,0:T(8,128)(2,1)}, bf16[512,2048]{1,0:T(8,128)(2,1)S(1)}, u32[]{:S(2)}, u32[]{:S(2)}) collective-permute-start(bf16[512,2048]{1,0:T(8,128)(2,1)} %convolution_convert_fusion.3), channel_id=1, source_target_pairs={{0,4},{4,0},{8,12},{12,8},{16,20},{20,16},{24,28},{28,24},{1,5},{5... | collective-permute-start | bytes 6291464 | tf_op jit(solution)/shard_map/ppermute | solution.py:38
  720.0 64.6 %collective-permute-start.38 = (bf16[512,2048]{1,0:T(8,128)(2,1)}, bf16[512,2048]{1,0:T(8,128)(2,1)}, u32[]{:S(2)}, u32[]{:S(2)}) collective-permute-start(bf16[512,2048]{1,0:T(8,128)(2,1)} %fusion.17), channel_id=1, source_target_pairs={{0,4},{4,0},{8,12},{12,8},{16,20},{20,16},{24,28},{28,24},{1,5},{5... | collective-permute-start | bytes 6291464 | tf_op jit(solution)/shard_map/ppermute | solution.py:38
  793.1 75.1 %collective-permute-start.41 = (bf16[128,2048]{1,0:T(8,128)(2,1)}, bf16[128,2048]{1,0:T(8,128)(2,1)}, u32[]{:S(2)}, u32[]{:S(2)}) collective-permute-start(bf16[128,2048]{1,0:T(8,128)(2,1)} %get-tuple-element.72), channel_id=1, source_target_pairs={{0,24},{4,28},{8,16},{12,20},{16,8},{20,12},{24,0},{28,4},{1,25},{... | collective-permute-start | bytes 1572872 | tf_op jit(solution)/shard_map/ppermute | solution.py:38
  795.0 73.2 %collective-permute-start.40 = (bf16[128,2048]{1,0:T(8,128)(2,1)}, bf16[128,2048]{1,0:T(8,128)(2,1)}, u32[]{:S(2)}, u32[]{:S(2)}) collective-permute-start(bf16[128,2048]{1,0:T(8,128)(2,1)} %get-tuple-element.73), channel_id=1, source_target_pairs={{0,8},{4,12},{8,0},{12,4},{16,24},{20,28},{24,16},{28,20},{1,9},{5... | collective-permute-start | bytes 1572872 | tf_op jit(solution)/shard_map/ppermute | solution.py:38
  796.5 71.7 %collective-permute-start.39 = (bf16[128,2048]{1,0:T(8,128)(2,1)}, bf16[128,2048]{1,0:T(8,128)(2,1)}, u32[]{:S(2)}, u32[]{:S(2)}) collective-permute-start(bf16[128,2048]{1,0:T(8,128)(2,1)} %get-tuple-element.71), channel_id=1, source_target_pairs={{0,16},{4,20},{8,24},{12,28},{16,0},{20,4},{24,8},{28,12},{1,17},{... | collective-permute-start | bytes 1572872 | tf_op jit(solution)/shard_map/ppermute | solution.py:38
  (114 other events, 1863.1 us)
Sparse Core Ops, SparseCore 0:
  387.2 28.6 reduce-scatter.6
  418.1 33.9 reduce-scatter.4
  454.4 75.6 reduce-scatter.10
  532.9 145.1 reduce-scatter.8
  679.5 28.5 all-gather.6
  709.5 36.5 all-gather.10
  747.7 79.8 all-gather.8
  829.2 148.7 all-gather.12

commit v2 on v1

v2 whole, which is shorter than its diff:
```python
import jax
import jax.numpy as jnp
from jax import lax
from jax.experimental import pallas as pl
from jax.experimental.pallas import tpu as pltpu
from jax.sharding import PartitionSpec as P

D = 2048
FF = 8192
HEADS = 32
KV_HEADS = 8
HEAD = 64
GROUP = HEADS // KV_HEADS

EPS = 1e-05
THETA = 10000000.0
SCALE = 0.015625
RESID = 0.22
TAU = 3.0

PLANE = ("pair", "fsdp")
F32 = jnp.float32
BF16 = jnp.bfloat16
ORDER = (0, 4, 2, 6, 1, 5, 3, 7)


def dot(left, right):
    return jnp.dot(left, right, preferred_element_type=F32)


def outer(left, right):
    return lax.dot_general(left, right, (((0,), (0,)), ((), ())), preferred_element_type=F32)


def times_t(left, right):
    return lax.dot_general(left, right, (((1,), (1,)), ((), ())), preferred_element_type=F32)


def swap(x, mask, devices=8):
    return lax.ppermute(x, PLANE, [(i, i ^ mask) for i in range(devices)])


def along(x, pairs):
    return lax.ppermute(x, "rep", pairs)


def after(x, *others):
    return lax.optimization_barrier((x,) + others)[0]


def rope_tables(places, heads):
    half = HEAD // 2
    inverse = THETA ** (-(jnp.arange(half, dtype=F32) * 2.0 / HEAD))
    angle = places.astype(F32)[:, None] * inverse[None, :]
    cosine, sine = jnp.cos(angle), jnp.sin(angle)
    ones, zeros = jnp.ones((places.shape[0], HEAD), F32), jnp.zeros((places.shape[0], HEAD), F32)
    cos_row = jnp.concatenate([cosine] * (2 * heads + 2) + [ones], axis=1)
    sin_row = jnp.concatenate([-sine, sine] * (heads + 1) + [zeros], axis=1)
    return cos_row, sin_row


def half_swap(x):
    width = x.shape[1]
    lane = lax.broadcasted_iota(jnp.int32, x.shape, 1)
    first = (lane & (HEAD - 1)) < HEAD // 2
    return jnp.where(first, pltpu.roll(x, width - HEAD // 2, 1), pltpu.roll(x, HEAD // 2, 1))


def mat_t(left, right):
    return lax.dot_general(left, right, (((1,), (1,)), ((), ())), preferred_element_type=F32)


def mat_tl(left, right):
    return lax.dot_general(left, right, (((0,), (0,)), ((), ())), preferred_element_type=F32)


def attend_kernel(heads, lin_ref, cos_ref, sin_ref, vis_ref, qkv_ref, att_ref, top_ref):
    x = lin_ref[...]
    row = (x * cos_ref[...] + half_swap(x) * sin_ref[...]).astype(BF16)
    qkv_ref[...] = row
    key = row[:, heads * HEAD : (heads + 1) * HEAD]
    value = row[:, (heads + 1) * HEAD :]
    visible = vis_ref[...] > 0.0
    top_ref[...] = jnp.full(top_ref.shape, -jnp.inf, F32)
    outs = []
    for h in range(heads):
        scores = mat_t(row[:, h * HEAD : (h + 1) * HEAD], key) * SCALE
        scores = jnp.where(visible, scores, -jnp.inf)
        peak = jnp.max(scores, axis=1, keepdims=True)
        grown = jnp.exp(scores - peak)
        probs = (grown / jnp.sum(grown, axis=1, keepdims=True)).astype(BF16)
        outs.append(dot(probs, value).astype(BF16))
        top_ref[h : h + 1, :] = jnp.broadcast_to(jnp.max(peak, axis=0, keepdims=True), (1, 128))
    att_ref[...] = jnp.concatenate(outs, axis=1)


def attend_back_kernel(heads, qkv_ref, cos_ref, sin_ref, vis_ref, grad_ref, out_ref):
    row = qkv_ref[...]
    key = row[:, heads * HEAD : (heads + 1) * HEAD]
    value = row[:, (heads + 1) * HEAD :]
    visible = vis_ref[...] > 0.0
    grad_att = grad_ref[...]
    grads = []
    grad_key = jnp.zeros((row.shape[0], HEAD), F32)
    grad_value = jnp.zeros((row.shape[0], HEAD), F32)
    for h in range(heads):
        query = row[:, h * HEAD : (h + 1) * HEAD]
        grad_h = grad_att[:, h * HEAD : (h + 1) * HEAD]
        scores = jnp.where(visible, mat_t(query, key) * SCALE, -jnp.inf)
        peak = jnp.max(scores, axis=1, keepdims=True)
        grown = jnp.exp(scores - peak)
        probs = grown / jnp.sum(grown, axis=1, keepdims=True)
        grad_probs = mat_t(grad_h, value)
        delta = jnp.sum(probs * grad_probs, axis=1, keepdims=True)
        grad_scores = (probs * (grad_probs - delta) * SCALE).astype(BF16)
        grads.append(dot(grad_scores, key))
        grad_key = grad_key + mat_tl(grad_scores, query)
        grad_value = grad_value + mat_tl(probs.astype(BF16), grad_h)
    x = jnp.concatenate(grads + [grad_key, grad_value], axis=1)
    out_ref[...] = (x * cos_ref[...] - half_swap(x) * sin_ref[...]).astype(BF16)


def by_group(kernel, heads, length, ins, outs, name, flops):
    groups = ins[0].shape[0] // length

    def spec(x):
        rows = x.shape[0] // groups
        return pl.BlockSpec((rows, x.shape[1]), lambda g: (g, 0))

    return pl.pallas_call(
        lambda *refs: kernel(heads, *refs),
        grid=(groups,),
        in_specs=[spec(x) for x in ins],
        out_specs=[spec(x) for x in outs],
        out_shape=outs,
        name=name,
        cost_estimate=pl.CostEstimate(
            flops=flops, bytes_accessed=4 * sum(x.size for x in ins), transcendentals=0
        ),
    )(*ins)


def place_kernel(count, table, *refs):
    which = table[0, pl.program_id(0)]
    out_ref = refs[-1]
    for b in range(count):

        @pl.when(which == b)
        def _():
            out_ref[...] = refs[b][0].astype(F32)


def place(shards, table, shape, into, name):
    _, rows, columns = shards[0].shape
    count = len(shards)
    steps = table.shape[1]

    def pick(b):
        return pl.BlockSpec((1, rows, columns), lambda i, t: (t[1 + b, i], 0, 0))

    in_specs = [pick(b) for b in range(count)]
    args = list(shards)
    aliases = {}
    if into is not None:
        in_specs.append(pl.BlockSpec(memory_space=pl.ANY))
        args.append(into)
        aliases = {1 + count: 0}
    return pl.pallas_call(
        lambda t, *refs: place_kernel(count, t, *refs),
        grid_spec=pltpu.PrefetchScalarGridSpec(
            num_scalar_prefetch=1,
            grid=(steps,),
            in_specs=in_specs,
            out_specs=pl.BlockSpec((rows, columns), lambda i, t: (t[1 + count, i], t[2 + count, i])),
        ),
        out_shape=jax.ShapeDtypeStruct(shape, F32),
        input_output_aliases=aliases,
        name=name,
        cost_estimate=pl.CostEstimate(
            flops=0, bytes_accessed=6 * steps * rows * columns, transcendentals=0
        ),
    )(table, *args)


class Plane:
    def __init__(self):
        self.np = lax.axis_size("pair")
        self.nf = lax.axis_size("fsdp")
        self.nr = lax.axis_size("rep")
        self.n = self.np * self.nf
        self.p = lax.axis_index("pair")
        self.f = lax.axis_index("fsdp")
        self.z = lax.axis_index("rep")
        self.place = self.p * self.nf + self.f
        self.unit = self.np * self.f + self.p
        self.cube = self.np == 2 and self.nf == 4
        self.line = self.nr == 4

    def gather(self, x, axis=0):
        if not self.cube:
            full = lax.all_gather(x, PLANE, axis=axis, tiled=True)
            return self.to_groups(full, axis)
        near = [x] + [swap(x, m) for m in ORDER[1:4]]
        far = [swap(piece, 1) for piece in near]
        return jnp.concatenate(near + far, axis=axis)

    def gather_x_first(self, x):
        if not self.cube:
            return self.gather(x)
        two = jnp.stack([x, swap(x, 2)])
        other = swap(two, 4)
        near = [two[0], other[0], two[1], other[1]]
        two_far, other_far = swap(two, 1), swap(other, 1)
        far = [two_far[0], other_far[0], two_far[1], other_far[1]]
        return jnp.concatenate(near + far, axis=0)

    def to_groups(self, x, axis=0):
        shape = x.shape
        y = x.reshape(shape[:axis] + (self.np, self.nf, -1) + shape[axis + 1 :])
        return jnp.swapaxes(y, axis, axis + 1).reshape(shape)

    def from_groups(self, x):
        y = x.reshape((self.nf, self.np, -1) + x.shape[1:])
        return jnp.swapaxes(y, 0, 1).reshape(x.shape)

    def scatter(self, left, right, product):
        rows = left.shape[0]
        if not self.cube:
            whole = self.from_groups(product(left, right).astype(BF16))
            return lax.psum_scatter(whole, PLANE, scatter_dimension=0, tiled=True).astype(F32)
        half = rows // 2
        far = swap(product(left[half:], right).astype(BF16), 1)
        near = product(left[:half], right) + far.astype(F32)
        size = half // 4
        total = near[:size]
        for i in (1, 2, 3):
            piece = near[i * size : (i + 1) * size].astype(BF16)
            total = total + swap(piece, ORDER[i]).astype(F32)
        return total

    def reshard(self, columns):
        if not self.cube:
            parts = jnp.stack([columns(self.np * i + self.p) for i in range(self.nf)])
            got = lax.all_to_all(parts, "fsdp", 0, 0, tiled=True)
            return got.reshape((-1,) + got.shape[2:])
        own = columns(self.unit)
        rows = own.shape[0]
        out = jnp.zeros((self.nf * rows,) + own.shape[1:], own.dtype)
        out = lax.dynamic_update_slice(out, own, (self.f * rows, 0))
        for k in (1, 2, 3):
            other = self.f ^ k
            got = swap(columns(self.np * other + self.p), k)
            out = lax.dynamic_update_slice(out, got, (other * rows, 0))
        return out

    def reshard_shared(self, columns, first):
        if not (self.cube and self.line):
            return self.reshard(columns)
        own = columns(self.unit)
        rows, width = own.shape
        quarter = rows // 4
        out = jnp.zeros((self.nf * rows, width), own.dtype)
        out = lax.dynamic_update_slice(out, own, (self.f * rows, 0))
        near = swap(columns(self.np * (self.f ^ 1) + self.p), 1)
        out = lax.dynamic_update_slice(out, near, ((self.f ^ 1) * rows, 0))
        got = []
        for k in (2, 3):
            piece = columns(self.np * (self.f ^ k) + self.p)
            piece = lax.dynamic_slice(piece, (self.z * quarter, 0), (quarter, width))
            got.append(swap(after(piece, *first), k))
        shards = self.line_gather(jnp.stack(got))
        for shard, where in zip(shards[::-1], self.line_shards()[::-1]):
            for i, k in enumerate((2, 3)):
                start = (self.f ^ k) * rows + where * quarter
                out = lax.dynamic_update_slice(out, shard[i], (start, 0))
        return out

    def line_shards(self):
        z = self.z
        return (
            z,
            jnp.maximum(z - 1, 0),
            jnp.minimum(z + 1, 3),
            jnp.where(z < 2, z + 2, z - 2),
            jnp.where(z == 0, 3, jnp.where(z == 3, 0, z)),
        )

    def line_gather(self, own):
        right = along(own, [(0, 1), (1, 2), (2, 3)])
        left = along(own, [(1, 0), (2, 1), (3, 2)])
        two = jnp.where(
            self.z < 2, along(left, [(1, 0), (2, 1)]), along(right, [(1, 2), (2, 3)])
        )
        three = along(two, [(2, 3), (1, 0)])
        return (own, right, left, two, three)

    def line_scatter(self, part):
        z = self.z

        def plus(i, *others):
            total = part(i).astype(F32)
            for other in others:
                total = total + other.astype(F32)
            return total.astype(BF16)

        three = along(plus(jnp.where(z == 0, 3, 0)), [(0, 1), (3, 2)])
        two = plus(jnp.where(z < 2, z + 2, z - 2), three)
        right = along(two, [(0, 1), (1, 2)])
        left = along(two, [(2, 1), (3, 2)])
        right = along(plus(jnp.minimum(z + 1, 3), right), [(0, 1), (1, 2), (2, 3)])
        left = along(plus(jnp.maximum(z - 1, 0), left), [(1, 0), (2, 1), (3, 2)])
        return plus(z, right, left)

    def table(self, blocks, rows_of, columns_of):
        z = self.z
        shard = jnp.repeat(jnp.arange(4), blocks)
        block = jnp.tile(jnp.arange(blocks), 4)
        apart = jnp.abs(shard - z)
        which = jnp.where(apart == 0, 0, jnp.where(apart == 1, jnp.where(shard < z, 1, 2), apart + 1))
        rows = [which]
        for b, held in enumerate(self.line_shards()):
            idle = jnp.where(shard > held, blocks - 1, 0)
            rows.append(jnp.where(which == b, block, idle))
        rows.append(rows_of(shard, block))
        rows.append(columns_of(shard, block))
        return jnp.stack([jnp.broadcast_to(r, shard.shape).astype(jnp.int32) for r in rows])

    def unit_of(self, place):
        return self.np * (place % self.nf) + place // self.nf

    def exchange(self, mine):
        if not self.cube:
            moved = lax.all_to_all(mine, PLANE, 0, 0, tiled=True)
            return moved, self.unit_of(jnp.arange(self.n))
        got = []
        for m in range(8):
            piece = lax.dynamic_index_in_dim(mine, self.place ^ m, 0, keepdims=False)
            got.append(swap(piece, m) if m else piece)
        return jnp.stack(got), self.unit_of(self.place ^ jnp.arange(8))

    def to_owner(self, x):
        pairs = []
        for p in range(self.np):
            for f in range(self.nf):
                pairs.append((p * self.nf + f, self.np * f + p))
        return lax.ppermute(x, PLANE, pairs)

    def sum_rows(self, term):
        rows, width = term.shape
        each = rows // (self.n * self.nr)
        split = term.astype(BF16).reshape(self.n, self.nr, each, width)
        if self.line:
            mine = self.line_scatter(lambda i: lax.dynamic_index_in_dim(split, i, 1, keepdims=False))
            moved, units = self.exchange(mine)
            return self.line_gather(moved), units
        mine = lax.psum_scatter(jnp.swapaxes(split, 0, 1), "rep", scatter_dimension=0)
        moved, units = self.exchange(mine)
        return lax.all_gather(moved, "rep", axis=0), units

    def sum_rows_full(self, term):
        shards, units = self.sum_rows(term)
        if self.line:
            full = jnp.zeros((4,) + shards[0].shape, BF16)
            for shard, where in zip(shards[::-1], self.line_shards()[::-1]):
                full = lax.dynamic_update_slice(full, shard[None], (where, 0, 0, 0))
        else:
            full = shards
        inverse = jnp.zeros((self.n,), jnp.int32).at[units].set(jnp.arange(self.n, dtype=jnp.int32))
        full = jnp.swapaxes(jnp.take(full, inverse, axis=1), 1, 2)
        return full.reshape((-1,) + full.shape[2:])

    def sum_units(self, term, name):
        rows, width = term.shape
        low = term.astype(BF16)
        if not self.line:
            mine = lax.psum_scatter(low, "rep", scatter_dimension=0, tiled=True)
            return lax.all_gather(self.to_owner(mine), "rep", axis=0, tiled=True).astype(F32)
        split = low.reshape(4, rows // 4, width)
        mine = self.line_scatter(lambda i: lax.dynamic_index_in_dim(split, i, 0, keepdims=False))
        shards = self.line_gather(self.to_owner(mine))
        table = self.table(1, lambda s, b: s, lambda s, b: 0)
        return place([x[None] for x in shards], table, (rows, width), None, name)

    def sum_gate_up(self, gate_term, up_term):
        ff = gate_term.shape[1]
        if not self.line:
            both = []
            for term in (gate_term, up_term):
                full = self.sum_rows_full(term)
                both.append(full.reshape(full.shape[0], -1))
            return jnp.concatenate(both, axis=1).astype(F32)
        out = None
        for i, term in enumerate((gate_term, up_term)):
            shards, units = self.sum_rows(term)
            table = self.table(
                self.n, lambda s, b: s, lambda s, b: i * self.n + jnp.take(units, b)
            )
            shape = (term.shape[0] // self.n, 2 * self.n * ff)
            out = place(shards, table, shape, out, "place_gate_up")
        return out

    def total(self, sums, top):
        if not (self.cube and self.line):
            everyone = ("pair", "fsdp", "rep")
            return lax.psum(sums, everyone), lax.pmax(top, everyone)
        count = sums.shape[0]
        both = jnp.concatenate([sums, top], axis=0)

        def join(a, b):
            return jnp.concatenate(
                [a[:count] + b[:count], jnp.maximum(a[count:], b[count:])], axis=0
            )

        for m in (1, 2, 4):
            both = join(both, swap(both, m))
        ends = [(0, 1), (3, 2)]
        inner = (self.z == 1) | (self.z == 2)
        both = jnp.where(inner, join(both, along(both, ends)), both)
        both = join(both, along(both, [(1, 2), (2, 1)]))
        both = jnp.where(inner, both, along(both, [(1, 0), (2, 3)]))
        return both[:count], both[count:]


def norm_back(grad_normed, unit, inv_scale, gain):
    scaled = grad_normed * gain
    grad_in = inv_scale * (scaled - unit * jnp.mean(scaled * unit, axis=-1, keepdims=True))
    return (grad_in, jnp.sum(grad_normed * unit, axis=0))


def on_device(
    tokens,
    cotangent,
    segment_ids,
    positions,
    q_weight,
    k_weight,
    v_weight,
    o_weight,
    attn_gain,
    gate_up_weight,
    down_weight,
    mlp_gain,
):
    plane = Plane()
    unit, n = plane.unit, plane.n
    heads = HEADS // n
    share = max(1, n // KV_HEADS)
    q_cols = heads * HEAD
    ff = FF // n
    length = plane.np * tokens.shape[0]

    def qkv_columns(u):
        rows = q_weight.shape[0]
        return jnp.concatenate(
            [
                lax.dynamic_slice(q_weight, (0, u * q_cols), (rows, q_cols)),
                lax.dynamic_slice(k_weight, (0, (u // share) * HEAD), (rows, HEAD)),
                lax.dynamic_slice(v_weight, (0, (u // share) * HEAD), (rows, HEAD)),
            ],
            axis=1,
        )

    def mlp_columns(u):
        rows = gate_up_weight.shape[0]
        return jnp.concatenate(
            [
                lax.dynamic_slice(gate_up_weight, (0, u * ff), (rows, ff)),
                lax.dynamic_slice(gate_up_weight, (0, FF + u * ff), (rows, ff)),
            ],
            axis=1,
        )

    tokens_all = plane.gather_x_first(tokens)
    w_qkv = plane.reshard(qkv_columns)
    gains = lax.all_gather(jnp.stack([attn_gain, mlp_gain]), "fsdp", axis=1, tiled=True)
    gain_one = gains[0].astype(F32)
    gain_two = gains[1].astype(F32)
    where = plane.gather(jnp.stack([segment_ids, positions]), axis=1)
    segments = where[0].reshape(-1, length)
    places = where[1].reshape(-1, length)
    visible = (
        (segments[:, None, :] == 0) | (segments[:, None, :] == segments[:, :, None])
    ) & (places[:, None, :] <= places[:, :, None])
    visible = visible.astype(F32).reshape(-1, length)
    cosine, sine = rope_tables(places.reshape(-1), heads)
    w_out = lax.dynamic_slice(o_weight, (plane.p * q_cols, 0), (q_cols, D))
    w_down = lax.dynamic_slice(down_weight, (plane.p * ff, 0), (ff, D))

    inputs_all = tokens_all.astype(F32)
    inv_all = lax.rsqrt(jnp.mean(inputs_all * inputs_all, axis=-1, keepdims=True) + EPS)
    normed = (inputs_all * inv_all * gain_one).astype(BF16)
    lin = dot(normed, w_qkv)
    count = lin.shape[0]
    flops = 4 * count * length * HEAD * heads
    qkv, attended, tops = by_group(
        attend_kernel,
        heads,
        length,
        [lin, cosine, sine, visible],
        [
            jax.ShapeDtypeStruct(lin.shape, BF16),
            jax.ShapeDtypeStruct((count, q_cols), BF16),
            jax.ShapeDtypeStruct((8 * (count // length), 128), F32),
        ],
        "attend",
        flops,
    )

    w_gate_up = plane.reshard_shared(mlp_columns, (tokens_all, w_qkv))
    grad_out = cotangent.astype(F32)
    low_out = after((RESID * grad_out).astype(BF16), tokens_all)
    grad_branch = plane.gather_x_first(low_out)
    grad_hidden = times_t(grad_branch, w_down)

    inputs = tokens.astype(F32)
    middle = inputs + RESID * plane.scatter(attended, w_out, dot)
    inv_two = lax.rsqrt(jnp.mean(middle * middle, axis=-1, keepdims=True) + EPS)
    unit_two = middle * inv_two
    normed_mlp = plane.gather((unit_two * gain_two).astype(BF16))

    gate_up = dot(normed_mlp, w_gate_up)
    gate = gate_up[:, :ff]
    up_part = gate_up[:, ff:]
    sigma = jax.nn.sigmoid(gate)
    silu_gate = gate * sigma
    hidden = (silu_gate * up_part).astype(BF16)
    grad_gate = (grad_hidden * up_part * sigma * (1.0 + gate * (1.0 - sigma))).astype(BF16)
    grad_up = (grad_hidden * silu_gate).astype(BF16)
    grad_gate_up = jnp.concatenate([grad_gate, grad_up], axis=1)
    down_grad = plane.sum_units(outer(hidden, grad_branch), "place_down")
    gate_up_grad = plane.sum_gate_up(outer(normed_mlp, grad_gate), outer(normed_mlp, grad_up))
    grad_normed_mlp = plane.scatter(grad_gate_up, w_gate_up, times_t)
    result = (middle + RESID * plane.scatter(hidden, w_down, dot)).astype(BF16)

    grad_mid_norm, gain_two_grad = norm_back(grad_normed_mlp, unit_two, inv_two, gain_two)
    grad_middle = grad_out + grad_mid_norm
    grad_attn_branch = plane.gather((RESID * grad_middle).astype(BF16))
    grad_attended = times_t(grad_attn_branch, w_out).astype(BF16)
    o_grad = plane.sum_units(outer(attended, grad_attn_branch), "place_o")
    (grad_lin,) = by_group(
        attend_back_kernel,
        heads,
        length,
        [qkv, cosine, sine, visible, grad_attended],
        [jax.ShapeDtypeStruct(lin.shape, BF16)],
        "attend_back",
        3 * flops,
    )
    grad_normed = plane.scatter(grad_lin, w_qkv, times_t)
    lin_rows = plane.sum_rows_full(outer(normed, grad_lin)).astype(F32)
    inv_one = lax.rsqrt(jnp.mean(inputs * inputs, axis=-1, keepdims=True) + EPS)
    grad_in_norm, gain_one_grad = norm_back(grad_normed, inputs * inv_one, inv_one, gain_one)
    input_grad = (grad_middle + grad_in_norm).astype(BF16)

    top_local = jnp.max(tops.reshape(-1, 8, 128), axis=(0, 2))[:heads]
    top_row = jnp.full((1, D), -jnp.inf, F32)
    top_row = lax.dynamic_update_slice(top_row, top_local[None], (0, unit * heads))
    gain_grads, top_row = plane.total(jnp.stack([gain_one_grad, gain_two_grad]), top_row)
    factor = TAU / jnp.maximum(top_row[0, :HEADS], TAU)
    k_factor = jnp.repeat(jnp.min(factor.reshape(KV_HEADS, GROUP), axis=1), HEAD)
    rows = lin_rows.shape[0]
    q_update = lin_rows[..., :q_cols].reshape(rows, D) * jnp.repeat(factor, HEAD)[None, :]
    kv = lin_rows[..., q_cols:].reshape(rows, n // share, share, 2 * HEAD).sum(axis=2)
    k_update = kv[..., :HEAD].reshape(rows, -1) * k_factor[None, :]
    v_grad = kv[..., HEAD:].reshape(rows, -1)
    gain_grads = lax.dynamic_slice(gain_grads, (0, plane.place * (D // n)), (2, D // n))
    return (
        result,
        input_grad,
        q_update,
        k_update,
        v_grad,
        o_grad,
        gain_grads[0],
        gate_up_grad,
        down_grad,
        gain_grads[1],
    )


def solution(mesh):
    tokens = P(("pair", "fsdp", "rep"))
    shard = P("fsdp")
    owned = P(("pair", "fsdp"))
    return jax.shard_map(
        on_device,
        mesh=mesh,
        in_specs=(tokens,) * 4 + (shard,) * 8,
        out_specs=(tokens, tokens) + (owned,) * 8,
        check_vma=False,
    )
```

time: 1090 us -> 993 us (0.911)
  starting transfers between devices: 52.8 us -> 221 us
  blocking collectives: 149 us -> 8.83 us
  waiting for transfers between devices: 486 us -> 404 us
  local copies, waits for them, and re-layouts: 183 us -> 105 us
  Pallas kernels: 0 us -> 70.3 us
  matrix products: 131 us -> 107 us
  between operations: 16.1 us -> 3.16 us
    ppermute x2 -> x60, waiting for transfers between devices: 0.01 us -> 311 us  [the longest x58 311 us: along(): return lax.ppermute(x, 'rep', pairs)]
    reduce_scatter x4 -> x0, waiting for transfers between devices: 213 us -> none  [the longest x2 150 us: sum_rows(): lax.psum_scatter(jnp.swapaxes(split, 0, 1), 'rep', scatter_dimension=0)]
    ppermute x2 -> x60, starting transfers between devices: 3.48 us -> 145 us  [the longest x58 135 us: along(): return lax.ppermute(x, 'rep', pairs)]
    ppermute x64 -> x75, waiting for transfers between devices: 195 us -> 93 us  [swap(): return lax.ppermute(x, PLANE, [(i, i ^ mask) for i in range(devices)])]
    all_gather x4 -> x0, waiting for transfers between devices: 78.7 us -> none  [the longest x2 78.6 us: sum_rows(): full = lax.all_gather(moved, 'rep', axis=0)]
    pallas_call x0 -> x6, Pallas kernels: none -> 70.3 us  [the longest x4 50.2 us: place(): pl.pallas_call(lambda t, *refs: place_kernel(count, t, *refs), grid_spec=...]
    convert_element_type x5 -> x0, local copies, waits for them, and re-layouts: 65.9 us -> none  [the longest x4 65.5 us: on_device(): jnp.swapaxes(gate_up_rows, 1, 2).reshape(owned, 2 * FF).astype(F32)]
    psum x1 -> x0, blocking collectives: 57.6 us -> none  [on_device(): lax.psum(jnp.stack([gain_one_grad, gain_two_grad]), ('pair', 'fsdp', 'rep'))]
  transfers between devices with their start and end apart: 74 -> 135, of which waited for: 28 -> 52; matrix products, arithmetic and copies ran while one was open for 20% -> 22% of each run, Pallas kernels for 0% -> 6%
where the time goes in v2:
time: 993 us; the launch traced here: 984 us
  waiting for transfers between devices  404 us (41%)
  starting transfers between devices  221 us (22%)
  matrix products  107 us (11%)
  local copies, waits for them, and re-layouts  105 us (11%)
  Pallas kernels  70.3 us (7%)
  other arithmetic  65.4 us (7%)
    ppermute x58, waiting for transfers between devices, along(): return lax.ppermute(x, 'rep', pairs)  311 us
    ppermute x58, starting transfers between devices, along(): return lax.ppermute(x, 'rep', pairs)  135 us
    ppermute x75, waiting for transfers between devices, swap(): return lax.ppermute(x, PLANE, [(i, i ^ mask) for i in range(devices)])  93 us
    ppermute x75, starting transfers between devices, swap(): return lax.ppermute(x, PLANE, [(i, i ^ mask) for i in range(devices)])  75.2 us
    pallas_call x4, Pallas kernels, place(): pl.pallas_call(lambda t, *refs: place_kernel(count, t, *refs), grid_spec=...  50.2 us
    dot_general x6, matrix products, times_t(): lax.dot_general(left, right, (((1,), (1,)), ((), ())), preferred_element_...  43.9 us
    dot_general x6, matrix products, dot(): return jnp.dot(left, right, preferred_element_type=F32)  35.1 us
    unnamed x185, local copies, waits for them, and re-layouts  29 us
  transfers between devices with their start and end apart: 135, of which 52 were waited for; matrix products, arithmetic and copies ran while one was open for 22% of the time, Pallas kernels for 6%

profile of v2, /device:TPU:0, one launch (start us, length us, event | category | flops | bytes accessed | tf_op | source)
XLA Modules:
  0.0 984.0 jit_solution(6878338412868947275)
XLA Ops:
  138.0 11.5 %collective-permute-done.26 = bf16[128,2048]{1,0:T(8,128)(2,1)} collective-permute-done((bf16[128,2048]{1,0:T(8,128)(2,1)}, bf16[128,2048]{1,0:T(8,128)(2,1)}, u32[]{:S(2)}, u32[]{:S(2)}) %collective-permute-start.26) | collective-permute-done | bytes 524320 | tf_op jit(solution)/shard_map/ppermute | solution.py:40
  165.2 12.4 %collective-permute-done.28 = bf16[2,128,2048]{2,1,0:T(8,128)(2,1)S(1)} collective-permute-done((bf16[2,128,2048]{2,1,0:T(8,128)(2,1)S(1)}, bf16[2,128,2048]{2,1,0:T(8,128)(2,1)S(1)}, u32[]{:S(2)}, u32[]{:S(2)}) %collective-permute-start.28) | collective-permute-done | bytes 1048608 | tf_op jit(solution)/shard_map/ppermute | solution.py:44
  190.3 14.9 %collective-permute-done.29 = bf16[2,128,2048]{2,1,0:T(8,128)(2,1)S(1)} collective-permute-done((bf16[2,128,2048]{2,1,0:T(8,128)(2,1)S(1)}, bf16[2,128,2048]{2,1,0:T(8,128)(2,1)S(1)}, u32[]{:S(2)}, u32[]{:S(2)}) %collective-permute-start.29) | collective-permute-done | bytes 1048608 | tf_op jit(solution)/shard_map/ppermute | solution.py:44
  222.7 12.1 %collective-permute-done.32 = bf16[2,128,2048]{2,1,0:T(8,128)(2,1)S(1)} collective-permute-done((bf16[2,128,2048]{2,1,0:T(8,128)(2,1)S(1)}, bf16[2,128,2048]{2,1,0:T(8,128)(2,1)S(1)}, u32[]{:S(2)}, u32[]{:S(2)}) %collective-permute-start.32) | collective-permute-done | bytes 1048608 | tf_op jit(solution)/shard_map/ppermute | solution.py:44
  245.2 13.2 %fusion.137 = f32[1024,2048]{1,0:T(8,128)} fusion(bf16[1024,2048]{1,0:T(8,128)(2,1)S(1)} %constant_dynamic-update-slice_fusion.10, bf16[2048,2048]{1,0:T(8,128)(2,1)} %constant_dynamic-update-slice_fusion.52), kind=kOutput, calls=%fused_computation.407 | convolution fusion | flops 8589934592 | bytes 20971520 | tf_op jit(solution)/shard_map/dot_general | solution.py:28
  258.4 11.3 %multiply_convert_fusion.1 = (bf16[1024,1024]{1,0:T(8,128)(2,1)}, bf16[1024,1024]{1,0:T(8,128)(2,1)}, bf16[1024,1024]{1,0:T(8,128)(2,1)}) fusion(f32[1024,2048]{1,0:T(8,128)} %fusion.137, bf16[1024,2048]{1,0:T(8,128)(2,1)S(1)} %fusion.77, bf16[2048,2048]{1,0:T(8,128)(2,1)} %param.24, s32[]{:T(128)S(6)} %select_n.669), kind=kOutput, calls=%fused_computation.13 | convolution fusion | flops 4310695936 | bytes 23068676 | tf_op jit(solution)/shard_map/dot_general | solution.py:36
  276.4 9.1 convolution_convert_fusion.5
  325.0 15.7 %collective-permute-done.107 = bf16[8,64,1024]{2,1,0:T(8,128)(2,1)S(1)} collective-permute-done((bf16[8,64,1024]{2,1,0:T(8,128)(2,1)S(1)}, bf16[8,64,1024]{2,1,0:T(8,128)(2,1)S(1)}, u32[]{:S(2)}, u32[]{:S(2)}) %collective-permute-start.107) | collective-permute-done | bytes 1048608 | tf_op jit(solution)/shard_map/ppermute | solution.py:44
  343.8 19.4 %collective-permute-done.124 = bf16[256,2048]{1,0:T(8,128)(2,1)S(1)} collective-permute-done((bf16[256,2048]{1,0:T(8,128)(2,1)S(1)}, bf16[256,2048]{1,0:T(8,128)(2,1)S(1)}, u32[]{:S(2)}, u32[]{:S(2)}) %collective-permute-start.124) | collective-permute-done | bytes 1048608 | tf_op jit(solution)/shard_map/ppermute | solution.py:44
  370.8 11.9 %fusion.134 = (bf16[512,2048]{1,0:T(8,128)(2,1)}, f32[512,2048]{1,0:T(8,128)}) fusion(bf16[512,2048]{1,0:T(8,128)(2,1)} %collective-permute-done.41, bf16[2048,2048]{1,0:T(8,128)(2,1)} %constant_dynamic-update-slice_fusion.52, bf16[1024,1024]{1,0:T(8,128)(2,1)} %get-tuple-element.71, bf16[1024,1024]{1,0:T(8,128)(2,1)} %get-tuple-element.72), kind=kOutput, calls=%fused_computation.404 | convolution fusion | flops 4302307328 | bytes 20971520 | tf_op jit(solution)/shard_map/dot_general | solution.py:36
  393.5 14.7 %collective-permute-done.108 = bf16[8,64,1024]{2,1,0:T(8,128)(2,1)S(1)} collective-permute-done((bf16[8,64,1024]{2,1,0:T(8,128)(2,1)}, bf16[8,64,1024]{2,1,0:T(8,128)(2,1)S(1)}, u32[]{:S(2)}, u32[]{:S(2)}) %collective-permute-start.108) | collective-permute-done | bytes 1048608 | tf_op jit(solution)/shard_map/ppermute | solution.py:44
  420.7 9.5 collective-permute-done.125
  448.2 10.3 %collective-permute-done.94 = bf16[8,64,1024]{2,1,0:T(8,128)(2,1)S(1)} collective-permute-done((bf16[8,64,1024]{2,1,0:T(8,128)(2,1)S(1)}, bf16[8,64,1024]{2,1,0:T(8,128)(2,1)S(1)}, u32[]{:S(2)}, u32[]{:S(2)}) %collective-permute-start.94) | collective-permute-done | bytes 1048608 | tf_op jit(solution)/shard_map/ppermute | solution.py:44
  464.8 16.1 %collective-permute-done.111 = bf16[8,64,1024]{2,1,0:T(8,128)(2,1)S(1)} collective-permute-done((bf16[8,64,1024]{2,1,0:T(8,128)(2,1)S(1)}, bf16[8,64,1024]{2,1,0:T(8,128)(2,1)S(1)}, u32[]{:S(2)}, u32[]{:S(2)}) %collective-permute-start.111) | collective-permute-done | bytes 1048608 | tf_op jit(solution)/shard_map/ppermute | solution.py:44
  485.4 10.4 %collective-permute-done.46 = bf16[128,2048]{1,0:T(8,128)(2,1)S(1)} collective-permute-done((bf16[128,2048]{1,0:T(8,128)(2,1)S(1)}, bf16[128,2048]{1,0:T(8,128)(2,1)S(1)}, u32[]{:S(2)}, u32[]{:S(2)}) %collective-permute-start.46) | collective-permute-done | bytes 524320 | tf_op jit(solution)/shard_map/ppermute | solution.py:40
  547.4 12.1 %attend_back.1 = bf16[1024,384]{1,0:T(8,128)(2,1)} custom-call(bf16[1024,384]{1,0:T(8,128)(2,1)} %get-tuple-element.21.refs_0_, f32[1024,384]{1,0:T(8,128)} %concatenate.73.refs_1_, f32[1024,384]{1,0:T(8,128)} %concatenate.74.refs_2_, f32[1024,256]{1,0:T(8,128)} %fusion.63.refs_3_, bf16[1024,256]{1,0:T(8,128)(2,1)} %convolution_convert_fusion.8.refs_4_), custom_call_target="tpu_custom_call" | custom-call | flops 805306368 | bytes 6815744 | tf_op jit(solution)/shard_map/attend_back/pallas_call | solution.py:130
  649.4 36.9 %collective-permute-done.86 = bf16[64,2048]{1,0:T(8,128)(2,1)S(1)} collective-permute-done((bf16[64,2048]{1,0:T(8,128)(2,1)S(1)}, bf16[64,2048]{1,0:T(8,128)(2,1)S(1)}, u32[]{:S(2)}, u32[]{:S(2)}) %collective-permute-start.86) | collective-permute-done | bytes 262176 | tf_op jit(solution)/shard_map/ppermute | solution.py:44
  705.9 22.4 %collective-permute-done.68 = bf16[8,64,384]{2,1,0:T(8,128)(2,1)} collective-permute-done((bf16[8,64,384]{2,1,0:T(8,128)(2,1)S(1)}, bf16[8,64,384]{2,1,0:T(8,128)(2,1)}, u32[]{:S(2)}, u32[]{:S(2)}) %collective-permute-start.68) | collective-permute-done | bytes 393248 | tf_op jit(solution)/shard_map/ppermute | solution.py:44
  737.7 18.5 %collective-permute-done.121 = bf16[8,64,1024]{2,1,0:T(8,128)(2,1)S(1)} collective-permute-done((bf16[8,64,1024]{2,1,0:T(8,128)(2,1)S(1)}, bf16[8,64,1024]{2,1,0:T(8,128)(2,1)S(1)}, u32[]{:S(2)}, u32[]{:S(2)}) %collective-permute-start.121) | collective-permute-done | bytes 1048608 | tf_op jit(solution)/shard_map/ppermute | solution.py:44
  769.9 9.5 collective-permute-start.129
  855.1 24.9 %collective-permute-done.132 = bf16[256,2048]{1,0:T(8,128)(2,1)S(1)} collective-permute-done((bf16[256,2048]{1,0:T(8,128)(2,1)}, bf16[256,2048]{1,0:T(8,128)(2,1)S(1)}, u32[]{:S(2)}, u32[]{:S(2)}) %collective-permute-start.132) | collective-permute-done | bytes 1048608 | tf_op jit(solution)/shard_map/ppermute | solution.py:44
  897.0 33.7 %collective-permute-done.123.refs_4_ = bf16[8,64,1024]{2,1,0:T(8,128)(2,1)} collective-permute-done((bf16[8,64,1024]{2,1,0:T(8,128)(2,1)}, bf16[8,64,1024]{2,1,0:T(8,128)(2,1)}, u32[]{:S(2)}, u32[]{:S(2)}) %collective-permute-start.123) | collective-permute-done | bytes 1048608 | tf_op jit(solution)/shard_map/ppermute | solution.py:44
  930.7 19.7 %place_gate_up.2.refs_5_ = f32[256,16384]{1,0:T(8,128)} custom-call(s32[8,32]{1,0:T(8,128)} %stack.207.t, bf16[8,64,1024]{2,1,0:T(8,128)(2,1)} %copy-done.19, bf16[8,64,1024]{2,1,0:T(8,128)(2,1)} %copy-done.23, bf16[8,64,1024]{2,1,0:T(8,128)(2,1)} %copy-done.24, bf16[8,64,1024]{2,1,0:T(8,128)(2,1)} %broadcast_select_fusion.1.refs_3_, ...), custom_call_target="tpu_custom_call" | custom-call | bytes 12582912 | tf_op jit(solution)/shard_map/place_gate_up/pallas_call | solution.py:168
  950.4 19.8 %place_gate_up.3 = f32[256,16384]{1,0:T(8,128)} custom-call(s32[8,32]{1,0:T(8,128)} %stack.197.t, bf16[8,64,1024]{2,1,0:T(8,128)(2,1)} %constant_dynamic-update-slice_fusion.36.refs_0_, bf16[8,64,1024]{2,1,0:T(8,128)(2,1)} %collective-permute-done.102.refs_1_, bf16[8,64,1024]{2,1,0:T(8,128)(2,1)} %copy-done.22, ...), custom_call_target="tpu_custom_call", output_to_operand_aliasing={{}: (6, {})} | custom-call | bytes 12582912 | tf_op jit(solution)/shard_map/place_gate_up/pallas_call | solution.py:168
  (627 shorter events, 590.7 us)
Async XLA Ops:
  2.1 50.3 %collective-permute-start.7 = (s32[2,128]{1,0:T(2,128)}, s32[2,128]{1,0:T(2,128)}, u32[]{:S(2)}, u32[]{:S(2)}) collective-permute-start(s32[2,128]{1,0:T(2,128)} %get-tuple-element.150), channel_id=1, source_target_pairs={{0,16},{4,20},{8,24},{12,28},{16,0},{20,4},{24,8},{28,12},{1,17},{... | collective-permute-start | bytes 3080 | tf_op jit(solution)/shard_map/ppermute | solution.py:40
  5.0 48.4 %collective-permute-start.8 = (s32[2,128]{1,0:T(2,128)}, s32[2,128]{1,0:T(2,128)}, u32[]{:S(2)}, u32[]{:S(2)}) collective-permute-start(s32[2,128]{1,0:T(2,128)} %get-tuple-element.150), channel_id=1, source_target_pairs={{0,8},{4,12},{8,0},{12,4},{16,24},{20,28},{24,16},{28,20},{1,9},{5... | collective-permute-start | bytes 3080 | tf_op jit(solution)/shard_map/ppermute | solution.py:40
  6.5 49.3 %collective-permute-start.9 = (s32[2,128]{1,0:T(2,128)}, s32[2,128]{1,0:T(2,128)}, u32[]{:S(2)}, u32[]{:S(2)}) collective-permute-start(s32[2,128]{1,0:T(2,128)} %get-tuple-element.150), channel_id=1, source_target_pairs={{0,24},{4,28},{8,16},{12,20},{16,8},{20,12},{24,0},{28,4},{1,25},{... | collective-permute-start | bytes 3080 | tf_op jit(solution)/shard_map/ppermute | solution.py:40
  6.5 50.0 %collective-permute-start.10 = (s32[2,128]{1,0:T(2,128)}, s32[2,128]{1,0:T(2,128)}, u32[]{:S(2)}, u32[]{:S(2)}) collective-permute-start(s32[2,128]{1,0:T(2,128)} %get-tuple-element.150), channel_id=1, source_target_pairs={{0,4},{4,0},{8,12},{12,8},{16,20},{20,16},{24,28},{28,24},{1,5},{5... | collective-permute-start | bytes 3080 | tf_op jit(solution)/shard_map/ppermute | solution.py:40
  6.5 54.2 %collective-permute-start = (bf16[128,2048]{1,0:T(8,128)(2,1)}, bf16[128,2048]{1,0:T(8,128)(2,1)}, u32[]{:S(2)}, u32[]{:S(2)}) collective-permute-start(bf16[128,2048]{1,0:T(8,128)(2,1)} %param.14), channel_id=1, source_target_pairs={{0,8},{4,12},{8,0},{12,4},{16,24},{20,28},{24,16},{28,20},{1,9},{5... | collective-permute-start | bytes 1572872 | tf_op jit(solution)/shard_map/ppermute | solution.py:40
  60.4 65.1 %collective-permute-start.25 = (bf16[512,2048]{1,0:T(8,128)(2,1)}, bf16[512,2048]{1,0:T(8,128)(2,1)}, u32[]{:S(2)}, u32[]{:S(2)}) collective-permute-start(bf16[512,2048]{1,0:T(8,128)(2,1)} %pad_maximum_fusion.2), channel_id=1, source_target_pairs={{0,4},{4,0},{8,12},{12,8},{16,20},{20,16},{24,28},{28,24},{1,5},{5... | collective-permute-start | bytes 6291464 | tf_op jit(solution)/shard_map/ppermute | solution.py:40
  292.7 76.3 %collective-permute-start.41 = (bf16[512,2048]{1,0:T(8,128)(2,1)S(1)}, bf16[512,2048]{1,0:T(8,128)(2,1)}, u32[]{:S(2)}, u32[]{:S(2)}) collective-permute-start(bf16[512,2048]{1,0:T(8,128)(2,1)S(1)} %copy-done.57), channel_id=1, source_target_pairs={{0,4},{4,0},{8,12},{12,8},{16,20},{20,16},{24,28},{28,24},{1,5},{5... | collective-permute-start | bytes 6291464 | tf_op jit(solution)/shard_map/ppermute | solution.py:40
  303.2 60.0 %collective-permute-start.124 = (bf16[256,2048]{1,0:T(8,128)(2,1)S(1)}, bf16[256,2048]{1,0:T(8,128)(2,1)S(1)}, u32[]{:S(2)}, u32[]{:S(2)}) collective-permute-start(bf16[256,2048]{1,0:T(8,128)(2,1)S(1)} %dynamic-slice_bitcast_fusion), channel_id=1, source_target_pairs={{0,1},{3,2},{4,5},{7,6},{8,9},{11,10},{12,13},{15,14},{16,17},{19,... | collective-permute-start | bytes 3145736 | tf_op jit(solution)/shard_map/ppermute | solution.py:44
  310.0 102.4 %collective-permute-start.33 = (bf16[512,2048]{1,0:T(8,128)(2,1)}, bf16[512,2048]{1,0:T(8,128)(2,1)}, u32[]{:S(2)}, u32[]{:S(2)}) collective-permute-start(bf16[512,2048]{1,0:T(8,128)(2,1)} %fusion.12), channel_id=1, source_target_pairs={{0,4},{4,0},{8,12},{12,8},{16,20},{20,16},{24,28},{28,24},{1,5},{5... | collective-permute-start | bytes 6291464 | tf_op jit(solution)/shard_map/ppermute | solution.py:40
  319.7 66.1 %collective-permute-start.91 = (bf16[8,64,1024]{2,1,0:T(8,128)(2,1)}, bf16[8,64,1024]{2,1,0:T(8,128)(2,1)}, u32[]{:S(2)}, u32[]{:S(2)}) collective-permute-start(bf16[8,64,1024]{2,1,0:T(8,128)(2,1)} %fusion.29), channel_id=1, source_target_pairs={{0,1},{1,2},{4,5},{5,6},{8,9},{9,10},{12,13},{13,14},{16,17},{17,1... | collective-permute-start | bytes 3145736 | tf_op jit(solution)/shard_map/ppermute | solution.py:44
  340.7 49.5 %collective-permute-start.93 = (bf16[8,64,1024]{2,1,0:T(8,128)(2,1)}, bf16[8,64,1024]{2,1,0:T(8,128)(2,1)}, u32[]{:S(2)}, u32[]{:S(2)}) collective-permute-start(bf16[8,64,1024]{2,1,0:T(8,128)(2,1)} %fusion.29), channel_id=1, source_target_pairs={{2,1},{3,2},{6,5},{7,6},{10,9},{11,10},{14,13},{15,14},{18,17},{19... | collective-permute-start | bytes 3145736 | tf_op jit(solution)/shard_map/ppermute | solution.py:44
  444.7 180.1 %collective-permute-start.128 = (bf16[256,2048]{1,0:T(8,128)(2,1)}, bf16[256,2048]{1,0:T(8,128)(2,1)}, u32[]{:S(2)}, u32[]{:S(2)}) collective-permute-start(bf16[256,2048]{1,0:T(8,128)(2,1)} %get-tuple-element.75), channel_id=1, source_target_pairs={{1,0},{2,1},{3,2},{5,4},{6,5},{7,6},{9,8},{10,9},{11,10},{13,12},{... | collective-permute-start | bytes 3145736 | tf_op jit(solution)/shard_map/ppermute | solution.py:44
  458.5 167.8 %collective-permute-start.126 = (bf16[256,2048]{1,0:T(8,128)(2,1)}, bf16[256,2048]{1,0:T(8,128)(2,1)}, u32[]{:S(2)}, u32[]{:S(2)}) collective-permute-start(bf16[256,2048]{1,0:T(8,128)(2,1)} %get-tuple-element.74), channel_id=1, source_target_pairs={{0,1},{1,2},{2,3},{4,5},{5,6},{6,7},{8,9},{9,10},{10,11},{12,13},{... | collective-permute-start | bytes 3145736 | tf_op jit(solution)/shard_map/ppermute | solution.py:44
  538.5 92.1 %collective-permute-start.102 = (bf16[8,64,1024]{2,1,0:T(8,128)(2,1)}, bf16[8,64,1024]{2,1,0:T(8,128)(2,1)}, u32[]{:S(2)}, u32[]{:S(2)}) collective-permute-start(bf16[8,64,1024]{2,1,0:T(8,128)(2,1)} %constant_dynamic-update-slice_fusion.36.refs_0_), channel_id=1, source_target_pairs={{0,1},{1,2},{2,3},{4,5},{5,6},{6,7},{8,9},{9,10},{10,11},{12,13},{... | collective-permute-start | bytes 3145736 | tf_op jit(solution)/shard_map/ppermute | solution.py:44
  630.7 57.6 %collective-permute-start.103 = (bf16[8,64,1024]{2,1,0:T(8,128)(2,1)}, bf16[8,64,1024]{2,1,0:T(8,128)(2,1)S(1)}, u32[]{:S(2)}, u32[]{:S(2)}) collective-permute-start(bf16[8,64,1024]{2,1,0:T(8,128)(2,1)} %constant_dynamic-update-slice_fusion.36.refs_0_), channel_id=1, source_target_pairs={{1,0},{2,1},{3,2},{5,4},{6,5},{7,6},{9,8},{10,9},{11,10},{13,12},{... | collective-permute-start | bytes 3145736 | tf_op jit(solution)/shard_map/ppermute | solution.py:44
  632.0 56.4 %collective-permute-start.119 = (bf16[8,64,1024]{2,1,0:T(8,128)(2,1)S(1)}, bf16[8,64,1024]{2,1,0:T(8,128)(2,1)S(1)}, u32[]{:S(2)}, u32[]{:S(2)}) collective-permute-start(bf16[8,64,1024]{2,1,0:T(8,128)(2,1)S(1)} %copy-done.20), channel_id=1, source_target_pairs={{0,1},{1,2},{2,3},{4,5},{5,6},{6,7},{8,9},{9,10},{10,11},{12,13},{... | collective-permute-start | bytes 3145736 | tf_op jit(solution)/shard_map/ppermute | solution.py:44
  637.1 52.6 %collective-permute-start.120 = (bf16[8,64,1024]{2,1,0:T(8,128)(2,1)S(1)}, bf16[8,64,1024]{2,1,0:T(8,128)(2,1)S(1)}, u32[]{:S(2)}, u32[]{:S(2)}) collective-permute-start(bf16[8,64,1024]{2,1,0:T(8,128)(2,1)S(1)} %copy-done.20), channel_id=1, source_target_pairs={{1,0},{2,1},{3,2},{5,4},{6,5},{7,6},{9,8},{10,9},{11,10},{13,12},{... | collective-permute-start | bytes 3145736 | tf_op jit(solution)/shard_map/ppermute | solution.py:44
  688.3 97.2 %collective-permute-start.52 = (bf16[512,2048]{1,0:T(8,128)(2,1)}, bf16[512,2048]{1,0:T(8,128)(2,1)}, u32[]{:S(2)}, u32[]{:S(2)}) collective-permute-start(bf16[512,2048]{1,0:T(8,128)(2,1)} %convolution_convert_fusion.4), channel_id=1, source_target_pairs={{0,4},{4,0},{8,12},{12,8},{16,20},{20,16},{24,28},{28,24},{1,5},{5... | collective-permute-start | bytes 6291464 | tf_op jit(solution)/shard_map/ppermute | solution.py:40
  733.9 49.4 %collective-permute-start.69 = (bf16[8,64,384]{2,1,0:T(8,128)(2,1)}, bf16[8,64,384]{2,1,0:T(8,128)(2,1)}, u32[]{:S(2)}, u32[]{:S(2)}) collective-permute-start(bf16[8,64,384]{2,1,0:T(8,128)(2,1)} %collective-permute-done.68), channel_id=1, source_target_pairs={{1,0},{2,1},{5,4},{6,5},{9,8},{10,9},{13,12},{14,13},{17,16},{18,1... | collective-permute-start | bytes 1179656 | tf_op jit(solution)/shard_map/ppermute | solution.py:44
  756.2 134.3 %collective-permute-start.36 = (bf16[128,2048]{1,0:T(8,128)(2,1)}, bf16[128,2048]{1,0:T(8,128)(2,1)}, u32[]{:S(2)}, u32[]{:S(2)}) collective-permute-start(bf16[128,2048]{1,0:T(8,128)(2,1)} %get-tuple-element.89), channel_id=1, source_target_pairs={{0,24},{4,28},{8,16},{12,20},{16,8},{20,12},{24,0},{28,4},{1,25},{... | collective-permute-start | bytes 1572872 | tf_op jit(solution)/shard_map/ppermute | solution.py:40
  812.2 79.7 %collective-permute-start.35 = (bf16[128,2048]{1,0:T(8,128)(2,1)}, bf16[128,2048]{1,0:T(8,128)(2,1)}, u32[]{:S(2)}, u32[]{:S(2)}) collective-permute-start(bf16[128,2048]{1,0:T(8,128)(2,1)} %get-tuple-element.90), channel_id=1, source_target_pairs={{0,8},{4,12},{8,0},{12,4},{16,24},{20,28},{24,16},{28,20},{1,9},{5... | collective-permute-start | bytes 1572872 | tf_op jit(solution)/shard_map/ppermute | solution.py:40
  880.0 70.4 %collective-permute-start.106 = (bf16[8,64,1024]{2,1,0:T(8,128)(2,1)}, bf16[8,64,1024]{2,1,0:T(8,128)(2,1)}, u32[]{:S(2)}, u32[]{:S(2)}) collective-permute-start(bf16[8,64,1024]{2,1,0:T(8,128)(2,1)} %broadcast_select_fusion.2.refs_3_), channel_id=1, source_target_pairs={{2,3},{1,0},{6,7},{5,4},{10,11},{9,8},{14,15},{13,12},{18,19},{17,... | collective-permute-start | bytes 3145736 | tf_op jit(solution)/shard_map/ppermute | solution.py:44
  890.6 86.4 %collective-permute-start.134 = (bf16[256,2048]{1,0:T(8,128)(2,1)}, bf16[256,2048]{1,0:T(8,128)(2,1)}, u32[]{:S(2)}, u32[]{:S(2)}) collective-permute-start(bf16[256,2048]{1,0:T(8,128)(2,1)} %broadcast_select_fusion), channel_id=1, source_target_pairs={{2,3},{1,0},{6,7},{5,4},{10,11},{9,8},{14,15},{13,12},{18,19},{17,... | collective-permute-start | bytes 3145736 | tf_op jit(solution)/shard_map/ppermute | solution.py:44
  891.9 78.3 %collective-permute-start.78 = (f32[3,2048]{1,0:T(4,128)S(1)}, f32[3,2048]{1,0:T(4,128)S(1)}, u32[]{:S(2)}, u32[]{:S(2)}) collective-permute-start(f32[3,2048]{1,0:T(4,128)S(1)} %pad_maximum_fusion.13), channel_id=1, source_target_pairs={{1,0},{2,3},{5,4},{6,7},{9,8},{10,11},{13,12},{14,15},{17,16},{18,... | collective-permute-start | bytes 73736 | tf_op jit(solution)/shard_map/ppermute | solution.py:44
  (176 other events, 3845.7 us)

commit v3 on v2

v3 whole, which is shorter than its diff:
```python
import jax
import jax.numpy as jnp
from jax import lax
from jax.experimental import pallas as pl
from jax.experimental.pallas import tpu as pltpu
from jax.sharding import PartitionSpec as P

D = 2048
FF = 8192
HEADS = 32
KV_HEADS = 8
HEAD = 64
GROUP = HEADS // KV_HEADS

EPS = 1e-05
THETA = 10000000.0
SCALE = 0.015625
RESID = 0.22
TAU = 3.0

PLANE = ("pair", "fsdp")
F32 = jnp.float32
BF16 = jnp.bfloat16
ORDER = (0, 4, 2, 6, 1, 5, 3, 7)


def dot(left, right):
    return jnp.dot(left, right, preferred_element_type=F32)


def outer(left, right):
    return lax.dot_general(left, right, (((0,), (0,)), ((), ())), preferred_element_type=F32)


def times_t(left, right):
    return lax.dot_general(left, right, (((1,), (1,)), ((), ())), preferred_element_type=F32)


def swap(x, mask, devices=8):
    return lax.ppermute(x, PLANE, [(i, i ^ mask) for i in range(devices)])


def along(x, pairs):
    return lax.ppermute(x, "rep", pairs)


def after(x, *others):
    return lax.optimization_barrier((x,) + others)[0]


def rope_tables(places):
    half = HEAD // 2
    lane = jnp.arange(2 * HEAD)
    inverse = THETA ** (-((lane % half).astype(F32) * 2.0 / HEAD))
    angle = places.astype(F32)[:, None] * inverse[None, :]
    sign = jnp.where(lane % HEAD < half, -1.0, 1.0)
    return jnp.cos(angle), jnp.sin(angle) * sign[None, :]


def whole_row(cos, sin, heads):
    turned = lax.broadcasted_iota(jnp.int32, cos.shape, 1) < HEAD
    pairs = heads // 2
    cos_row = jnp.concatenate([cos] * pairs + [jnp.where(turned, cos, 1.0)], axis=1)
    sin_row = jnp.concatenate([sin] * pairs + [jnp.where(turned, sin, 0.0)], axis=1)
    return cos_row, sin_row


def half_swap(x):
    width = x.shape[1]
    lane = lax.broadcasted_iota(jnp.int32, x.shape, 1)
    first = (lane & (HEAD - 1)) < HEAD // 2
    return jnp.where(first, pltpu.roll(x, width - HEAD // 2, 1), pltpu.roll(x, HEAD // 2, 1))


def mat_t(left, right):
    return lax.dot_general(left, right, (((1,), (1,)), ((), ())), preferred_element_type=F32)


def mat_tl(left, right):
    return lax.dot_general(left, right, (((0,), (0,)), ((), ())), preferred_element_type=F32)


def attend_kernel(
    heads,
    near,
    first_near,
    second_near,
    first_far,
    second_far,
    gain_ref,
    weight_ref,
    cos_ref,
    sin_ref,
    vis_ref,
    normed_ref,
    qkv_ref,
    att_ref,
    top_ref,
    tokens_ref,
):
    rows = first_near.shape[1]

    @pl.when(pl.program_id(0) < near)
    def _():
        tokens_ref[:rows] = first_near[0]
        tokens_ref[rows:] = second_near[0]

    @pl.when(pl.program_id(0) >= near)
    def _():
        tokens_ref[:rows] = first_far[0]
        tokens_ref[rows:] = second_far[0]

    inputs = tokens_ref[...].astype(F32)
    inv = lax.rsqrt(jnp.mean(inputs * inputs, axis=1, keepdims=True) + EPS)
    normed = (inputs * inv * gain_ref[...]).astype(BF16)
    normed_ref[...] = normed
    x = dot(normed, weight_ref[...])
    cos_row, sin_row = whole_row(cos_ref[...], sin_ref[...], heads)
    row = (x * cos_row + half_swap(x) * sin_row).astype(BF16)
    qkv_ref[...] = row
    key = row[:, heads * HEAD : (heads + 1) * HEAD]
    value = row[:, (heads + 1) * HEAD :]
    visible = vis_ref[...] > 0.0
    top_ref[...] = jnp.full(top_ref.shape, -jnp.inf, F32)
    outs = []
    for h in range(heads):
        scores = mat_t(row[:, h * HEAD : (h + 1) * HEAD], key) * SCALE
        scores = jnp.where(visible, scores, -jnp.inf)
        peak = jnp.max(scores, axis=1, keepdims=True)
        grown = jnp.exp(scores - peak)
        probs = (grown / jnp.sum(grown, axis=1, keepdims=True)).astype(BF16)
        outs.append(dot(probs, value).astype(BF16))
        top_ref[h : h + 1, :] = jnp.broadcast_to(jnp.max(peak, axis=0, keepdims=True), (1, 128))
    att_ref[...] = jnp.concatenate(outs, axis=1)


def attend(heads, parts, gain, weight, cosine, sine, visible):
    near = parts[0].shape[0]
    groups = near + parts[2].shape[0]
    length = parts[0].shape[1] + parts[1].shape[1]
    width = weight.shape[1]

    def part(x, is_near):
        block = (1,) + x.shape[1:]
        if is_near:
            return pl.BlockSpec(block, lambda g: (jnp.minimum(g, near - 1), 0, 0))
        return pl.BlockSpec(block, lambda g: (jnp.maximum(g - near, 0), 0, 0))

    def whole(x):
        return pl.BlockSpec(x.shape, lambda g: (0, 0))

    def rows(columns, each=length):
        return pl.BlockSpec((each, columns), lambda g: (g, 0))

    total = groups * length
    return pl.pallas_call(
        lambda *refs: attend_kernel(heads, near, *refs),
        grid=(groups,),
        in_specs=[part(x, i < 2) for i, x in enumerate(parts)]
        + [whole(gain), whole(weight), rows(cosine.shape[1]), rows(sine.shape[1]), rows(visible.shape[1])],
        out_specs=[rows(D), rows(width), rows(heads * HEAD), rows(128, 8)],
        out_shape=[
            jax.ShapeDtypeStruct((total, D), BF16),
            jax.ShapeDtypeStruct((total, width), BF16),
            jax.ShapeDtypeStruct((total, heads * HEAD), BF16),
            jax.ShapeDtypeStruct((8 * groups, 128), F32),
        ],
        scratch_shapes=[pltpu.VMEM((length, D), BF16)],
        name="attend",
        cost_estimate=pl.CostEstimate(
            flops=2 * total * D * width, bytes_accessed=8 * total * D, transcendentals=0
        ),
    )(*parts, gain, weight, cosine, sine, visible)


def attend_back_kernel(heads, qkv_ref, cos_ref, sin_ref, vis_ref, grad_ref, out_ref):
    row = qkv_ref[...]
    key = row[:, heads * HEAD : (heads + 1) * HEAD]
    value = row[:, (heads + 1) * HEAD :]
    visible = vis_ref[...] > 0.0
    grad_att = grad_ref[...]
    grads = []
    grad_key = jnp.zeros((row.shape[0], HEAD), F32)
    grad_value = jnp.zeros((row.shape[0], HEAD), F32)
    for h in range(heads):
        query = row[:, h * HEAD : (h + 1) * HEAD]
        grad_h = grad_att[:, h * HEAD : (h + 1) * HEAD]
        scores = jnp.where(visible, mat_t(query, key) * SCALE, -jnp.inf)
        peak = jnp.max(scores, axis=1, keepdims=True)
        grown = jnp.exp(scores - peak)
        probs = grown / jnp.sum(grown, axis=1, keepdims=True)
        grad_probs = mat_t(grad_h, value)
        delta = jnp.sum(probs * grad_probs, axis=1, keepdims=True)
        grad_scores = (probs * (grad_probs - delta) * SCALE).astype(BF16)
        grads.append(dot(grad_scores, key))
        grad_key = grad_key + mat_tl(grad_scores, query)
        grad_value = grad_value + mat_tl(probs.astype(BF16), grad_h)
    x = jnp.concatenate(grads + [grad_key, grad_value], axis=1)
    cos_row, sin_row = whole_row(cos_ref[...], sin_ref[...], heads)
    out_ref[...] = (x * cos_row - half_swap(x) * sin_row).astype(BF16)


def per_group(kernel, heads, length, ins, outs, name, flops):
    groups = ins[0].shape[0] // length

    def spec(x):
        rows = x.shape[0] // groups
        return pl.BlockSpec((rows, x.shape[1]), lambda g: (g, 0))

    return pl.pallas_call(
        lambda *refs: kernel(heads, *refs),
        grid=(groups,),
        in_specs=[spec(x) for x in ins],
        out_specs=[spec(x) for x in outs],
        out_shape=outs,
        name=name,
        cost_estimate=pl.CostEstimate(
            flops=flops, bytes_accessed=4 * sum(x.size for x in ins), transcendentals=0
        ),
    )(*ins)


def place_kernel(table, sum_ref, copy_ref, *refs):
    out_ref = refs[-1]

    @pl.when(table[0] == 1)
    def _():
        out_ref[...] = sum_ref[...].astype(F32)

    @pl.when(table[0] == 0)
    def _():
        out_ref[...] = copy_ref[...].astype(F32)


def place(table, summed, copied, into, shape, name):
    rows, width = summed.shape
    half = rows // 2
    columns = width // 2
    piece = pl.BlockSpec((half, columns), lambda i, j, t: (j, i))
    in_specs = [piece, piece]
    args = [summed, copied]
    aliases = {}
    if into is not None:
        in_specs.append(pl.BlockSpec(memory_space=pl.ANY))
        args.append(into)
        aliases = {3: 0}
    return pl.pallas_call(
        place_kernel,
        grid_spec=pltpu.PrefetchScalarGridSpec(
            num_scalar_prefetch=1,
            grid=(2, 2),
            in_specs=in_specs,
            out_specs=pl.BlockSpec((half, columns), lambda i, j, t: (j, t[1 + i])),
        ),
        out_shape=jax.ShapeDtypeStruct(shape, F32),
        input_output_aliases=aliases,
        name=name,
        cost_estimate=pl.CostEstimate(flops=0, bytes_accessed=8 * rows * width, transcendentals=0),
    )(table, *args)


class Line:
    def __init__(self, z):
        self.inner = (z == 1) | (z == 2)
        self.rounds = ([], [], [])

    def send(self, stage, x, pairs):
        sent = self.rounds[stage]
        if len(sent) >= 2:
            x = after(x, sent[-2])
        sent.append(along(x, pairs))
        return x, sent[-1]

    def sum(self, x):
        x, more = self.send(0, x, [(0, 1), (3, 2)])
        x, more = self.send(1, x + more, [(1, 2), (2, 1)])
        return self.send(2, x + more, [(1, 0), (2, 3)])

    def pick(self, summed, copied):
        return jnp.where(self.inner, summed, copied)


class Plane:
    def __init__(self):
        self.np = lax.axis_size("pair")
        self.nf = lax.axis_size("fsdp")
        self.nr = lax.axis_size("rep")
        self.n = self.np * self.nf
        self.p = lax.axis_index("pair")
        self.f = lax.axis_index("fsdp")
        self.z = lax.axis_index("rep")
        self.place = self.p * self.nf + self.f
        self.unit = self.np * self.f + self.p
        self.cube = self.np == 2 and self.nf == 4
        self.line = self.nr == 4

    def gather(self, x, axis=0):
        if not self.cube:
            full = lax.all_gather(x, PLANE, axis=axis, tiled=True)
            return self.to_groups(full, axis)
        near = [x] + [swap(x, m) for m in ORDER[1:4]]
        far = [swap(piece, 1) for piece in near]
        return jnp.concatenate(near + far, axis=axis)

    def gather_parts(self, x, swapped, hold=()):
        two = jnp.stack([x, swapped])
        other = swap(after(two, *hold), 4)
        return two, other, swap(two, 1), swap(other, 1)

    def gather_small(self, x):
        pair = jnp.concatenate([x, swap(x, 4)], axis=1)
        quad = jnp.concatenate([pair, swap(pair, 2)], axis=1)
        return jnp.concatenate([quad, swap(quad, 1)], axis=1)

    def gather_gains(self, x):
        for k in (1, 2):
            other = swap(x, k)
            odd = (self.f & k) > 0
            x = jnp.concatenate([jnp.where(odd, other, x), jnp.where(odd, x, other)], axis=1)
        return x

    def to_groups(self, x, axis=0):
        shape = x.shape
        y = x.reshape(shape[:axis] + (self.np, self.nf, -1) + shape[axis + 1 :])
        return jnp.swapaxes(y, axis, axis + 1).reshape(shape)

    def from_groups(self, x):
        y = x.reshape((self.nf, self.np, -1) + x.shape[1:])
        return jnp.swapaxes(y, 0, 1).reshape(x.shape)

    def scatter(self, left, right, product):
        rows = left.shape[0]
        if not self.cube:
            whole = self.from_groups(product(left, right).astype(BF16))
            total = lax.psum_scatter(whole, PLANE, scatter_dimension=0, tiled=True).astype(F32)
            return total, whole
        half = rows // 2
        far = swap(product(left[half:], right).astype(BF16), 1)
        near = product(left[:half], right) + far.astype(F32)
        size = half // 4
        total = near[:size]
        pieces = [near[i * size : (i + 1) * size].astype(BF16) for i in (1, 2, 3)]
        for i, piece in enumerate(pieces):
            total = total + swap(piece, ORDER[i + 1]).astype(F32)
        return total, pieces[0]

    def reshard(self, columns):
        if not self.cube:
            parts = jnp.stack([columns(self.np * i + self.p) for i in range(self.nf)])
            got = lax.all_to_all(parts, "fsdp", 0, 0, tiled=True)
            return got.reshape((-1,) + got.shape[2:]), ()
        own = columns(self.unit)
        rows = own.shape[0]
        got = [swap(columns(self.np * (self.f ^ k) + self.p), k) for k in (1, 2, 3)]
        out = jnp.zeros((self.nf * rows,) + own.shape[1:], own.dtype)
        out = lax.dynamic_update_slice(out, own, (self.f * rows, 0))
        for k, piece in zip((1, 2, 3), got):
            out = lax.dynamic_update_slice(out, piece, ((self.f ^ k) * rows, 0))
        return out, tuple(got[1:])

    def reshard_shared(self, columns, first):
        own = columns(self.unit, 0, 1)
        rows, width = own.shape
        half = rows // 2
        part = self.z & 1
        near = swap(columns(self.np * (self.f ^ 1) + self.p, 0, 1), 1)
        got = []
        for k in (2, 3):
            piece = columns(self.np * (self.f ^ k) + self.p, part, 2)
            got.append(swap(after(piece, *first, *got), k))

        def finish(hold):
            out = jnp.zeros((self.nf * rows, width), own.dtype)
            out = lax.dynamic_update_slice(out, own, (self.f * rows, 0))
            out = lax.dynamic_update_slice(out, near, ((self.f ^ 1) * rows, 0))
            for k, piece in zip((2, 3), got):
                start = (self.f ^ k) * rows
                other = along(after(piece, hold), [(0, 1), (1, 0), (2, 3), (3, 2)])
                out = lax.dynamic_update_slice(out, piece, (start + part * half, 0))
                out = lax.dynamic_update_slice(out, other, (start + (1 - part) * half, 0))
            return out

        return finish

    def unit_of(self, place):
        return self.np * (place % self.nf) + place // self.nf

    def to_owner(self, x):
        pairs = []
        for p in range(self.np):
            for f in range(self.nf):
                pairs.append((p * self.nf + f, self.np * f + p))
        return lax.ppermute(x, PLANE, pairs)

    def sum_rows(self, term):
        rows, width = term.shape
        each = rows // (self.n * self.nr)
        split = term.astype(BF16).reshape(self.n, self.nr, each, width)
        mine = lax.psum_scatter(jnp.swapaxes(split, 0, 1), "rep", scatter_dimension=0)
        moved = lax.all_to_all(mine, PLANE, 0, 0, tiled=True)
        full = jnp.swapaxes(lax.all_gather(moved, "rep", axis=0), 0, 1)
        return full.reshape(self.n, -1, width), self.unit_of(jnp.arange(self.n))

    def in_order(self, full, units):
        inverse = jnp.zeros((self.n,), jnp.int32).at[units].set(jnp.arange(self.n, dtype=jnp.int32))
        return jnp.swapaxes(jnp.take(full, inverse, axis=0), 0, 1)

    def sum_units(self, term):
        mine = lax.psum_scatter(term.astype(BF16), "rep", scatter_dimension=0, tiled=True)
        return lax.all_gather(self.to_owner(mine), "rep", axis=0, tiled=True)

    def block_for(self, split, m):
        return lax.dynamic_index_in_dim(split, self.place ^ m, 0, keepdims=False)

    def exchange(self, split):
        order = jnp.take(split, self.place ^ jnp.arange(8), axis=0)
        near = order[0::2]
        far = swap(order[1::2], 1)
        both = [jnp.stack([near[j], far[j]]) for j in range(4)]
        return jnp.concatenate([both[0]] + [swap(both[j], 2 * j) for j in (1, 2, 3)], axis=0)

    def total(self, sums, top):
        if not (self.cube and self.line):
            everyone = ("pair", "fsdp", "rep")
            return lax.psum(sums, everyone), lax.pmax(top, everyone)
        count = sums.shape[0]
        both = jnp.concatenate([sums, top], axis=0)

        def join(a, b):
            return jnp.concatenate(
                [a[:count] + b[:count], jnp.maximum(a[count:], b[count:])], axis=0
            )

        for m in (1, 2, 4):
            both = join(both, swap(both, m))
        ends = [(0, 1), (3, 2)]
        inner = (self.z == 1) | (self.z == 2)
        both = jnp.where(inner, join(both, along(both, ends)), both)
        both = join(both, along(both, [(1, 2), (2, 1)]))
        both = jnp.where(inner, both, along(both, [(1, 0), (2, 3)]))
        return both[:count], both[count:]


def norm_back(grad_normed, unit, inv_scale, gain):
    scaled = grad_normed * gain
    grad_in = inv_scale * (scaled - unit * jnp.mean(scaled * unit, axis=-1, keepdims=True))
    return (grad_in, jnp.sum(grad_normed * unit, axis=0))


def on_device(
    tokens,
    cotangent,
    segment_ids,
    positions,
    q_weight,
    k_weight,
    v_weight,
    o_weight,
    attn_gain,
    gate_up_weight,
    down_weight,
    mlp_gain,
):
    plane = Plane()
    fast = plane.cube and plane.line
    unit, n = plane.unit, plane.n
    heads = HEADS // n
    share = max(1, n // KV_HEADS)
    q_cols = heads * HEAD
    ff = FF // n
    length = plane.np * tokens.shape[0]

    def qkv_columns(u):
        rows = q_weight.shape[0]
        return jnp.concatenate(
            [
                lax.dynamic_slice(q_weight, (0, u * q_cols), (rows, q_cols)),
                lax.dynamic_slice(k_weight, (0, (u // share) * HEAD), (rows, HEAD)),
                lax.dynamic_slice(v_weight, (0, (u // share) * HEAD), (rows, HEAD)),
            ],
            axis=1,
        )

    def mlp_columns(u, part=0, parts=1):
        rows = gate_up_weight.shape[0] // parts
        return jnp.concatenate(
            [
                lax.dynamic_slice(gate_up_weight, (part * rows, u * ff), (rows, ff)),
                lax.dynamic_slice(gate_up_weight, (part * rows, FF + u * ff), (rows, ff)),
            ],
            axis=1,
        )

    grad_out = cotangent.astype(F32)
    low_out = (RESID * grad_out).astype(BF16)
    gains = jnp.stack([attn_gain, mlp_gain])
    where = jnp.stack([segment_ids, positions])
    w_out = lax.dynamic_slice(o_weight, (plane.p * q_cols, 0), (q_cols, D))
    w_down = lax.dynamic_slice(down_weight, (plane.p * ff, 0), (ff, D))
    if fast:
        crossed = swap(tokens, 2)
        parts = plane.gather_parts(tokens, crossed)
        where = plane.gather_small(where)
        gains = plane.gather_gains(gains)
        w_qkv, arrived = plane.reshard(qkv_columns)
        finish_gate_up = plane.reshard_shared(mlp_columns, (crossed,) + arrived)
        low_crossed = swap(after(low_out, crossed), 2)
        low_parts = plane.gather_parts(low_out, low_crossed, (parts[1],))
        grad_branch = jnp.concatenate(
            [low_parts[i][j] for i, j in ((0, 0), (1, 0), (0, 1), (1, 1), (2, 0), (3, 0), (2, 1), (3, 1))], axis=0
        )
    else:
        by_group = plane.gather(tokens).reshape(-1, 2, length // 2, D)
        near = by_group.shape[0] // 2
        parts = [by_group[:near, 0], by_group[:near, 1], by_group[near:, 0], by_group[near:, 1]]
        where = plane.gather(where, axis=1)
        gains = lax.all_gather(gains, "fsdp", axis=1, tiled=True)
        w_qkv, _ = plane.reshard(qkv_columns)
        w_gate_up, _ = plane.reshard(mlp_columns)
        grad_branch = plane.gather(low_out)
    gain_one = gains[0].astype(F32)
    gain_two = gains[1].astype(F32)
    segments = where[0].reshape(-1, length)
    places = where[1].reshape(-1, length)
    visible = (
        (segments[:, None, :] == 0) | (segments[:, None, :] == segments[:, :, None])
    ) & (places[:, None, :] <= places[:, :, None])
    visible = visible.astype(F32).reshape(-1, length)
    cosine, sine = rope_tables(places.reshape(-1))

    normed, qkv, attended, tops = attend(
        heads, parts, gain_one[None], w_qkv, cosine, sine, visible
    )
    count = qkv.shape[0]
    flops = 4 * count * length * HEAD * heads

    inputs = tokens.astype(F32)
    branch, sent = plane.scatter(attended, w_out, dot)
    if fast:
        w_gate_up = finish_gate_up(sent)
    middle = inputs + RESID * branch
    inv_two = lax.rsqrt(jnp.mean(middle * middle, axis=-1, keepdims=True) + EPS)
    unit_two = middle * inv_two
    low_two = (unit_two * gain_two).astype(BF16)
    normed_mlp = plane.gather(low_two)
    grad_hidden = lax.optimization_barrier(times_t(grad_branch, w_down))

    gate = lax.optimization_barrier(dot(normed_mlp, w_gate_up[:, :ff]))
    up_part = dot(normed_mlp, w_gate_up[:, ff:])
    sigma = jax.nn.sigmoid(gate)
    silu_gate = gate * sigma
    hidden = (silu_gate * up_part).astype(BF16)
    grad_gate = (grad_hidden * up_part * sigma * (1.0 + gate * (1.0 - sigma))).astype(BF16)
    grad_up = (grad_hidden * silu_gate).astype(BF16)
    grad_gate_up = jnp.concatenate([grad_gate, grad_up], axis=1)

    def back(grad_normed_mlp):
        grad_mid_norm, gain_two_grad = norm_back(grad_normed_mlp, unit_two, inv_two, gain_two)
        grad_middle = grad_out + grad_mid_norm
        grad_attn_branch = plane.gather((RESID * grad_middle).astype(BF16))
        grad_attended = times_t(grad_attn_branch, w_out).astype(BF16)
        (grad_lin,) = per_group(
            attend_back_kernel,
            heads,
            length,
            [qkv, cosine, sine, visible, grad_attended],
            [jax.ShapeDtypeStruct(qkv.shape, BF16)],
            "attend_back",
            3 * flops,
        )
        return grad_middle, grad_attn_branch, grad_lin, gain_two_grad

    rows = D // n
    shape = (rows, 2 * FF)
    if fast:
        line = Line(plane.z)
        each = ff // 4
        downs = [
            outer(hidden[:, i * each : (i + 1) * each], grad_branch).astype(BF16) for i in range(4)
        ]
        grad_gate_up = after(grad_gate_up, *downs)
        downs = [line.sum(x) for x in downs]
        grad_normed_mlp, sent = plane.scatter(grad_gate_up, w_gate_up, times_t)
        term = outer(after(normed_mlp, sent), grad_gate_up).astype(BF16).reshape(n, rows, 2 * ff)
        blocks = {0: plane.block_for(term, 0), 1: swap(plane.block_for(term, 1), 1)}
        hold = (grad_normed_mlp,)
        for pair in ((2, 4), (3, 5), (6,), (7,)):
            for m in pair:
                blocks[m] = swap(after(plane.block_for(term, m), *hold), m)
            hold = tuple(blocks[m] for m in pair)
        grad_middle, grad_attn_branch, grad_lin, gain_two_grad = back(grad_normed_mlp)
        o_term = outer(attended, grad_attn_branch).astype(BF16)
        branch, _ = plane.scatter(after(hidden, grad_attn_branch), w_down, dot)
        grad_normed, _ = plane.scatter(grad_lin, w_qkv, times_t)
        lin_term = plane.exchange(outer(normed, grad_lin).astype(BF16).reshape(n, rows, -1))
        gate_up_grad = None

        def put(m, into):
            u = plane.unit_of(plane.place ^ m)
            table = jnp.stack([line.inner.astype(jnp.int32), u, n + u])
            return place(table, *line.sum(blocks[m]), into, shape, "place_gate_up")

        for m in (0, 1, 2, 4, 3, 5, 6):
            gate_up_grad = put(m, gate_up_grad)
        o_grad = plane.to_owner(line.pick(*line.sum(o_term))).astype(F32)
        lin_rows = line.pick(*line.sum(lin_term))
        lin_units = plane.unit_of(plane.place ^ jnp.arange(8))
        gate_up_grad = put(7, gate_up_grad)
        down_grad = jnp.concatenate(
            [plane.to_owner(line.pick(*x)).astype(F32) for x in downs], axis=0
        )
    else:
        down_grad = plane.sum_units(outer(hidden, grad_branch)).astype(F32)
        full, units = plane.sum_rows(outer(normed_mlp, grad_gate_up))
        full = plane.in_order(full, units).reshape(rows, n, 2, ff)
        gate_up_grad = jnp.swapaxes(full, 1, 2).reshape(shape).astype(F32)
        grad_normed_mlp, _ = plane.scatter(grad_gate_up, w_gate_up, times_t)
        grad_middle, grad_attn_branch, grad_lin, gain_two_grad = back(grad_normed_mlp)
        branch, _ = plane.scatter(hidden, w_down, dot)
        grad_normed, _ = plane.scatter(grad_lin, w_qkv, times_t)
        o_grad = plane.sum_units(outer(attended, grad_attn_branch)).astype(F32)
        lin_rows, lin_units = plane.sum_rows(outer(normed, grad_lin))

    result = (middle + RESID * branch).astype(BF16)
    inv_one = lax.rsqrt(jnp.mean(inputs * inputs, axis=-1, keepdims=True) + EPS)
    grad_in_norm, gain_one_grad = norm_back(grad_normed, inputs * inv_one, inv_one, gain_one)
    input_grad = (grad_middle + grad_in_norm).astype(BF16)

    top_local = jnp.max(tops.reshape(-1, 8, 128), axis=(0, 2))[:heads]
    top_row = jnp.full((1, D), -jnp.inf, F32)
    top_row = lax.dynamic_update_slice(top_row, top_local[None], (0, unit * heads))
    gain_grads, top_row = plane.total(jnp.stack([gain_one_grad, gain_two_grad]), top_row)
    factor = TAU / jnp.maximum(top_row[0, :HEADS], TAU)
    k_factor = jnp.repeat(jnp.min(factor.reshape(KV_HEADS, GROUP), axis=1), HEAD)
    lin_rows = plane.in_order(lin_rows, lin_units).astype(F32)
    q_update = lin_rows[..., :q_cols].reshape(rows, D) * jnp.repeat(factor, HEAD)[None, :]
    kv = lin_rows[..., q_cols:].reshape(rows, n // share, share, 2 * HEAD).sum(axis=2)
    k_update = kv[..., :HEAD].reshape(rows, -1) * k_factor[None, :]
    v_grad = kv[..., HEAD:].reshape(rows, -1)
    gain_grads = lax.dynamic_slice(gain_grads, (0, plane.place * rows), (2, rows))
    return (
        result,
        input_grad,
        q_update,
        k_update,
        v_grad,
        o_grad,
        gain_grads[0],
        gate_up_grad,
        down_grad,
        gain_grads[1],
    )


def solution(mesh):
    tokens = P(("pair", "fsdp", "rep"))
    shard = P("fsdp")
    owned = P(("pair", "fsdp"))
    return jax.shard_map(
        on_device,
        mesh=mesh,
        in_specs=(tokens,) * 4 + (shard,) * 8,
        out_specs=(tokens, tokens) + (owned,) * 8,
        check_vma=False,
    )
```

time: 993 us -> 918 us (0.924)
  waiting for transfers between devices: 404 us -> 317 us
  other arithmetic: 65.4 us -> 110 us
  starting transfers between devices: 221 us -> 255 us
  local copies, waits for them, and re-layouts: 105 us -> 71.3 us
  matrix products: 107 us -> 91.9 us
  Pallas kernels: 70.3 us -> 59.5 us
    ppermute x58 -> x47, waiting for transfers between devices: 311 us -> 199 us  [along(): return lax.ppermute(x, 'rep', pairs)]
    add x1 -> x28, other arithmetic: 0.01 us -> 40.7 us  [the longest x14 21.2 us: sum(): x, more = self.send(1, x + more, [(1, 2), (2, 1)])]
    ppermute x58 -> x47, starting transfers between devices: 135 us -> 160 us  [along(): return lax.ppermute(x, 'rep', pairs)]
    ppermute x75 -> x63, waiting for transfers between devices: 93 us -> 118 us  [swap(): return lax.ppermute(x, PLANE, [(i, i ^ mask) for i in range(devices)])]
    unnamed x185 -> x181, local copies, waits for them, and re-layouts: 29 us -> 17.1 us
    convert_element_type x17 -> x3, other arithmetic: 18.8 us -> 7.29 us  [the longest x1 2.82 us: on_device(): (grad_hidden * up_part * sigma * (1.0 + gate * (1.0 - sigma))).astype(BF16)]
    ppermute x2 -> x5, starting transfers between devices: 10.1 us -> 21.4 us  [to_owner(): return lax.ppermute(x, PLANE, pairs)]
    pallas_call x6 -> x10, Pallas kernels: 70.3 us -> 59.5 us  [the longest x8 35.6 us: place(): pl.pallas_call(place_kernel, grid_spec=pltpu.PrefetchScalarGridSpec(num_s...]
  transfers between devices with their start and end apart: 135 -> 115, of which waited for: 52 -> 34; matrix products, arithmetic and copies ran while one was open for 22% -> 23% of each run, Pallas kernels for 6% -> 7%
where the time goes in v3:
time: 918 us; the launch traced here: 907 us
  waiting for transfers between devices  317 us (35%)
  starting transfers between devices  255 us (28%)
  other arithmetic  110 us (12%)
  matrix products  91.9 us (10%)
  local copies, waits for them, and re-layouts  71.3 us (8%)
  Pallas kernels  59.5 us (6%)
    ppermute x47, waiting for transfers between devices, along(): return lax.ppermute(x, 'rep', pairs)  199 us
    ppermute x47, starting transfers between devices, along(): return lax.ppermute(x, 'rep', pairs)  160 us
    ppermute x63, waiting for transfers between devices, swap(): return lax.ppermute(x, PLANE, [(i, i ^ mask) for i in range(devices)])  118 us
    ppermute x63, starting transfers between devices, swap(): return lax.ppermute(x, PLANE, [(i, i ^ mask) for i in range(devices)])  72.8 us
    pallas_call x8, Pallas kernels, place(): pl.pallas_call(place_kernel, grid_spec=pltpu.PrefetchScalarGridSpec(num_s...  35.6 us
    dot_general x6, matrix products, times_t(): lax.dot_general(left, right, (((1,), (1,)), ((), ())), preferred_element_...  34.7 us
    dot_general x6, matrix products, dot(): return jnp.dot(left, right, preferred_element_type=F32)  29.9 us
    dot_general x7, matrix products, outer(): lax.dot_general(left, right, (((0,), (0,)), ((), ())), preferred_element_...  27.3 us
  transfers between devices with their start and end apart: 115, of which 34 were waited for; matrix products, arithmetic and copies ran while one was open for 23% of the time, Pallas kernels for 7%

profile of v3, /device:TPU:0, one launch (start us, length us, event | category | flops | bytes accessed | tf_op | source)
XLA Modules:
  0.0 907.4 jit_solution(3896812520094764541)
XLA Ops:
  59.4 12.8 %collective-permute-done.1.refs_1_ = bf16[2,128,2048]{2,1,0:T(8,128)(2,1)} collective-permute-done((bf16[2,128,2048]{2,1,0:T(8,128)(2,1)}, bf16[2,128,2048]{2,1,0:T(8,128)(2,1)}, u32[]{:S(2)}, u32[]{:S(2)}) %collective-permute-start.1) | collective-permute-done | bytes 1048608 | tf_op jit(solution)/shard_map/ppermute | solution.py:40
  93.5 11.8 %attend.1 = (bf16[1024,2048]{1,0:T(8,128)(2,1)}, bf16[1024,384]{1,0:T(8,128)(2,1)}, bf16[1024,256]{1,0:T(8,128)(2,1)}, f32[32,128]{1,0:T(8,128)}) custom-call(bf16[2,128,2048]{2,1,0:T(8,128)(2,1)} %pad_maximum_fusion.2.refs_0_, bf16[2,128,2048]{2,1,0:T(8,128)(2,1)} %collective-permute-done.1.refs_1_, bf16[2,128,2048]{2,1,0:T(8,128)(2,1)} %collective-permute-done.2.refs_2_, ...), custom_call_target="tpu_custom_call" | custom-call | flops 1610612736 | bytes 16777216 | tf_op jit(solution)/shard_map/attend/pallas_call | solution.py:156
  129.8 10.5 %collective-permute-done.14 = bf16[128,2048]{1,0:T(8,128)(2,1)S(1)} collective-permute-done((bf16[128,2048]{1,0:T(8,128)(2,1)S(1)}, bf16[128,2048]{1,0:T(8,128)(2,1)S(1)}, u32[]{:S(2)}, u32[]{:S(2)}) %collective-permute-start.14) | collective-permute-done | bytes 524320 | tf_op jit(solution)/shard_map/ppermute | solution.py:40
  201.3 10.6 %convolution_convert_fusion.3 = bf16[512,2048]{1,0:T(8,128)(2,1)} fusion(bf16[2048,2048]{1,0:T(8,128)(2,1)} %constant_dynamic-update-slice_fusion.21, bf16[1024,2048]{1,0:T(8,128)(2,1)S(1)} %pad_maximum_fusion), kind=kOutput, calls=%fused_computation.29 | convolution fusion | flops 4296015872 | bytes 12582912 | tf_op jit(solution)/shard_map/dot_general | solution.py:36
  225.3 17.8 %collective-permute-done.60 = bf16[256,2048]{1,0:T(8,128)(2,1)} collective-permute-done((bf16[256,2048]{1,0:T(8,128)(2,1)}, bf16[256,2048]{1,0:T(8,128)(2,1)}, u32[]{:S(2)}, u32[]{:S(2)}) %collective-permute-start.60) | collective-permute-done | bytes 1048608 | tf_op jit(solution)/shard_map/ppermute | solution.py:44
  250.3 15.2 %collective-permute-done.88 = bf16[256,2048]{1,0:T(8,128)(2,1)} collective-permute-done((bf16[256,2048]{1,0:T(8,128)(2,1)}, bf16[256,2048]{1,0:T(8,128)(2,1)}, u32[]{:S(2)}, u32[]{:S(2)}) %collective-permute-start.88) | collective-permute-done | bytes 1048608 | tf_op jit(solution)/shard_map/ppermute | solution.py:44
  289.7 20.3 %collective-permute-done.89 = bf16[256,2048]{1,0:T(8,128)(2,1)S(1)} collective-permute-done((bf16[256,2048]{1,0:T(8,128)(2,1)}, bf16[256,2048]{1,0:T(8,128)(2,1)S(1)}, u32[]{:S(2)}, u32[]{:S(2)}) %collective-permute-start.89) | collective-permute-done | bytes 1048608 | tf_op jit(solution)/shard_map/ppermute | solution.py:44
  311.7 11.1 %convolution_convert_fusion = bf16[2048,2048]{1,0:T(8,128)(2,1)S(1)} fusion(bf16[1024,2048]{1,0:T(8,128)(2,1)} %copy-done.68, bf16[1024,2048]{1,0:T(8,128)(2,1)S(1)} %copy-done.25), kind=kOutput, calls=%fused_computation.3 | convolution fusion | flops 8594128896 | bytes 16777216 | tf_op jit(solution)/shard_map/dot_general | solution.py:32
  347.8 11.9 %collective-permute-done.100 = bf16[256,2048]{1,0:T(8,128)(2,1)S(1)} collective-permute-done((bf16[256,2048]{1,0:T(8,128)(2,1)S(1)}, bf16[256,2048]{1,0:T(8,128)(2,1)S(1)}, u32[]{:S(2)}, u32[]{:S(2)}) %collective-permute-start.100) | collective-permute-done | bytes 1048608 | tf_op jit(solution)/shard_map/ppermute | solution.py:44
  376.6 17.2 %collective-permute-done.55 = bf16[256,2048]{1,0:T(8,128)(2,1)S(1)} collective-permute-done((bf16[256,2048]{1,0:T(8,128)(2,1)S(1)}, bf16[256,2048]{1,0:T(8,128)(2,1)S(1)}, u32[]{:S(2)}, u32[]{:S(2)}) %collective-permute-start.55) | collective-permute-done | bytes 1048608 | tf_op jit(solution)/shard_map/ppermute | solution.py:40
  404.6 20.1 %collective-permute-start.90 = (bf16[256,2048]{1,0:T(8,128)(2,1)}, bf16[256,2048]{1,0:T(8,128)(2,1)}, u32[]{:S(2)}, u32[]{:S(2)}) collective-permute-start(bf16[256,2048]{1,0:T(8,128)(2,1)} %collective-permute-done.87), channel_id=1, source_target_pairs={{0,1},{3,2},{4,5},{7,6},{8,9},{11,10},{12,13},{15,14},{16,17},{19,... | collective-permute-start | bytes 3145736 | tf_op jit(solution)/shard_map/ppermute | solution.py:44
  428.9 12.1 %attend_back.1 = bf16[1024,384]{1,0:T(8,128)(2,1)} custom-call(bf16[1024,384]{1,0:T(8,128)(2,1)} %get-tuple-element.75.refs_0_, f32[1024,128]{1,0:T(8,128)} %get-tuple-element.236.refs_6_.refs_1_, f32[1024,128]{1,0:T(8,128)} %get-tuple-element.235.refs_7_.refs_2_, f32[1024,256]{1,0:T(8,128)} %fusion.45.refs_8_.refs_3_, ...), custom_call_target="tpu_custom_call" | custom-call | flops 805306368 | bytes 4718592 | tf_op jit(solution)/shard_map/attend_back/pallas_call | solution.py:210
  478.3 13.1 %collective-permute-done.101 = bf16[256,2048]{1,0:T(8,128)(2,1)S(1)} collective-permute-done((bf16[256,2048]{1,0:T(8,128)(2,1)S(1)}, bf16[256,2048]{1,0:T(8,128)(2,1)S(1)}, u32[]{:S(2)}, u32[]{:S(2)}) %collective-permute-start.101) | collective-permute-done | bytes 1048608 | tf_op jit(solution)/shard_map/ppermute | solution.py:44
  517.6 23.0 %collective-permute-start.50 = (bf16[128,2048]{1,0:T(8,128)(2,1)S(1)}, bf16[128,2048]{1,0:T(8,128)(2,1)S(1)}, u32[]{:S(2)}, u32[]{:S(2)}) collective-permute-start(bf16[128,2048]{1,0:T(8,128)(2,1)S(1)} %get-tuple-element.189), channel_id=1, source_target_pairs={{0,24},{4,28},{8,16},{12,20},{16,8},{20,12},{24,0},{28,4},{1,25},{... | collective-permute-start | bytes 1572872 | tf_op jit(solution)/shard_map/ppermute | solution.py:40
  540.6 12.8 %collective-permute-done.48 = bf16[128,2048]{1,0:T(8,128)(2,1)S(1)} collective-permute-done((bf16[128,2048]{1,0:T(8,128)(2,1)S(1)}, bf16[128,2048]{1,0:T(8,128)(2,1)S(1)}, u32[]{:S(2)}, u32[]{:S(2)}) %collective-permute-start.48) | collective-permute-done | bytes 524320 | tf_op jit(solution)/shard_map/ppermute | solution.py:40
  584.7 11.4 %collective-permute-done.76.copy_ref = bf16[256,2048]{1,0:T(8,128)(2,1)S(1)} collective-permute-done((bf16[256,2048]{1,0:T(8,128)(2,1)S(1)}, bf16[256,2048]{1,0:T(8,128)(2,1)S(1)}, u32[]{:S(2)}, u32[]{:S(2)}) %collective-permute-start.76) | collective-permute-done | bytes 1048608 | tf_op jit(solution)/shard_map/ppermute | solution.py:44
  597.8 10.8 %collective-permute-start.92 = (bf16[256,2048]{1,0:T(8,128)(2,1)}, bf16[256,2048]{1,0:T(8,128)(2,1)}, u32[]{:S(2)}, u32[]{:S(2)}) collective-permute-start(bf16[256,2048]{1,0:T(8,128)(2,1)} %collective-permute-done.58), channel_id=1, source_target_pairs={{0,1},{3,2},{4,5},{7,6},{8,9},{11,10},{12,13},{15,14},{16,17},{19,... | collective-permute-start | bytes 3145736 | tf_op jit(solution)/shard_map/ppermute | solution.py:44
  657.5 19.0 %collective-permute-start.93 = (bf16[256,2048]{1,0:T(8,128)(2,1)}, bf16[256,2048]{1,0:T(8,128)(2,1)}, u32[]{:S(2)}, u32[]{:S(2)}) collective-permute-start(bf16[256,2048]{1,0:T(8,128)(2,1)} %convolution_convert_fusion.5), channel_id=1, source_target_pairs={{0,1},{3,2},{4,5},{7,6},{8,9},{11,10},{12,13},{15,14},{16,17},{19,... | collective-permute-start | bytes 3145736 | tf_op jit(solution)/shard_map/ppermute | solution.py:44
  682.0 14.6 %collective-permute-start.84 = (f32[3,2048]{1,0:T(4,128)S(1)}, f32[3,2048]{1,0:T(4,128)S(1)}, u32[]{:S(2)}, u32[]{:S(2)}) collective-permute-start(f32[3,2048]{1,0:T(4,128)S(1)} %pad_maximum_fusion.15), channel_id=1, source_target_pairs={{0,1},{3,2},{4,5},{7,6},{8,9},{11,10},{12,13},{15,14},{16,17},{19,... | collective-permute-start | bytes 73736 | tf_op jit(solution)/shard_map/ppermute | solution.py:44
  711.7 18.4 %collective-permute-done.84 = f32[3,2048]{1,0:T(4,128)S(1)} collective-permute-done((f32[3,2048]{1,0:T(4,128)S(1)}, f32[3,2048]{1,0:T(4,128)S(1)}, u32[]{:S(2)}, u32[]{:S(2)}) %collective-permute-start.84) | collective-permute-done | bytes 24608 | tf_op jit(solution)/shard_map/ppermute | solution.py:44
  744.9 11.2 %collective-permute-done.104.copy_ref = bf16[256,2048]{1,0:T(8,128)(2,1)S(1)} collective-permute-done((bf16[256,2048]{1,0:T(8,128)(2,1)S(1)}, bf16[256,2048]{1,0:T(8,128)(2,1)S(1)}, u32[]{:S(2)}, u32[]{:S(2)}) %collective-permute-start.104) | collective-permute-done | bytes 1048608 | tf_op jit(solution)/shard_map/ppermute | solution.py:44
  764.6 16.4 %collective-permute-done.79.copy_ref = bf16[256,2048]{1,0:T(8,128)(2,1)S(1)} collective-permute-done((bf16[256,2048]{1,0:T(8,128)(2,1)S(1)}, bf16[256,2048]{1,0:T(8,128)(2,1)S(1)}, u32[]{:S(2)}, u32[]{:S(2)}) %collective-permute-start.79) | collective-permute-done | bytes 1048608 | tf_op jit(solution)/shard_map/ppermute | solution.py:44
  784.1 28.5 %collective-permute-done.105 = bf16[256,2048]{1,0:T(8,128)(2,1)S(1)} collective-permute-done((bf16[256,2048]{1,0:T(8,128)(2,1)S(1)}, bf16[256,2048]{1,0:T(8,128)(2,1)S(1)}, u32[]{:S(2)}, u32[]{:S(2)}) %collective-permute-start.105) | collective-permute-done | bytes 1048608 | tf_op jit(solution)/shard_map/ppermute | solution.py:44
  832.0 20.6 %collective-permute-done.86 = f32[3,2048]{1,0:T(4,128)S(1)} collective-permute-done((f32[3,2048]{1,0:T(4,128)S(1)}, f32[3,2048]{1,0:T(4,128)S(1)}, u32[]{:S(2)}, u32[]{:S(2)}) %collective-permute-start.86) | collective-permute-done | bytes 24608 | tf_op jit(solution)/shard_map/ppermute | solution.py:44
  (586 shorter events, 533.0 us)
Async XLA Ops:
  86.7 62.5 %collective-permute-start.26 = (bf16[256,2048]{1,0:T(8,128)(2,1)}, bf16[256,2048]{1,0:T(8,128)(2,1)}, u32[]{:S(2)}, u32[]{:S(2)}) collective-permute-start(bf16[256,2048]{1,0:T(8,128)(2,1)} %pad_maximum_fusion.4), channel_id=1, source_target_pairs={{0,12},{4,8},{8,4},{12,0},{16,28},{20,24},{24,20},{28,16},{1,13},{... | collective-permute-start | bytes 3145736 | tf_op jit(solution)/shard_map/ppermute | solution.py:40
  118.7 49.2 %collective-permute-start.25 = (bf16[256,2048]{1,0:T(8,128)(2,1)}, bf16[256,2048]{1,0:T(8,128)(2,1)S(1)}, u32[]{:S(2)}, u32[]{:S(2)}) collective-permute-start(bf16[256,2048]{1,0:T(8,128)(2,1)} %collective-permute-done.24), channel_id=1, source_target_pairs={{0,1},{1,0},{2,3},{3,2},{4,5},{5,4},{6,7},{7,6},{8,9},{9,8},{10,11... | collective-permute-start | bytes 3145736 | tf_op jit(solution)/shard_map/ppermute | solution.py:44
  211.9 60.7 %collective-permute-start.32 = (bf16[512,2048]{1,0:T(8,128)(2,1)}, bf16[512,2048]{1,0:T(8,128)(2,1)}, u32[]{:S(2)}, u32[]{:S(2)}) collective-permute-start(bf16[512,2048]{1,0:T(8,128)(2,1)} %convolution_convert_fusion.3), channel_id=1, source_target_pairs={{0,4},{4,0},{8,12},{12,8},{16,20},{20,16},{24,28},{28,24},{1,5},{5... | collective-permute-start | bytes 6291464 | tf_op jit(solution)/shard_map/ppermute | solution.py:40
  271.9 51.8 %collective-permute-start.94 = (bf16[256,2048]{1,0:T(8,128)(2,1)S(1)}, bf16[256,2048]{1,0:T(8,128)(2,1)S(1)}, u32[]{:S(2)}, u32[]{:S(2)}) collective-permute-start(bf16[256,2048]{1,0:T(8,128)(2,1)S(1)} %add.600), channel_id=1, source_target_pairs={{1,2},{2,1},{5,6},{6,5},{9,10},{10,9},{13,14},{14,13},{17,18},{18,... | collective-permute-start | bytes 3145736 | tf_op jit(solution)/shard_map/ppermute | solution.py:44
  285.5 56.4 %collective-permute-start.74 = (bf16[256,2048]{1,0:T(8,128)(2,1)S(1)}, bf16[256,2048]{1,0:T(8,128)(2,1)}, u32[]{:S(2)}, u32[]{:S(2)}) collective-permute-start(bf16[256,2048]{1,0:T(8,128)(2,1)S(1)} %add.584), channel_id=1, source_target_pairs={{1,0},{2,3},{5,4},{6,7},{9,8},{10,11},{13,12},{14,15},{17,16},{18,... | collective-permute-start | bytes 3145736 | tf_op jit(solution)/shard_map/ppermute | solution.py:44
  375.2 49.5 %collective-permute-start.41 = (bf16[128,2048]{1,0:T(8,128)(2,1)S(1)}, bf16[128,2048]{1,0:T(8,128)(2,1)S(1)}, u32[]{:S(2)}, u32[]{:S(2)}) collective-permute-start(bf16[128,2048]{1,0:T(8,128)(2,1)S(1)} %collective-permute-done.37), channel_id=1, source_target_pairs={{0,4},{4,0},{8,12},{12,8},{16,20},{20,16},{24,28},{28,24},{1,5},{5... | collective-permute-start | bytes 1572872 | tf_op jit(solution)/shard_map/ppermute | solution.py:40
  393.8 73.2 %collective-permute-start.75 = (bf16[256,2048]{1,0:T(8,128)(2,1)}, bf16[256,2048]{1,0:T(8,128)(2,1)}, u32[]{:S(2)}, u32[]{:S(2)}) collective-permute-start(bf16[256,2048]{1,0:T(8,128)(2,1)} %add.583), channel_id=1, source_target_pairs={{1,0},{2,3},{5,4},{6,7},{9,8},{10,11},{13,12},{14,15},{17,16},{18,... | collective-permute-start | bytes 3145736 | tf_op jit(solution)/shard_map/ppermute | solution.py:44
  395.1 72.0 %collective-permute-start.111 = (bf16[256,2048]{1,0:T(8,128)(2,1)}, bf16[256,2048]{1,0:T(8,128)(2,1)}, u32[]{:S(2)}, u32[]{:S(2)}) collective-permute-start(bf16[256,2048]{1,0:T(8,128)(2,1)} %broadcast_select_fusion.5), channel_id=1, source_target_pairs={{0,0},{4,8},{8,16},{12,24},{16,4},{20,12},{24,20},{28,28},{1,1},{5... | collective-permute-start | bytes 3145736 | tf_op jit(solution)/shard_map/ppermute | solution.py:393
  404.6 59.2 %collective-permute-start.90 = (bf16[256,2048]{1,0:T(8,128)(2,1)}, bf16[256,2048]{1,0:T(8,128)(2,1)}, u32[]{:S(2)}, u32[]{:S(2)}) collective-permute-start(bf16[256,2048]{1,0:T(8,128)(2,1)} %collective-permute-done.87), channel_id=1, source_target_pairs={{0,1},{3,2},{4,5},{7,6},{8,9},{11,10},{12,13},{15,14},{16,17},{19,... | collective-permute-start | bytes 3145736 | tf_op jit(solution)/shard_map/ppermute | solution.py:44
  494.9 58.4 %collective-permute-start.48 = (bf16[128,2048]{1,0:T(8,128)(2,1)S(1)}, bf16[128,2048]{1,0:T(8,128)(2,1)S(1)}, u32[]{:S(2)}, u32[]{:S(2)}) collective-permute-start(bf16[128,2048]{1,0:T(8,128)(2,1)S(1)} %get-tuple-element.188), channel_id=1, source_target_pairs={{0,16},{4,20},{8,24},{12,28},{16,0},{20,4},{24,8},{28,12},{1,17},{... | collective-permute-start | bytes 1572872 | tf_op jit(solution)/shard_map/ppermute | solution.py:40
  497.1 76.2 %collective-permute-start.112 = (bf16[256,2048]{1,0:T(8,128)(2,1)S(1)}, bf16[256,2048]{1,0:T(8,128)(2,1)S(1)}, u32[]{:S(2)}, u32[]{:S(2)}) collective-permute-start(bf16[256,2048]{1,0:T(8,128)(2,1)S(1)} %copy-done.57), channel_id=1, source_target_pairs={{0,0},{4,8},{8,16},{12,24},{16,4},{20,12},{24,20},{28,28},{1,1},{5... | collective-permute-start | bytes 3145736 | tf_op jit(solution)/shard_map/ppermute | solution.py:393
  503.4 70.4 %collective-permute-start.113 = (bf16[256,2048]{1,0:T(8,128)(2,1)S(1)}, bf16[256,2048]{1,0:T(8,128)(2,1)S(1)}, u32[]{:S(2)}, u32[]{:S(2)}) collective-permute-start(bf16[256,2048]{1,0:T(8,128)(2,1)S(1)} %broadcast_select_fusion.3), channel_id=1, source_target_pairs={{0,0},{4,8},{8,16},{12,24},{16,4},{20,12},{24,20},{28,28},{1,1},{5... | collective-permute-start | bytes 3145736 | tf_op jit(solution)/shard_map/ppermute | solution.py:393
  511.8 60.5 %collective-permute-start.91 = (bf16[256,2048]{1,0:T(8,128)(2,1)S(1)}, bf16[256,2048]{1,0:T(8,128)(2,1)S(1)}, u32[]{:S(2)}, u32[]{:S(2)}) collective-permute-start(bf16[256,2048]{1,0:T(8,128)(2,1)S(1)} %copy-done.33), channel_id=1, source_target_pairs={{0,1},{3,2},{4,5},{7,6},{8,9},{11,10},{12,13},{15,14},{16,17},{19,... | collective-permute-start | bytes 3145736 | tf_op jit(solution)/shard_map/ppermute | solution.py:44
  573.3 61.9 %collective-permute-start.43 = (bf16[512,2048]{1,0:T(8,128)(2,1)}, bf16[512,2048]{1,0:T(8,128)(2,1)}, u32[]{:S(2)}, u32[]{:S(2)}) collective-permute-start(bf16[512,2048]{1,0:T(8,128)(2,1)} %fusion.13), channel_id=1, source_target_pairs={{0,4},{4,0},{8,12},{12,8},{16,20},{20,16},{24,28},{28,24},{1,5},{5... | collective-permute-start | bytes 6291464 | tf_op jit(solution)/shard_map/ppermute | solution.py:40
  657.4 74.1 %collective-permute-start.107 = (bf16[256,2048]{1,0:T(8,128)(2,1)}, bf16[256,2048]{1,0:T(8,128)(2,1)}, u32[]{:S(2)}, u32[]{:S(2)}) collective-permute-start(bf16[256,2048]{1,0:T(8,128)(2,1)} %get-tuple-element.117), channel_id=1, source_target_pairs={{0,28},{4,24},{8,20},{12,16},{16,12},{20,8},{24,4},{28,0},{1,29},{... | collective-permute-start | bytes 3145736 | tf_op jit(solution)/shard_map/ppermute | solution.py:40
  657.5 51.0 %collective-permute-start.93 = (bf16[256,2048]{1,0:T(8,128)(2,1)}, bf16[256,2048]{1,0:T(8,128)(2,1)}, u32[]{:S(2)}, u32[]{:S(2)}) collective-permute-start(bf16[256,2048]{1,0:T(8,128)(2,1)} %convolution_convert_fusion.5), channel_id=1, source_target_pairs={{0,1},{3,2},{4,5},{7,6},{8,9},{11,10},{12,13},{15,14},{16,17},{19,... | collective-permute-start | bytes 3145736 | tf_op jit(solution)/shard_map/ppermute | solution.py:44
  677.8 54.5 %collective-permute-start.66 = (bf16[8,256,384]{2,1,0:T(8,128)(2,1)}, bf16[8,256,384]{2,1,0:T(8,128)(2,1)}, u32[]{:S(2)}, u32[]{:S(2)}) collective-permute-start(bf16[8,256,384]{2,1,0:T(8,128)(2,1)} %constant_dynamic-update-slice_fusion.18), channel_id=1, source_target_pairs={{0,1},{3,2},{4,5},{7,6},{8,9},{11,10},{12,13},{15,14},{16,17},{19,... | collective-permute-start | bytes 4718600 | tf_op jit(solution)/shard_map/ppermute | solution.py:44
  744.4 73.3 %collective-permute-start.44 = (bf16[128,2048]{1,0:T(8,128)(2,1)S(1)}, bf16[128,2048]{1,0:T(8,128)(2,1)S(1)}, u32[]{:S(2)}, u32[]{:S(2)}) collective-permute-start(bf16[128,2048]{1,0:T(8,128)(2,1)S(1)} %copy-done.66), channel_id=1, source_target_pairs={{0,16},{4,20},{8,24},{12,28},{16,0},{20,4},{24,8},{28,12},{1,17},{... | collective-permute-start | bytes 1572872 | tf_op jit(solution)/shard_map/ppermute | solution.py:40
  757.4 55.2 %collective-permute-start.105 = (bf16[256,2048]{1,0:T(8,128)(2,1)S(1)}, bf16[256,2048]{1,0:T(8,128)(2,1)S(1)}, u32[]{:S(2)}, u32[]{:S(2)}) collective-permute-start(bf16[256,2048]{1,0:T(8,128)(2,1)S(1)} %add.601), channel_id=1, source_target_pairs={{1,0},{2,3},{5,4},{6,7},{9,8},{10,11},{13,12},{14,15},{17,16},{18,... | collective-permute-start | bytes 3145736 | tf_op jit(solution)/shard_map/ppermute | solution.py:44
  760.4 54.6 %collective-permute-start.109 = (bf16[256,2048]{1,0:T(8,128)(2,1)S(1)}, bf16[256,2048]{1,0:T(8,128)(2,1)S(1)}, u32[]{:S(2)}, u32[]{:S(2)}) collective-permute-start(bf16[256,2048]{1,0:T(8,128)(2,1)S(1)} %add.612), channel_id=1, source_target_pairs={{1,2},{2,1},{5,6},{6,5},{9,10},{10,9},{13,14},{14,13},{17,18},{18,... | collective-permute-start | bytes 3145736 | tf_op jit(solution)/shard_map/ppermute | solution.py:44
  761.2 57.9 %collective-permute-start.46 = (bf16[128,2048]{1,0:T(8,128)(2,1)S(1)}, bf16[128,2048]{1,0:T(8,128)(2,1)S(1)}, u32[]{:S(2)}, u32[]{:S(2)}) collective-permute-start(bf16[128,2048]{1,0:T(8,128)(2,1)S(1)} %copy-done.65), channel_id=1, source_target_pairs={{0,24},{4,28},{8,16},{12,20},{16,8},{20,12},{24,0},{28,4},{1,25},{... | collective-permute-start | bytes 1572872 | tf_op jit(solution)/shard_map/ppermute | solution.py:40
  812.6 71.9 %collective-permute-start.80 = (bf16[8,256,384]{2,1,0:T(8,128)(2,1)}, bf16[8,256,384]{2,1,0:T(8,128)(2,1)}, u32[]{:S(2)}, u32[]{:S(2)}) collective-permute-start(bf16[8,256,384]{2,1,0:T(8,128)(2,1)} %add.578), channel_id=1, source_target_pairs={{1,0},{2,3},{5,4},{6,7},{9,8},{10,11},{13,12},{14,15},{17,16},{18,... | collective-permute-start | bytes 4718600 | tf_op jit(solution)/shard_map/ppermute | solution.py:44
  817.7 62.3 %collective-permute-start.110 = (bf16[256,2048]{1,0:T(8,128)(2,1)}, bf16[256,2048]{1,0:T(8,128)(2,1)}, u32[]{:S(2)}, u32[]{:S(2)}) collective-permute-start(bf16[256,2048]{1,0:T(8,128)(2,1)} %add.613.sum_ref), channel_id=1, source_target_pairs={{1,0},{2,3},{5,4},{6,7},{9,8},{10,11},{13,12},{14,15},{17,16},{18,... | collective-permute-start | bytes 3145736 | tf_op jit(solution)/shard_map/ppermute | solution.py:44
  819.0 58.2 %collective-permute-start.106 = (bf16[256,2048]{1,0:T(8,128)(2,1)}, bf16[256,2048]{1,0:T(8,128)(2,1)}, u32[]{:S(2)}, u32[]{:S(2)}) collective-permute-start(bf16[256,2048]{1,0:T(8,128)(2,1)} %broadcast_select_fusion.6), channel_id=1, source_target_pairs={{0,0},{4,8},{8,16},{12,24},{16,4},{20,12},{24,20},{28,28},{1,1},{5... | collective-permute-start | bytes 3145736 | tf_op jit(solution)/shard_map/ppermute | solution.py:393
  (170 other events, 3864.5 us)

commit v4 on v3

--- a/solution.py
+++ b/solution.py
@@ -259,22 +259,46 @@
     )(table, *args)
 
 
+class Clock:
+    def __init__(self):
+        self.kept = []
+        self.before = ()
+
+    def start(self, x):
+        return after(x, *self.before) if self.before else x
+
+    def keep(self, x):
+        self.kept.append(x)
+        return x
+
+    def next(self):
+        self.before, self.kept = tuple(self.kept), []
+
+
 class Line:
-    def __init__(self, z):
+    def __init__(self, clock, z):
+        self.clock = clock
         self.inner = (z == 1) | (z == 2)
-        self.rounds = ([], [], [])
-
-    def send(self, stage, x, pairs):
-        sent = self.rounds[stage]
-        if len(sent) >= 2:
-            x = after(x, sent[-2])
-        sent.append(along(x, pairs))
-        return x, sent[-1]
-
-    def sum(self, x):
-        x, more = self.send(0, x, [(0, 1), (3, 2)])
-        x, more = self.send(1, x + more, [(1, 2), (2, 1)])
-        return self.send(2, x + more, [(1, 0), (2, 3)])
+        self.across = None
+        self.back = None
+
+    def send(self, x, pairs):
+        x = self.clock.start(x)
+        return x, self.clock.keep(along(x, pairs))
+
+    def step(self, x=None):
+        done = None
+        chunk, middle, self.across = x, self.across, None
+        if chunk is not None:
+            chunk, more = self.send(chunk, [(0, 1), (3, 2)])
+            self.across = chunk + more
+        if self.back is not None:
+            done = self.send(self.back, [(1, 0), (2, 3)])
+            self.back = None
+        if middle is not None:
+            middle, more = self.send(middle, [(1, 2), (2, 1)])
+            self.back = middle + more
+        return done
 
     def pick(self, summed, copied):
         return jnp.where(self.inner, summed, copied)
@@ -329,20 +353,29 @@
         return jnp.swapaxes(y, 0, 1).reshape(x.shape)
 
     def scatter(self, left, right, product):
-        rows = left.shape[0]
         if not self.cube:
             whole = self.from_groups(product(left, right).astype(BF16))
-            total = lax.psum_scatter(whole, PLANE, scatter_dimension=0, tiled=True).astype(F32)
-            return total, whole
-        half = rows // 2
-        far = swap(product(left[half:], right).astype(BF16), 1)
+            return lax.psum_scatter(whole, PLANE, scatter_dimension=0, tiled=True).astype(F32)
+        return self.close(*self.near_half(left, right, product, self.far_half(left, right, product)))
+
+    def far_half(self, left, right, product):
+        return swap(product(left[left.shape[0] // 2 :], right).astype(BF16), 1)
+
+    def near_half(self, left, right, product, far):
+        half = left.shape[0] // 2
+        size = half // 4
         near = product(left[:half], right) + far.astype(F32)
-        size = half // 4
-        total = near[:size]
-        pieces = [near[i * size : (i + 1) * size].astype(BF16) for i in (1, 2, 3)]
+        return near[:size], [near[i * size : (i + 1) * size].astype(BF16) for i in (1, 2, 3)]
+
+    def close(self, total, pieces, clock=None):
+        got = []
         for i, piece in enumerate(pieces):
-            total = total + swap(piece, ORDER[i + 1]).astype(F32)
-        return total, pieces[0]
+            got.append(swap(clock.start(piece) if clock else piece, ORDER[i + 1]))
+        for piece in got:
+            if clock:
+                clock.keep(piece)
+            total = total + piece.astype(F32)
+        return total
 
     def reshard(self, columns):
         if not self.cube:
@@ -359,18 +392,19 @@
         return out, tuple(got[1:])
 
     def reshard_shared(self, columns, first):
-        own = columns(self.unit, 0, 1)
-        rows, width = own.shape
-        half = rows // 2
         part = self.z & 1
-        near = swap(columns(self.np * (self.f ^ 1) + self.p, 0, 1), 1)
         got = []
         for k in (2, 3):
             piece = columns(self.np * (self.f ^ k) + self.p, part, 2)
-            got.append(swap(after(piece, *first, *got), k))
+            got.append(swap(after(piece, *first), k))
 
         def finish(hold):
-            out = jnp.zeros((self.nf * rows, width), own.dtype)
+            zero = after(jnp.zeros((), BF16), hold)
+            own = columns(after(self.unit, hold), 0, 1)
+            rows, width = own.shape
+            half = rows // 2
+            near = swap(columns(after(self.np * (self.f ^ 1) + self.p, hold), 0, 1), 1)
+            out = jnp.broadcast_to(zero, (self.nf * rows, width))
             out = lax.dynamic_update_slice(out, own, (self.f * rows, 0))
             out = lax.dynamic_update_slice(out, near, ((self.f ^ 1) * rows, 0))
             for k, piece in zip((2, 3), got):
@@ -412,17 +446,7 @@
     def block_for(self, split, m):
         return lax.dynamic_index_in_dim(split, self.place ^ m, 0, keepdims=False)
 
-    def exchange(self, split):
-        order = jnp.take(split, self.place ^ jnp.arange(8), axis=0)
-        near = order[0::2]
-        far = swap(order[1::2], 1)
-        both = [jnp.stack([near[j], far[j]]) for j in range(4)]
-        return jnp.concatenate([both[0]] + [swap(both[j], 2 * j) for j in (1, 2, 3)], axis=0)
-
     def total(self, sums, top):
-        if not (self.cube and self.line):
-            everyone = ("pair", "fsdp", "rep")
-            return lax.psum(sums, everyone), lax.pmax(top, everyone)
         count = sums.shape[0]
         both = jnp.concatenate([sums, top], axis=0)
 
@@ -433,12 +457,13 @@
 
         for m in (1, 2, 4):
             both = join(both, swap(both, m))
-        ends = [(0, 1), (3, 2)]
+            yield both
         inner = (self.z == 1) | (self.z == 2)
-        both = jnp.where(inner, join(both, along(both, ends)), both)
+        both = jnp.where(inner, join(both, along(both, [(0, 1), (3, 2)])), both)
+        yield both
         both = join(both, along(both, [(1, 2), (2, 1)]))
-        both = jnp.where(inner, both, along(both, [(1, 0), (2, 3)]))
-        return both[:count], both[count:]
+        yield both
+        yield jnp.where(inner, both, along(both, [(1, 0), (2, 3)]))
 
 
 def norm_back(grad_normed, unit, inv_scale, gain):
@@ -503,7 +528,7 @@
         where = plane.gather_small(where)
         gains = plane.gather_gains(gains)
         w_qkv, arrived = plane.reshard(qkv_columns)
-        finish_gate_up = plane.reshard_shared(mlp_columns, (crossed,) + arrived)
+        finish_gate_up = plane.reshard_shared(mlp_columns, (parts[0],) + arrived)
         low_crossed = swap(after(low_out, crossed), 2)
         low_parts = plane.gather_parts(low_out, low_crossed, (parts[1],))
         grad_branch = jnp.concatenate(
@@ -535,9 +560,13 @@
     flops = 4 * count * length * HEAD * heads
 
     inputs = tokens.astype(F32)
-    branch, sent = plane.scatter(attended, w_out, dot)
     if fast:
-        w_gate_up = finish_gate_up(sent)
+        far = plane.far_half(attended, w_out, dot)
+        total, pieces = plane.near_half(attended, w_out, dot, far)
+        w_gate_up = finish_gate_up(pieces[0])
+        branch = plane.close(total, pieces)
+    else:
+        branch = plane.scatter(attended, w_out, dot)
     middle = inputs + RESID * branch
     inv_two = lax.rsqrt(jnp.mean(middle * middle, axis=-1, keepdims=True) + EPS)
     unit_two = middle * inv_two
@@ -554,10 +583,12 @@
     grad_up = (grad_hidden * silu_gate).astype(BF16)
     grad_gate_up = jnp.concatenate([grad_gate, grad_up], axis=1)
 
-    def back(grad_normed_mlp):
+    def branch_back(grad_normed_mlp):
         grad_mid_norm, gain_two_grad = norm_back(grad_normed_mlp, unit_two, inv_two, gain_two)
         grad_middle = grad_out + grad_mid_norm
-        grad_attn_branch = plane.gather((RESID * grad_middle).astype(BF16))
+        return grad_middle, gain_two_grad, (RESID * grad_middle).astype(BF16)
+
+    def attention_back(grad_attn_branch):
         grad_attended = times_t(grad_attn_branch, w_out).astype(BF16)
         (grad_lin,) = per_group(
             attend_back_kernel,
@@ -568,68 +599,146 @@
             "attend_back",
             3 * flops,
         )
-        return grad_middle, grad_attn_branch, grad_lin, gain_two_grad
-
+        return grad_lin
+
+    inv_one = lax.rsqrt(jnp.mean(inputs * inputs, axis=-1, keepdims=True) + EPS)
+
+    def input_back(grad_normed):
+        return norm_back(grad_normed, inputs * inv_one, inv_one, gain_one)
+
+    top_local = jnp.max(tops.reshape(-1, 8, 128), axis=(0, 2))[:heads]
+    top_row = jnp.full((1, D), -jnp.inf, F32)
+    top_row = lax.dynamic_update_slice(top_row, top_local[None], (0, unit * heads))
     rows = D // n
     shape = (rows, 2 * FF)
     if fast:
-        line = Line(plane.z)
+        clock = Clock()
+        start, keep, tick = clock.start, clock.keep, clock.next
+        line = Line(clock, plane.z)
         each = ff // 4
-        downs = [
-            outer(hidden[:, i * each : (i + 1) * each], grad_branch).astype(BF16) for i in range(4)
-        ]
-        grad_gate_up = after(grad_gate_up, *downs)
-        downs = [line.sum(x) for x in downs]
-        grad_normed_mlp, sent = plane.scatter(grad_gate_up, w_gate_up, times_t)
-        term = outer(after(normed_mlp, sent), grad_gate_up).astype(BF16).reshape(n, rows, 2 * ff)
-        blocks = {0: plane.block_for(term, 0), 1: swap(plane.block_for(term, 1), 1)}
-        hold = (grad_normed_mlp,)
-        for pair in ((2, 4), (3, 5), (6,), (7,)):
-            for m in pair:
-                blocks[m] = swap(after(plane.block_for(term, m), *hold), m)
-            hold = tuple(blocks[m] for m in pair)
-        grad_middle, grad_attn_branch, grad_lin, gain_two_grad = back(grad_normed_mlp)
-        o_term = outer(attended, grad_attn_branch).astype(BF16)
-        branch, _ = plane.scatter(after(hidden, grad_attn_branch), w_down, dot)
-        grad_normed, _ = plane.scatter(grad_lin, w_qkv, times_t)
-        lin_term = plane.exchange(outer(normed, grad_lin).astype(BF16).reshape(n, rows, -1))
-        gate_up_grad = None
-
-        def put(m, into):
+
+        def down_term(i):
+            return outer(hidden[:, i * each : (i + 1) * each], grad_branch).astype(BF16)
+
+        def put(m, sums, into):
             u = plane.unit_of(plane.place ^ m)
             table = jnp.stack([line.inner.astype(jnp.int32), u, n + u])
-            return place(table, *line.sum(blocks[m]), into, shape, "place_gate_up")
-
-        for m in (0, 1, 2, 4, 3, 5, 6):
-            gate_up_grad = put(m, gate_up_grad)
-        o_grad = plane.to_owner(line.pick(*line.sum(o_term))).astype(F32)
-        lin_rows = line.pick(*line.sum(lin_term))
+            return keep(place(table, *sums, into, shape, "place_gate_up"))
+
+        def own_down(sums):
+            return keep(plane.to_owner(start(line.pick(*sums))))
+
+        line.step(down_term(0))
+        down_next = keep(down_term(1))
+        far = keep(plane.far_half(grad_gate_up, w_gate_up, times_t))
+        tick()
+        line.step(down_next)
+        down_next, down_last = keep(down_term(2)), keep(down_term(3))
+        grad_mlp = plane.near_half(start(grad_gate_up), w_gate_up, times_t, far)
+        keep(grad_mlp[0])
+        tick()
+        downs = [line.step(down_next)]
+        grad_normed_mlp = plane.close(*grad_mlp, clock)
+        term = outer(start(normed_mlp), grad_gate_up).astype(BF16).reshape(n, rows, 2 * ff)
+        blocks = [keep(plane.block_for(term, m)) for m in range(8)]
+        tick()
+        downs.append(line.step(down_last))
+        for m in (1, 2, 4):
+            blocks[m] = keep(swap(start(blocks[m]), m))
+        grad_middle, gain_two_grad, low_branch = branch_back(grad_normed_mlp)
+        keep(low_branch)
+        far = keep(plane.far_half(start(hidden), w_down, dot))
+        tick()
+        downs.append(line.step(blocks[0]))
+        low_branch = start(low_branch)
+        near = [low_branch] + [keep(swap(low_branch, m)) for m in ORDER[1:4]]
+        branch = plane.near_half(start(hidden), w_down, dot, far)
+        keep(branch[0])
+        tick()
+        downs.append(line.step(blocks[1]))
+        near += [swap(start(piece), 1) for piece in near]
+        for m in (3, 5):
+            blocks[m] = keep(swap(start(blocks[m]), m))
+        grad_attn_branch = jnp.concatenate(near, axis=0)
+        grad_lin = keep(attention_back(grad_attn_branch))
+        tick()
+        sums = {0: line.step(blocks[2])}
+        blocks[6] = keep(swap(start(blocks[6]), 6))
+        o_term = keep(outer(start(attended), grad_attn_branch).astype(BF16))
+        far = keep(plane.far_half(start(grad_lin), w_qkv, times_t))
+        lin_term = outer(normed, start(grad_lin)).astype(BF16).reshape(n, rows, -1)
+        lin_term = keep(jnp.take(lin_term, plane.place ^ jnp.arange(8), axis=0))
+        tick()
+        sums[1] = line.step(blocks[4])
+        blocks[7] = keep(swap(start(blocks[7]), 7))
+        lin_far = keep(swap(start(lin_term[1::2]), 1))
+        grad_in = plane.near_half(start(grad_lin), w_qkv, times_t, far)
+        keep(grad_in[0])
+        gate_up_grad = put(0, sums[0], None)
+        tick()
+        sums[2] = line.step(blocks[3])
+        grad_normed = plane.close(*grad_in, clock)
+        lin_both = [keep(jnp.stack([start(lin_term[2 * j]), lin_far[j]])) for j in range(4)]
+        gate_up_grad = put(1, sums[1], gate_up_grad)
+        tick()
+        sums[4] = line.step(blocks[5])
+        lin_both = lin_both[:1] + [keep(swap(start(lin_both[j]), 2 * j)) for j in (1, 2, 3)]
+        grad_in_norm, gain_one_grad = input_back(grad_normed)
+        keep(gain_one_grad)
+        gate_up_grad = put(2, sums[2], gate_up_grad)
+        rounds = plane.total(start(jnp.stack([gain_one_grad, gain_two_grad])), top_row)
+        keep(next(rounds))
+        tick()
+        sums[3] = line.step(blocks[6])
+        branch = plane.close(*branch, clock)
+        lin_both = keep(jnp.concatenate(lin_both, axis=0))
+        gate_up_grad = put(4, sums[4], gate_up_grad)
+        keep(next(rounds))
+        tick()
+        sums[5] = line.step(o_term)
+        down_grads = [own_down(downs[0])]
+        gate_up_grad = put(3, sums[3], gate_up_grad)
+        keep(next(rounds))
+        tick()
+        sums[6] = line.step(lin_both)
+        down_grads.append(own_down(downs[1]))
+        gate_up_grad = put(5, sums[5], gate_up_grad)
+        keep(next(rounds))
+        tick()
+        o_sums = line.step(blocks[7])
+        down_grads += [own_down(downs[2]), own_down(downs[3])]
+        gate_up_grad = put(6, sums[6], gate_up_grad)
+        keep(next(rounds))
+        tick()
+        lin_rows = line.pick(*line.step())
+        o_grad = keep(plane.to_owner(start(line.pick(*o_sums)))).astype(F32)
+        everything = keep(next(rounds))
+        gain_grads, top_row = everything[:2], everything[2:]
+        tick()
+        last = line.step()
         lin_units = plane.unit_of(plane.place ^ jnp.arange(8))
-        gate_up_grad = put(7, gate_up_grad)
-        down_grad = jnp.concatenate(
-            [plane.to_owner(line.pick(*x)).astype(F32) for x in downs], axis=0
-        )
+        down_grad = jnp.concatenate([x.astype(F32) for x in down_grads], axis=0)
+        gate_up_grad = put(7, last, gate_up_grad)
     else:
         down_grad = plane.sum_units(outer(hidden, grad_branch)).astype(F32)
         full, units = plane.sum_rows(outer(normed_mlp, grad_gate_up))
         full = plane.in_order(full, units).reshape(rows, n, 2, ff)
         gate_up_grad = jnp.swapaxes(full, 1, 2).reshape(shape).astype(F32)
-        grad_normed_mlp, _ = plane.scatter(grad_gate_up, w_gate_up, times_t)
-        grad_middle, grad_attn_branch, grad_lin, gain_two_grad = back(grad_normed_mlp)
-        branch, _ = plane.scatter(hidden, w_down, dot)
-        grad_normed, _ = plane.scatter(grad_lin, w_qkv, times_t)
+        grad_normed_mlp = plane.scatter(grad_gate_up, w_gate_up, times_t)
+        grad_middle, gain_two_grad, low_branch = branch_back(grad_normed_mlp)
+        grad_attn_branch = plane.gather(low_branch)
+        grad_lin = attention_back(grad_attn_branch)
+        branch = plane.scatter(hidden, w_down, dot)
+        grad_normed = plane.scatter(grad_lin, w_qkv, times_t)
+        grad_in_norm, gain_one_grad = input_back(grad_normed)
         o_grad = plane.sum_units(outer(attended, grad_attn_branch)).astype(F32)
         lin_rows, lin_units = plane.sum_rows(outer(normed, grad_lin))
+        everyone = ("pair", "fsdp", "rep")
+        gain_grads = lax.psum(jnp.stack([gain_one_grad, gain_two_grad]), everyone)
+        top_row = lax.pmax(top_row, everyone)
 
     result = (middle + RESID * branch).astype(BF16)
-    inv_one = lax.rsqrt(jnp.mean(inputs * inputs, axis=-1, keepdims=True) + EPS)
-    grad_in_norm, gain_one_grad = norm_back(grad_normed, inputs * inv_one, inv_one, gain_one)
     input_grad = (grad_middle + grad_in_norm).astype(BF16)
-
-    top_local = jnp.max(tops.reshape(-1, 8, 128), axis=(0, 2))[:heads]
-    top_row = jnp.full((1, D), -jnp.inf, F32)
-    top_row = lax.dynamic_update_slice(top_row, top_local[None], (0, unit * heads))
-    gain_grads, top_row = plane.total(jnp.stack([gain_one_grad, gain_two_grad]), top_row)
     factor = TAU / jnp.maximum(top_row[0, :HEADS], TAU)
     k_factor = jnp.repeat(jnp.min(factor.reshape(KV_HEADS, GROUP), axis=1), HEAD)
     lin_rows = plane.in_order(lin_rows, lin_units).astype(F32)

time: 918 us -> 867 us (0.944)
  waiting for transfers between devices: 317 us -> 272 us
  starting transfers between devices: 255 us -> 220 us
  other arithmetic: 110 us -> 140 us
    ppermute x47, waiting for transfers between devices: 199 us -> 159 us  [along(): return lax.ppermute(x, 'rep', pairs)]
    ppermute x47, starting transfers between devices: 160 us -> 128 us  [along(): return lax.ppermute(x, 'rep', pairs)]
    add x28, other arithmetic: 40.7 us -> 66.7 us  [the longest x14 33.7 us: step(): self.across = chunk + more]
    ppermute x63, starting transfers between devices: 72.8 us -> 53.2 us  [swap(): return lax.ppermute(x, PLANE, [(i, i ^ mask) for i in range(devices)])]
    ppermute x5, starting transfers between devices: 21.4 us -> 38.5 us  [to_owner(): return lax.ppermute(x, PLANE, pairs)]
    unnamed x181 -> x184, local copies, waits for them, and re-layouts: 17.1 us -> 21.5 us
  transfers between devices with their start and end apart: 115 -> 115, of which waited for: 34 -> 38; matrix products, arithmetic and copies ran while one was open for 23% -> 31% of each run, Pallas kernels for 7% -> 6%
where the time goes in v4:
time: 867 us; the launch traced here: 857 us
  waiting for transfers between devices  272 us (31%)
  starting transfers between devices  220 us (25%)
  other arithmetic  140 us (16%)
  matrix products  97.2 us (11%)
  local copies, waits for them, and re-layouts  65.6 us (8%)
  Pallas kernels  59.7 us (7%)
    ppermute x47, waiting for transfers between devices, along(): return lax.ppermute(x, 'rep', pairs)  159 us
    ppermute x47, starting transfers between devices, along(): return lax.ppermute(x, 'rep', pairs)  128 us
    ppermute x63, waiting for transfers between devices, swap(): return lax.ppermute(x, PLANE, [(i, i ^ mask) for i in range(devices)])  113 us
    ppermute x63, starting transfers between devices, swap(): return lax.ppermute(x, PLANE, [(i, i ^ mask) for i in range(devices)])  53.2 us
    ppermute x5, starting transfers between devices, to_owner(): return lax.ppermute(x, PLANE, pairs)  38.5 us
    dot_general x7, matrix products, outer(): lax.dot_general(left, right, (((0,), (0,)), ((), ())), preferred_element_...  35.9 us
    pallas_call x8, Pallas kernels, place(): pl.pallas_call(place_kernel, grid_spec=pltpu.PrefetchScalarGridSpec(num_s...  35.8 us
    add x14, other arithmetic, step(): self.across = chunk + more  33.7 us
  transfers between devices with their start and end apart: 115, of which 38 were waited for; matrix products, arithmetic and copies ran while one was open for 31% of the time, Pallas kernels for 6%

profile of v4, /device:TPU:0, one launch (start us, length us, event | category | flops | bytes accessed | tf_op | source)
XLA Modules:
  0.0 856.8 jit_solution(16301812447637682652)
XLA Ops:
  42.5 16.2 %collective-permute-done.1.refs_1_ = bf16[2,128,2048]{2,1,0:T(8,128)(2,1)} collective-permute-done((bf16[2,128,2048]{2,1,0:T(8,128)(2,1)}, bf16[2,128,2048]{2,1,0:T(8,128)(2,1)}, u32[]{:S(2)}, u32[]{:S(2)}) %collective-permute-start.1) | collective-permute-done | bytes 1048608 | tf_op jit(solution)/shard_map/ppermute | solution.py:40
  75.7 11.8 %attend.1 = (bf16[1024,2048]{1,0:T(8,128)(2,1)}, bf16[1024,384]{1,0:T(8,128)(2,1)}, bf16[1024,256]{1,0:T(8,128)(2,1)}, f32[32,128]{1,0:T(8,128)}) custom-call(bf16[2,128,2048]{2,1,0:T(8,128)(2,1)} %pad_maximum_fusion.2.refs_0_, bf16[2,128,2048]{2,1,0:T(8,128)(2,1)} %collective-permute-done.1.refs_1_, bf16[2,128,2048]{2,1,0:T(8,128)(2,1)} %collective-permute-done.2.refs_2_, ...), custom_call_target="tpu_custom_call" | custom-call | flops 1610612736 | bytes 16777216 | tf_op jit(solution)/shard_map/attend/pallas_call | solution.py:156
  117.1 16.4 %collective-permute-done.14 = bf16[128,2048]{1,0:T(8,128)(2,1)S(1)} collective-permute-done((bf16[128,2048]{1,0:T(8,128)(2,1)}, bf16[128,2048]{1,0:T(8,128)(2,1)S(1)}, u32[]{:S(2)}, u32[]{:S(2)}) %collective-permute-start.14) | collective-permute-done | bytes 524320 | tf_op jit(solution)/shard_map/ppermute | solution.py:40
  133.5 10.4 %collective-permute-done.15 = bf16[128,2048]{1,0:T(8,128)(2,1)} collective-permute-done((bf16[128,2048]{1,0:T(8,128)(2,1)}, bf16[128,2048]{1,0:T(8,128)(2,1)}, u32[]{:S(2)}, u32[]{:S(2)}) %collective-permute-start.15) | collective-permute-done | bytes 524320 | tf_op jit(solution)/shard_map/ppermute | solution.py:40
  149.2 8.6 fusion.9
  163.0 10.2 %collective-permute-done.18 = bf16[128,2048]{1,0:T(8,128)(2,1)S(1)} collective-permute-done((bf16[128,2048]{1,0:T(8,128)(2,1)S(1)}, bf16[128,2048]{1,0:T(8,128)(2,1)S(1)}, u32[]{:S(2)}, u32[]{:S(2)}) %collective-permute-start.18) | collective-permute-done | bytes 524320 | tf_op jit(solution)/shard_map/ppermute | solution.py:40
  178.3 8.6 %collective-permute-done.25 = bf16[256,2048]{1,0:T(8,128)(2,1)S(1)} collective-permute-done((bf16[256,2048]{1,0:T(8,128)(2,1)}, bf16[256,2048]{1,0:T(8,128)(2,1)S(1)}, u32[]{:S(2)}, u32[]{:S(2)}) %collective-permute-start.25) | collective-permute-done | bytes 1048608 | tf_op jit(solution)/shard_map/ppermute | solution.py:44
  188.4 19.0 %collective-permute-done.27 = bf16[256,2048]{1,0:T(8,128)(2,1)S(1)} collective-permute-done((bf16[256,2048]{1,0:T(8,128)(2,1)}, bf16[256,2048]{1,0:T(8,128)(2,1)S(1)}, u32[]{:S(2)}, u32[]{:S(2)}) %collective-permute-start.27) | collective-permute-done | bytes 1048608 | tf_op jit(solution)/shard_map/ppermute | solution.py:44
  275.5 12.7 %collective-permute-done.34 = bf16[256,2048]{1,0:T(8,128)(2,1)} collective-permute-done((bf16[256,2048]{1,0:T(8,128)(2,1)}, bf16[256,2048]{1,0:T(8,128)(2,1)}, u32[]{:S(2)}, u32[]{:S(2)}) %collective-permute-start.34) | collective-permute-done | bytes 1048608 | tf_op jit(solution)/shard_map/ppermute | solution.py:44
  304.3 10.9 %convolution_convert_fusion = bf16[2048,2048]{1,0:T(8,128)(2,1)S(1)} fusion(bf16[1024,2048]{1,0:T(8,128)(2,1)} %copy-done.58, bf16[1024,1024]{1,0:T(8,128)(2,1)S(1)} %copy-done.12, bf16[1024,1024]{1,0:T(8,128)(2,1)S(1)} %copy-done.14), kind=kOutput, calls=%fused_computation.3 | convolution fusion | flops 8602517504 | bytes 16777216 | tf_op jit(solution)/shard_map/dot_general | solution.py:32
  361.0 12.4 %collective-permute-done.43 = bf16[256,2048]{1,0:T(8,128)(2,1)S(1)} collective-permute-done((bf16[256,2048]{1,0:T(8,128)(2,1)S(1)}, bf16[256,2048]{1,0:T(8,128)(2,1)S(1)}, u32[]{:S(2)}, u32[]{:S(2)}) %collective-permute-start.43) | collective-permute-done | bytes 1048608 | tf_op jit(solution)/shard_map/ppermute | solution.py:44
  428.1 12.1 %attend_back.1 = bf16[1024,384]{1,0:T(8,128)(2,1)} custom-call(bf16[1024,384]{1,0:T(8,128)(2,1)} %get-tuple-element.144.refs_0_, f32[1024,128]{1,0:T(8,128)} %get-tuple-element.315.refs_6_.refs_1_, f32[1024,128]{1,0:T(8,128)} %get-tuple-element.314.refs_7_.refs_2_, f32[1024,256]{1,0:T(8,128)} %fusion.37.refs_8_.refs_3_, ...), custom_call_target="tpu_custom_call" | custom-call | flops 805306368 | bytes 4718592 | tf_op jit(solution)/shard_map/attend_back/pallas_call | solution.py:210
  462.6 8.3 collective-permute-start.64
  483.9 8.2 collective-permute-done.64
  561.8 8.9 %collective-permute-done.75.copy_ref = bf16[256,2048]{1,0:T(8,128)(2,1)} collective-permute-done((bf16[256,2048]{1,0:T(8,128)(2,1)}, bf16[256,2048]{1,0:T(8,128)(2,1)}, u32[]{:S(2)}, u32[]{:S(2)}) %collective-permute-start.75) | collective-permute-done | bytes 1048608 | tf_op jit(solution)/shard_map/ppermute | solution.py:44
  635.6 8.0 collective-permute-done.87
  662.8 9.4 %collective-permute-start.97 = (bf16[256,2048]{1,0:T(8,128)(2,1)}, bf16[256,2048]{1,0:T(8,128)(2,1)}, u32[]{:S(2)}, u32[]{:S(2)}) collective-permute-start(bf16[256,2048]{1,0:T(8,128)(2,1)} %broadcast_select_fusion.6), channel_id=1, source_target_pairs={{0,0},{4,8},{8,16},{12,24},{16,4},{20,12},{24,20},{28,28},{1,1},{5... | collective-permute-start | bytes 3145736 | tf_op jit(solution)/shard_map/ppermute | solution.py:427
  686.9 8.2 collective-permute-done.95.copy_ref
  713.4 9.4 %collective-permute-start.102 = (bf16[256,2048]{1,0:T(8,128)(2,1)}, bf16[256,2048]{1,0:T(8,128)(2,1)}, u32[]{:S(2)}, u32[]{:S(2)}) collective-permute-start(bf16[256,2048]{1,0:T(8,128)(2,1)} %broadcast_select_fusion.5), channel_id=1, source_target_pairs={{0,0},{4,8},{8,16},{12,24},{16,4},{20,12},{24,20},{28,28},{1,1},{5... | collective-permute-start | bytes 3145736 | tf_op jit(solution)/shard_map/ppermute | solution.py:427
  735.1 8.0 collective-permute-done.100.copy_ref
  750.3 9.5 %collective-permute-start.108 = (bf16[256,2048]{1,0:T(8,128)(2,1)}, bf16[256,2048]{1,0:T(8,128)(2,1)}, u32[]{:S(2)}, u32[]{:S(2)}) collective-permute-start(bf16[256,2048]{1,0:T(8,128)(2,1)} %broadcast_select_fusion.3), channel_id=1, source_target_pairs={{0,0},{4,8},{8,16},{12,24},{16,4},{20,12},{24,20},{28,28},{1,1},{5... | collective-permute-start | bytes 3145736 | tf_op jit(solution)/shard_map/ppermute | solution.py:427
  759.7 9.4 %collective-permute-start.107 = (bf16[256,2048]{1,0:T(8,128)(2,1)}, bf16[256,2048]{1,0:T(8,128)(2,1)}, u32[]{:S(2)}, u32[]{:S(2)}) collective-permute-start(bf16[256,2048]{1,0:T(8,128)(2,1)} %broadcast_select_fusion.4), channel_id=1, source_target_pairs={{0,0},{4,8},{8,16},{12,24},{16,4},{20,12},{24,20},{28,28},{1,1},{5... | collective-permute-start | bytes 3145736 | tf_op jit(solution)/shard_map/ppermute | solution.py:427
  788.6 12.0 %collective-permute-done.106 = bf16[256,2048]{1,0:T(8,128)(2,1)} collective-permute-done((bf16[256,2048]{1,0:T(8,128)(2,1)}, bf16[256,2048]{1,0:T(8,128)(2,1)}, u32[]{:S(2)}, u32[]{:S(2)}) %collective-permute-start.106) | collective-permute-done | bytes 1048608 | tf_op jit(solution)/shard_map/ppermute | solution.py:44
  816.6 17.7 %collective-permute-done.110 = bf16[8,256,384]{2,1,0:T(8,128)(2,1)S(1)} collective-permute-done((bf16[8,256,384]{2,1,0:T(8,128)(2,1)S(1)}, bf16[8,256,384]{2,1,0:T(8,128)(2,1)S(1)}, u32[]{:S(2)}, u32[]{:S(2)}) %collective-permute-start.110) | collective-permute-done | bytes 1572896 | tf_op jit(solution)/shard_map/ppermute | solution.py:44
  (590 shorter events, 587.4 us)
Async XLA Ops:
  6.2 57.6 %collective-permute-start.6 = (bf16[512,384]{1,0:T(8,128)(2,1)}, bf16[512,384]{1,0:T(8,128)(2,1)}, u32[]{:S(2)}, u32[]{:S(2)}) collective-permute-start(bf16[512,384]{1,0:T(8,128)(2,1)} %pad_maximum_fusion.6), channel_id=1, source_target_pairs={{0,4},{4,0},{8,12},{12,8},{16,20},{20,16},{24,28},{28,24},{1,5},{5... | collective-permute-start | bytes 1179656 | tf_op jit(solution)/shard_map/ppermute | solution.py:40
  7.5 63.5 %collective-permute-start.7 = (bf16[512,384]{1,0:T(8,128)(2,1)}, bf16[512,384]{1,0:T(8,128)(2,1)}, u32[]{:S(2)}, u32[]{:S(2)}) collective-permute-start(bf16[512,384]{1,0:T(8,128)(2,1)} %pad_maximum_fusion.7), channel_id=1, source_target_pairs={{0,8},{4,12},{8,0},{12,4},{16,24},{20,28},{24,16},{28,20},{1,9},{5... | collective-permute-start | bytes 1179656 | tf_op jit(solution)/shard_map/ppermute | solution.py:40
  42.5 32.2 %collective-permute-start.2 = (bf16[2,128,2048]{2,1,0:T(8,128)(2,1)}, bf16[2,128,2048]{2,1,0:T(8,128)(2,1)}, u32[]{:S(2)}, u32[]{:S(2)}) collective-permute-start(bf16[2,128,2048]{2,1,0:T(8,128)(2,1)} %pad_maximum_fusion.2.refs_0_), channel_id=1, source_target_pairs={{0,4},{4,0},{8,12},{12,8},{16,20},{20,16},{24,28},{28,24},{1,5},{5... | collective-permute-start | bytes 3145736 | tf_op jit(solution)/shard_map/ppermute | solution.py:40
  73.6 84.2 %collective-permute-start.24 = (bf16[256,2048]{1,0:T(8,128)(2,1)}, bf16[256,2048]{1,0:T(8,128)(2,1)}, u32[]{:S(2)}, u32[]{:S(2)}) collective-permute-start(bf16[256,2048]{1,0:T(8,128)(2,1)} %get-tuple-element.111), channel_id=1, source_target_pairs={{0,8},{4,12},{8,0},{12,4},{16,24},{20,28},{24,16},{28,20},{1,9},{5... | collective-permute-start | bytes 3145736 | tf_op jit(solution)/shard_map/ppermute | solution.py:40
  74.1 86.6 %collective-permute-start.26 = (bf16[256,2048]{1,0:T(8,128)(2,1)}, bf16[256,2048]{1,0:T(8,128)(2,1)}, u32[]{:S(2)}, u32[]{:S(2)}) collective-permute-start(bf16[256,2048]{1,0:T(8,128)(2,1)} %get-tuple-element.113), channel_id=1, source_target_pairs={{0,12},{4,8},{8,4},{12,0},{16,28},{20,24},{24,20},{28,16},{1,13},{... | collective-permute-start | bytes 3145736 | tf_op jit(solution)/shard_map/ppermute | solution.py:40
  104.4 39.6 %collective-permute-start.15 = (bf16[128,2048]{1,0:T(8,128)(2,1)}, bf16[128,2048]{1,0:T(8,128)(2,1)}, u32[]{:S(2)}, u32[]{:S(2)}) collective-permute-start(bf16[128,2048]{1,0:T(8,128)(2,1)} %get-tuple-element.278), channel_id=1, source_target_pairs={{0,24},{4,28},{8,16},{12,20},{16,8},{20,12},{24,0},{28,4},{1,25},{... | collective-permute-start | bytes 1572872 | tf_op jit(solution)/shard_map/ppermute | solution.py:40
  117.1 58.8 %collective-permute-start.23 = (bf16[512,2048]{1,0:T(8,128)(2,1)S(1)}, bf16[512,2048]{1,0:T(8,128)(2,1)S(1)}, u32[]{:S(2)}, u32[]{:S(2)}) collective-permute-start(bf16[512,2048]{1,0:T(8,128)(2,1)S(1)} %pad_maximum_fusion.1), channel_id=1, source_target_pairs={{0,4},{4,0},{8,12},{12,8},{16,20},{20,16},{24,28},{28,24},{1,5},{5... | collective-permute-start | bytes 6291464 | tf_op jit(solution)/shard_map/ppermute | solution.py:40
  173.9 33.6 %collective-permute-start.27 = (bf16[256,2048]{1,0:T(8,128)(2,1)}, bf16[256,2048]{1,0:T(8,128)(2,1)S(1)}, u32[]{:S(2)}, u32[]{:S(2)}) collective-permute-start(bf16[256,2048]{1,0:T(8,128)(2,1)} %collective-permute-done.26), channel_id=1, source_target_pairs={{0,1},{1,0},{2,3},{3,2},{4,5},{5,4},{6,7},{7,6},{8,9},{9,8},{10,11... | collective-permute-start | bytes 3145736 | tf_op jit(solution)/shard_map/ppermute | solution.py:44
  290.8 34.5 %collective-permute-start.38 = (bf16[256,2048]{1,0:T(8,128)(2,1)S(1)}, bf16[256,2048]{1,0:T(8,128)(2,1)S(1)}, u32[]{:S(2)}, u32[]{:S(2)}) collective-permute-start(bf16[256,2048]{1,0:T(8,128)(2,1)S(1)} %add.551), channel_id=1, source_target_pairs={{1,2},{2,1},{5,6},{6,5},{9,10},{10,9},{13,14},{14,13},{17,18},{18,... | collective-permute-start | bytes 3145736 | tf_op jit(solution)/shard_map/ppermute | solution.py:44
  334.3 39.1 %collective-permute-start.48 = (bf16[512,2048]{1,0:T(8,128)(2,1)}, bf16[512,2048]{1,0:T(8,128)(2,1)}, u32[]{:S(2)}, u32[]{:S(2)}) collective-permute-start(bf16[512,2048]{1,0:T(8,128)(2,1)} %fusion.13), channel_id=1, source_target_pairs={{0,4},{4,0},{8,12},{12,8},{16,20},{20,16},{24,28},{28,24},{1,5},{5... | collective-permute-start | bytes 6291464 | tf_op jit(solution)/shard_map/ppermute | solution.py:40
  449.5 48.4 %collective-permute-start.68 = (bf16[512,2048]{1,0:T(8,128)(2,1)}, bf16[512,2048]{1,0:T(8,128)(2,1)}, u32[]{:S(2)}, u32[]{:S(2)}) collective-permute-start(bf16[512,2048]{1,0:T(8,128)(2,1)} %convolution_convert_fusion.2), channel_id=1, source_target_pairs={{0,4},{4,0},{8,12},{12,8},{16,20},{20,16},{24,28},{28,24},{1,5},{5... | collective-permute-start | bytes 6291464 | tf_op jit(solution)/shard_map/ppermute | solution.py:40
  455.3 42.6 %collective-permute-start.65 = (bf16[256,2048]{1,0:T(8,128)(2,1)}, bf16[256,2048]{1,0:T(8,128)(2,1)}, u32[]{:S(2)}, u32[]{:S(2)}) collective-permute-start(bf16[256,2048]{1,0:T(8,128)(2,1)} %add.572.sum_ref), channel_id=1, source_target_pairs={{1,0},{2,3},{5,4},{6,7},{9,8},{10,11},{13,12},{14,15},{17,16},{18,... | collective-permute-start | bytes 3145736 | tf_op jit(solution)/shard_map/ppermute | solution.py:44
  456.6 41.4 %collective-permute-start.67 = (bf16[256,2048]{1,0:T(8,128)(2,1)}, bf16[256,2048]{1,0:T(8,128)(2,1)}, u32[]{:S(2)}, u32[]{:S(2)}) collective-permute-start(bf16[256,2048]{1,0:T(8,128)(2,1)} %get-tuple-element.152), channel_id=1, source_target_pairs={{0,24},{4,28},{8,16},{12,20},{16,8},{20,12},{24,0},{28,4},{1,25},{... | collective-permute-start | bytes 3145736 | tf_op jit(solution)/shard_map/ppermute | solution.py:40
  461.0 34.1 %collective-permute-start.66 = (bf16[256,2048]{1,0:T(8,128)(2,1)}, bf16[256,2048]{1,0:T(8,128)(2,1)}, u32[]{:S(2)}, u32[]{:S(2)}) collective-permute-start(bf16[256,2048]{1,0:T(8,128)(2,1)} %add.573), channel_id=1, source_target_pairs={{1,2},{2,1},{5,6},{6,5},{9,10},{10,9},{13,14},{14,13},{17,18},{18,... | collective-permute-start | bytes 3145736 | tf_op jit(solution)/shard_map/ppermute | solution.py:44
  622.1 34.8 %collective-permute-start.92 = (bf16[256,2048]{1,0:T(8,128)(2,1)}, bf16[256,2048]{1,0:T(8,128)(2,1)}, u32[]{:S(2)}, u32[]{:S(2)}) collective-permute-start(bf16[256,2048]{1,0:T(8,128)(2,1)} %add.602), channel_id=1, source_target_pairs={{1,2},{2,1},{5,6},{6,5},{9,10},{10,9},{13,14},{14,13},{17,18},{18,... | collective-permute-start | bytes 3145736 | tf_op jit(solution)/shard_map/ppermute | solution.py:44
  623.8 33.2 %collective-permute-start.91 = (bf16[256,2048]{1,0:T(8,128)(2,1)}, bf16[256,2048]{1,0:T(8,128)(2,1)}, u32[]{:S(2)}, u32[]{:S(2)}) collective-permute-start(bf16[256,2048]{1,0:T(8,128)(2,1)} %add.601.sum_ref), channel_id=1, source_target_pairs={{1,0},{2,3},{5,4},{6,7},{9,8},{10,11},{13,12},{14,15},{17,16},{18,... | collective-permute-start | bytes 3145736 | tf_op jit(solution)/shard_map/ppermute | solution.py:44
  625.2 31.7 %collective-permute-start.90 = (bf16[256,2048]{1,0:T(8,128)(2,1)}, bf16[256,2048]{1,0:T(8,128)(2,1)}, u32[]{:S(2)}, u32[]{:S(2)}) collective-permute-start(bf16[256,2048]{1,0:T(8,128)(2,1)} %collective-permute-done.67), channel_id=1, source_target_pairs={{0,1},{3,2},{4,5},{7,6},{8,9},{11,10},{12,13},{15,14},{16,17},{19,... | collective-permute-start | bytes 3145736 | tf_op jit(solution)/shard_map/ppermute | solution.py:44
  648.7 33.0 %collective-permute-start.103 = (f32[3,2048]{1,0:T(4,128)S(1)}, f32[3,2048]{1,0:T(4,128)S(1)}, u32[]{:S(2)}, u32[]{:S(2)}) collective-permute-start(f32[3,2048]{1,0:T(4,128)S(1)} %pad_maximum_fusion.16), channel_id=1, source_target_pairs={{0,1},{3,2},{4,5},{7,6},{8,9},{11,10},{12,13},{15,14},{16,17},{19,... | collective-permute-start | bytes 73736 | tf_op jit(solution)/shard_map/ppermute | solution.py:44
  681.8 44.1 %collective-permute-start.109 = (f32[3,2048]{1,0:T(4,128)S(1)}, f32[3,2048]{1,0:T(4,128)S(1)}, u32[]{:S(2)}, u32[]{:S(2)}) collective-permute-start(f32[3,2048]{1,0:T(4,128)S(1)} %maximum_select_fusion), channel_id=1, source_target_pairs={{1,2},{2,1},{5,6},{6,5},{9,10},{10,9},{13,14},{14,13},{17,18},{18,... | collective-permute-start | bytes 73736 | tf_op jit(solution)/shard_map/ppermute | solution.py:44
  699.7 32.0 %collective-permute-start.99 = (bf16[8,256,384]{2,1,0:T(8,128)(2,1)}, bf16[8,256,384]{2,1,0:T(8,128)(2,1)}, u32[]{:S(2)}, u32[]{:S(2)}) collective-permute-start(bf16[8,256,384]{2,1,0:T(8,128)(2,1)} %constant_dynamic-update-slice_fusion.18), channel_id=1, source_target_pairs={{0,1},{3,2},{4,5},{7,6},{8,9},{11,10},{12,13},{15,14},{16,17},{19,... | collective-permute-start | bytes 4718600 | tf_op jit(solution)/shard_map/ppermute | solution.py:44
  725.9 46.6 %collective-permute-start.111 = (f32[3,2048]{1,0:T(4,128)S(1)}, f32[3,2048]{1,0:T(4,128)S(1)}, u32[]{:S(2)}, u32[]{:S(2)}) collective-permute-start(f32[3,2048]{1,0:T(4,128)S(1)} %pad_maximum_fusion.17), channel_id=1, source_target_pairs={{1,0},{2,3},{5,4},{6,7},{9,8},{10,11},{13,12},{14,15},{17,16},{18,... | collective-permute-start | bytes 73736 | tf_op jit(solution)/shard_map/ppermute | solution.py:44
  743.1 43.0 %collective-permute-start.104 = (bf16[8,256,384]{2,1,0:T(8,128)(2,1)}, bf16[8,256,384]{2,1,0:T(8,128)(2,1)}, u32[]{:S(2)}, u32[]{:S(2)}) collective-permute-start(bf16[8,256,384]{2,1,0:T(8,128)(2,1)} %add.613), channel_id=1, source_target_pairs={{1,2},{2,1},{5,6},{6,5},{9,10},{10,9},{13,14},{14,13},{17,18},{18,... | collective-permute-start | bytes 4718600 | tf_op jit(solution)/shard_map/ppermute | solution.py:44
  750.3 38.3 %collective-permute-start.108 = (bf16[256,2048]{1,0:T(8,128)(2,1)}, bf16[256,2048]{1,0:T(8,128)(2,1)}, u32[]{:S(2)}, u32[]{:S(2)}) collective-permute-start(bf16[256,2048]{1,0:T(8,128)(2,1)} %broadcast_select_fusion.3), channel_id=1, source_target_pairs={{0,0},{4,8},{8,16},{12,24},{16,4},{20,12},{24,20},{28,28},{1,1},{5... | collective-permute-start | bytes 3145736 | tf_op jit(solution)/shard_map/ppermute | solution.py:427
  800.6 33.8 %collective-permute-start.110 = (bf16[8,256,384]{2,1,0:T(8,128)(2,1)S(1)}, bf16[8,256,384]{2,1,0:T(8,128)(2,1)S(1)}, u32[]{:S(2)}, u32[]{:S(2)}) collective-permute-start(bf16[8,256,384]{2,1,0:T(8,128)(2,1)S(1)} %add.620), channel_id=1, source_target_pairs={{1,0},{2,3},{5,4},{6,7},{9,8},{10,11},{13,12},{14,15},{17,16},{18,... | collective-permute-start | bytes 4718600 | tf_op jit(solution)/shard_map/ppermute | solution.py:44
  (171 other events, 3387.2 us)

commit v5 on v4

--- a/solution.py
+++ b/solution.py
@@ -22,6 +22,7 @@
 F32 = jnp.float32
 BF16 = jnp.bfloat16
 ORDER = (0, 4, 2, 6, 1, 5, 3, 7)
+LAG = 1
 
 
 def dot(left, right):
@@ -225,18 +226,17 @@
 
     @pl.when(table[0] == 1)
     def _():
-        out_ref[...] = sum_ref[...].astype(F32)
+        out_ref[...] = sum_ref[0].astype(F32)
 
     @pl.when(table[0] == 0)
     def _():
-        out_ref[...] = copy_ref[...].astype(F32)
+        out_ref[...] = copy_ref[0].astype(F32)
 
 
 def place(table, summed, copied, into, shape, name):
-    rows, width = summed.shape
-    half = rows // 2
+    count, rows, width = summed.shape
     columns = width // 2
-    piece = pl.BlockSpec((half, columns), lambda i, j, t: (j, i))
+    piece = pl.BlockSpec((1, rows, columns), lambda b, i, t: (b, 0, i))
     in_specs = [piece, piece]
     args = [summed, copied]
     aliases = {}
@@ -248,31 +248,36 @@
         place_kernel,
         grid_spec=pltpu.PrefetchScalarGridSpec(
             num_scalar_prefetch=1,
-            grid=(2, 2),
+            grid=(count, 2),
             in_specs=in_specs,
-            out_specs=pl.BlockSpec((half, columns), lambda i, j, t: (j, t[1 + i])),
+            out_specs=pl.BlockSpec((rows, columns), lambda b, i, t: (0, t[1 + 2 * b + i])),
         ),
         out_shape=jax.ShapeDtypeStruct(shape, F32),
         input_output_aliases=aliases,
         name=name,
-        cost_estimate=pl.CostEstimate(flops=0, bytes_accessed=8 * rows * width, transcendentals=0),
+        cost_estimate=pl.CostEstimate(
+            flops=0, bytes_accessed=8 * count * rows * width, transcendentals=0
+        ),
     )(table, *args)
 
 
 class Clock:
     def __init__(self):
         self.kept = []
-        self.before = ()
+        self.past = []
 
     def start(self, x):
-        return after(x, *self.before) if self.before else x
+        if len(self.past) < LAG:
+            return x
+        return after(x, *self.past[-LAG])
 
     def keep(self, x):
         self.kept.append(x)
         return x
 
     def next(self):
-        self.before, self.kept = tuple(self.kept), []
+        self.past.append(tuple(self.kept))
+        self.kept = []
 
 
 class Line:
@@ -282,23 +287,29 @@
         self.across = None
         self.back = None
 
-    def send(self, x, pairs):
-        x = self.clock.start(x)
-        return x, self.clock.keep(along(x, pairs))
-
-    def step(self, x=None):
-        done = None
-        chunk, middle, self.across = x, self.across, None
-        if chunk is not None:
-            chunk, more = self.send(chunk, [(0, 1), (3, 2)])
-            self.across = chunk + more
-        if self.back is not None:
-            done = self.send(self.back, [(1, 0), (2, 3)])
-            self.back = None
-        if middle is not None:
+    def send(self, arrays, pairs):
+        arrays = [self.clock.start(x) for x in arrays]
+        return arrays, [self.clock.keep(along(x, pairs)) for x in arrays]
+
+    def step(self, chunk=None):
+        total, self.back = self.back, None
+        middle, self.across = self.across, None
+        out, home = [(0, 1), (3, 2)], [(1, 0), (2, 3)]
+        done = got = ()
+        if total and chunk and [x.shape for x in total] == [x.shape for x in chunk]:
+            mixed = [jnp.where(self.inner, x, y) for x, y in zip(total, chunk)]
+            done, got = self.send(mixed, out + home)
+            self.across = [x + y for x, y in zip(chunk, got)]
+        else:
+            if chunk:
+                chunk, more = self.send(chunk, out)
+                self.across = [x + y for x, y in zip(chunk, more)]
+            if total:
+                done, got = self.send(total, home)
+        if middle:
             middle, more = self.send(middle, [(1, 2), (2, 1)])
-            self.back = middle + more
-        return done
+            self.back = [x + y for x, y in zip(middle, more)]
+        return list(zip(done, got))
 
     def pick(self, summed, copied):
         return jnp.where(self.inner, summed, copied)
@@ -329,7 +340,7 @@
     def gather_parts(self, x, swapped, hold=()):
         two = jnp.stack([x, swapped])
         other = swap(after(two, *hold), 4)
-        return two, other, swap(two, 1), swap(other, 1)
+        return two, other, swap(after(two, other), 1), swap(other, 1)
 
     def gather_small(self, x):
         pair = jnp.concatenate([x, swap(x, 4)], axis=1)
@@ -384,7 +395,8 @@
             return got.reshape((-1,) + got.shape[2:]), ()
         own = columns(self.unit)
         rows = own.shape[0]
-        got = [swap(columns(self.np * (self.f ^ k) + self.p), k) for k in (1, 2, 3)]
+        got = [swap(columns(self.np * (self.f ^ k) + self.p), k) for k in (2, 3)]
+        got = [swap(columns(after(self.np * (self.f ^ 1) + self.p, *got)), 1)] + got
         out = jnp.zeros((self.nf * rows,) + own.shape[1:], own.dtype)
         out = lax.dynamic_update_slice(out, own, (self.f * rows, 0))
         for k, piece in zip((1, 2, 3), got):
@@ -392,29 +404,48 @@
         return out, tuple(got[1:])
 
     def reshard_shared(self, columns, first):
-        part = self.z & 1
         got = []
         for k in (2, 3):
-            piece = columns(self.np * (self.f ^ k) + self.p, part, 2)
-            got.append(swap(after(piece, *first), k))
+            got.append(swap(columns(after(self.np * (self.f ^ k) + self.p, *first), self.z, 4), k))
+        sides = self.line_sides(jnp.stack(got))
 
         def finish(hold):
             zero = after(jnp.zeros((), BF16), hold)
             own = columns(after(self.unit, hold), 0, 1)
             rows, width = own.shape
-            half = rows // 2
+            quarter = rows // 4
             near = swap(columns(after(self.np * (self.f ^ 1) + self.p, hold), 0, 1), 1)
+            shards = sides + self.line_rest(*[after(side, hold) for side in sides[1:]])
             out = jnp.broadcast_to(zero, (self.nf * rows, width))
             out = lax.dynamic_update_slice(out, own, (self.f * rows, 0))
             out = lax.dynamic_update_slice(out, near, ((self.f ^ 1) * rows, 0))
-            for k, piece in zip((2, 3), got):
-                start = (self.f ^ k) * rows
-                other = along(after(piece, hold), [(0, 1), (1, 0), (2, 3), (3, 2)])
-                out = lax.dynamic_update_slice(out, piece, (start + part * half, 0))
-                out = lax.dynamic_update_slice(out, other, (start + (1 - part) * half, 0))
+            for shard, where in reversed(list(zip(shards, self.line_shards()))):
+                for i, k in enumerate((2, 3)):
+                    start = (self.f ^ k) * rows + where * quarter
+                    out = lax.dynamic_update_slice(out, shard[i], (start, 0))
             return out
 
-        return finish
+        return finish, tuple(got)
+
+    def line_shards(self):
+        z = self.z
+        return (
+            z,
+            jnp.maximum(z - 1, 0),
+            jnp.minimum(z + 1, 3),
+            jnp.where(z < 2, z + 2, z - 2),
+            jnp.where(z == 0, 3, jnp.where(z == 3, 0, z)),
+        )
+
+    def line_sides(self, own):
+        right = along(own, [(0, 1), (1, 2), (2, 3)])
+        return own, right, along(own, [(1, 0), (2, 1), (3, 2)])
+
+    def line_rest(self, right, left):
+        two = jnp.where(
+            self.z < 2, along(left, [(1, 0), (2, 1)]), along(right, [(1, 2), (2, 3)])
+        )
+        return two, along(two, [(2, 3), (1, 0)])
 
     def unit_of(self, place):
         return self.np * (place % self.nf) + place // self.nf
@@ -424,7 +455,8 @@
         for p in range(self.np):
             for f in range(self.nf):
                 pairs.append((p * self.nf + f, self.np * f + p))
-        return lax.ppermute(x, PLANE, pairs)
+        moved = lax.ppermute(x, PLANE, [pair for pair in pairs if pair[0] != pair[1]])
+        return jnp.where(self.place == self.unit, x, moved)
 
     def sum_rows(self, term):
         rows, width = term.shape
@@ -527,13 +559,13 @@
         parts = plane.gather_parts(tokens, crossed)
         where = plane.gather_small(where)
         gains = plane.gather_gains(gains)
-        w_qkv, arrived = plane.reshard(qkv_columns)
-        finish_gate_up = plane.reshard_shared(mlp_columns, (parts[0],) + arrived)
-        low_crossed = swap(after(low_out, crossed), 2)
-        low_parts = plane.gather_parts(low_out, low_crossed, (parts[1],))
-        grad_branch = jnp.concatenate(
-            [low_parts[i][j] for i, j in ((0, 0), (1, 0), (0, 1), (1, 1), (2, 0), (3, 0), (2, 1), (3, 1))], axis=0
-        )
+        w_qkv, arrived = plane.reshard(lambda u: qkv_columns(after(u, parts[0])))
+        finish_gate_up, quarters = plane.reshard_shared(mlp_columns, (parts[0],))
+        w_qkv = after(w_qkv, *quarters)
+        low_swapped = swap(after(low_out, parts[1]), 4)
+        w_qkv = after(w_qkv, low_swapped)
+        low_pair = jnp.stack([low_out, low_swapped])
+        low_other = swap(after(low_pair, *quarters), 2)
     else:
         by_group = plane.gather(tokens).reshape(-1, 2, length // 2, D)
         near = by_group.shape[0] // 2
@@ -572,6 +604,10 @@
     unit_two = middle * inv_two
     low_two = (unit_two * gain_two).astype(BF16)
     normed_mlp = plane.gather(low_two)
+    if fast:
+        low_parts = [after(low_pair, *pieces), after(low_other, *pieces)]
+        low_parts += [swap(part, 1) for part in low_parts]
+        grad_branch = jnp.concatenate([part.reshape(-1, D) for part in low_parts], axis=0)
     grad_hidden = lax.optimization_barrier(times_t(grad_branch, w_down))
 
     gate = lax.optimization_barrier(dot(normed_mlp, w_gate_up[:, :ff]))
@@ -615,110 +651,93 @@
         clock = Clock()
         start, keep, tick = clock.start, clock.keep, clock.next
         line = Line(clock, plane.z)
-        each = ff // 4
+        each = ff // 2
 
         def down_term(i):
-            return outer(hidden[:, i * each : (i + 1) * each], grad_branch).astype(BF16)
-
-        def put(m, sums, into):
-            u = plane.unit_of(plane.place ^ m)
-            table = jnp.stack([line.inner.astype(jnp.int32), u, n + u])
-            return keep(place(table, *sums, into, shape, "place_gate_up"))
-
-        def own_down(sums):
+            columns = hidden[:, i * each : (i + 1) * each]
+            return outer(start(columns), grad_branch).astype(BF16)
+
+        def put(pair, sums, into):
+            units = [plane.unit_of(plane.place ^ m) for m in pair]
+            table = jnp.stack([line.inner.astype(jnp.int32)] + [i * n + u for u in units for i in (0, 1)])
+            return keep(place(table, *sums[0], into, shape, "place_gate_up"))
+
+        def own_rows(sums):
             return keep(plane.to_owner(start(line.pick(*sums))))
 
-        line.step(down_term(0))
+        def both(pair):
+            return [jnp.stack([blocks[m] for m in pair])]
+
+        down_first = down_term(0)
+        line.step([down_first])
+        grad_gate_up = after(grad_gate_up, down_first)
         down_next = keep(down_term(1))
-        far = keep(plane.far_half(grad_gate_up, w_gate_up, times_t))
+        far = plane.far_half(grad_gate_up, w_gate_up, times_t)
+        grad_mlp = plane.near_half(grad_gate_up, w_gate_up, times_t, far)
+        grad_normed_mlp = plane.close(*grad_mlp, clock)
+        late = after(normed_mlp, grad_mlp[1][0])
+        term = outer(late, grad_gate_up).astype(BF16).reshape(n, rows, 2 * ff)
+        blocks = [keep(plane.block_for(term, m)) for m in range(8)]
+        blocks[1] = keep(swap(blocks[1], 1))
         tick()
-        line.step(down_next)
-        down_next, down_last = keep(down_term(2)), keep(down_term(3))
-        grad_mlp = plane.near_half(start(grad_gate_up), w_gate_up, times_t, far)
-        keep(grad_mlp[0])
-        tick()
-        downs = [line.step(down_next)]
-        grad_normed_mlp = plane.close(*grad_mlp, clock)
-        term = outer(start(normed_mlp), grad_gate_up).astype(BF16).reshape(n, rows, 2 * ff)
-        blocks = [keep(plane.block_for(term, m)) for m in range(8)]
-        tick()
-        downs.append(line.step(down_last))
-        for m in (1, 2, 4):
-            blocks[m] = keep(swap(start(blocks[m]), m))
+        line.step([down_next])
         grad_middle, gain_two_grad, low_branch = branch_back(grad_normed_mlp)
-        keep(low_branch)
-        far = keep(plane.far_half(start(hidden), w_down, dot))
-        tick()
-        downs.append(line.step(blocks[0]))
-        low_branch = start(low_branch)
-        near = [low_branch] + [keep(swap(low_branch, m)) for m in ORDER[1:4]]
-        branch = plane.near_half(start(hidden), w_down, dot, far)
+        near = [low_branch] + [swap(low_branch, m) for m in ORDER[1:4]]
+        near += [keep(swap(piece, 1)) for piece in near]
+        late = after(start(hidden), low_branch)
+        branch = plane.near_half(late, w_down, dot, plane.far_half(late, w_down, dot))
         keep(branch[0])
         tick()
-        downs.append(line.step(blocks[1]))
-        near += [swap(start(piece), 1) for piece in near]
+        downs = line.step(both((0, 1)))
+        for m in (2, 4):
+            blocks[m] = keep(swap(start(blocks[m]), m))
+        grad_attn_branch = start(jnp.concatenate(near, axis=0))
+        grad_lin = attention_back(grad_attn_branch)
+        grad_in = plane.near_half(grad_lin, w_qkv, times_t, plane.far_half(grad_lin, w_qkv, times_t))
+        keep(grad_in[0])
+        lin_term = outer(normed, grad_lin).astype(BF16).reshape(n, rows, -1)
+        lin_term = keep(jnp.take(lin_term, plane.place ^ jnp.arange(8), axis=0))
+        o_term = keep(outer(attended, after(grad_attn_branch, lin_term)).astype(BF16))
+        tick()
+        downs += line.step(both((2, 4)))
+        grad_normed = plane.close(*grad_in, clock)
         for m in (3, 5):
-            blocks[m] = keep(swap(start(blocks[m]), m))
-        grad_attn_branch = jnp.concatenate(near, axis=0)
-        grad_lin = keep(attention_back(grad_attn_branch))
+            blocks[m] = keep(swap(after(start(blocks[m]), grad_normed), m))
+        lin_far = keep(swap(start(lin_term[1::2]), 1))
         tick()
-        sums = {0: line.step(blocks[2])}
-        blocks[6] = keep(swap(start(blocks[6]), 6))
-        o_term = keep(outer(start(attended), grad_attn_branch).astype(BF16))
-        far = keep(plane.far_half(start(grad_lin), w_qkv, times_t))
-        lin_term = outer(normed, start(grad_lin)).astype(BF16).reshape(n, rows, -1)
-        lin_term = keep(jnp.take(lin_term, plane.place ^ jnp.arange(8), axis=0))
-        tick()
-        sums[1] = line.step(blocks[4])
-        blocks[7] = keep(swap(start(blocks[7]), 7))
-        lin_far = keep(swap(start(lin_term[1::2]), 1))
-        grad_in = plane.near_half(start(grad_lin), w_qkv, times_t, far)
-        keep(grad_in[0])
-        gate_up_grad = put(0, sums[0], None)
-        tick()
-        sums[2] = line.step(blocks[3])
-        grad_normed = plane.close(*grad_in, clock)
-        lin_both = [keep(jnp.stack([start(lin_term[2 * j]), lin_far[j]])) for j in range(4)]
-        gate_up_grad = put(1, sums[1], gate_up_grad)
-        tick()
-        sums[4] = line.step(blocks[5])
+        first = line.step(both((3, 5)))
+        lin_both = [jnp.stack([lin_term[2 * j], lin_far[j]]) for j in range(4)]
         lin_both = lin_both[:1] + [keep(swap(start(lin_both[j]), 2 * j)) for j in (1, 2, 3)]
-        grad_in_norm, gain_one_grad = input_back(grad_normed)
-        keep(gain_one_grad)
-        gate_up_grad = put(2, sums[2], gate_up_grad)
-        rounds = plane.total(start(jnp.stack([gain_one_grad, gain_two_grad])), top_row)
+        blocks[6] = keep(swap(after(start(blocks[6]), *lin_both[1:]), 6))
+        grad_in_norm, gain_one_grad = input_back(start(grad_normed))
+        rounds = plane.total(jnp.stack([gain_one_grad, gain_two_grad]), top_row)
         keep(next(rounds))
         tick()
-        sums[3] = line.step(blocks[6])
-        branch = plane.close(*branch, clock)
-        lin_both = keep(jnp.concatenate(lin_both, axis=0))
-        gate_up_grad = put(4, sums[4], gate_up_grad)
+        second = line.step([o_term, jnp.concatenate(lin_both, axis=0)])
+        blocks[7] = keep(swap(start(blocks[7]), 7))
+        gate_up_grad = put((0, 1), first, None)
+        next(rounds)
         keep(next(rounds))
         tick()
-        sums[5] = line.step(o_term)
-        down_grads = [own_down(downs[0])]
-        gate_up_grad = put(3, sums[3], gate_up_grad)
+        third = line.step(both((6, 7)))
+        gate_up_grad = put((2, 4), second, gate_up_grad)
+        down_grads = [own_rows(downs[0])]
         keep(next(rounds))
         tick()
-        sums[6] = line.step(lin_both)
-        down_grads.append(own_down(downs[1]))
-        gate_up_grad = put(5, sums[5], gate_up_grad)
+        mixed = line.step()
+        gate_up_grad = put((3, 5), third, gate_up_grad)
+        down_grads.append(own_rows(downs[1]))
         keep(next(rounds))
-        tick()
-        o_sums = line.step(blocks[7])
-        down_grads += [own_down(downs[2]), own_down(downs[3])]
-        gate_up_grad = put(6, sums[6], gate_up_grad)
-        keep(next(rounds))
-        tick()
-        lin_rows = line.pick(*line.step())
-        o_grad = keep(plane.to_owner(start(line.pick(*o_sums)))).astype(F32)
         everything = keep(next(rounds))
         gain_grads, top_row = everything[:2], everything[2:]
         tick()
         last = line.step()
+        branch = plane.close(*branch, clock)
+        o_grad = own_rows(mixed[0]).astype(F32)
+        lin_rows = line.pick(*mixed[1])
         lin_units = plane.unit_of(plane.place ^ jnp.arange(8))
         down_grad = jnp.concatenate([x.astype(F32) for x in down_grads], axis=0)
-        gate_up_grad = put(7, last, gate_up_grad)
+        gate_up_grad = put((6, 7), last, gate_up_grad)
     else:
         down_grad = plane.sum_units(outer(hidden, grad_branch)).astype(F32)
         full, units = plane.sum_rows(outer(normed_mlp, grad_gate_up))

time: 867 us -> 866 us (level)
  starting transfers between devices: 220 us -> 151 us
  waiting for transfers between devices: 272 us -> 333 us
  local copies, waits for them, and re-layouts: 65.6 us -> 91 us
  Pallas kernels: 59.7 us -> 45.7 us
  other arithmetic: 140 us -> 130 us
    ppermute x63, waiting for transfers between devices: 113 us -> 155 us  [swap(): return lax.ppermute(x, PLANE, [(i, i ^ mask) for i in range(devices)])]
    ppermute x47 -> x30, starting transfers between devices: 128 us -> 89.9 us  [along(): return lax.ppermute(x, 'rep', pairs)]
    ppermute x5 -> x3, starting transfers between devices: 38.5 us -> 4.89 us  [to_owner(): lax.ppermute(x, PLANE, [pair for pair in pairs if pair[0] != pair[1]])]
    add x28 -> x15, other arithmetic: 66.7 us -> 43.7 us  [the longest x6 17.9 us: step(): self.back = [x + y for x, y in zip(middle, more)]]
    ppermute x47 -> x30, waiting for transfers between devices: 159 us -> 178 us  [along(): return lax.ppermute(x, 'rep', pairs)]
    pallas_call x8 -> x4, Pallas kernels: 35.8 us -> 21.6 us  [place(): pl.pallas_call(place_kernel, grid_spec=pltpu.PrefetchScalarGridSpec(num_s...]
    select_n x0 -> x5, other arithmetic: none -> 12.3 us  [the longest x2 7.33 us: step(): mixed = [jnp.where(self.inner, x, y) for x, y in zip(total, chunk)]]
    unnamed x184 -> x149, local copies, waits for them, and re-layouts: 21.5 us -> 27.7 us
  transfers between devices with their start and end apart: 115 -> 96, of which waited for: 38 -> 40; matrix products, arithmetic and copies ran while one was open for 31% -> 29% of each run, Pallas kernels for 6% -> 2%
where the time goes in v5:
time: 866 us; the launch traced here: 854 us
  waiting for transfers between devices  333 us (38%)
  starting transfers between devices  151 us (17%)
  other arithmetic  130 us (15%)
  matrix products  101 us (12%)
  local copies, waits for them, and re-layouts  91 us (11%)
  Pallas kernels  45.7 us (5%)
    ppermute x30, waiting for transfers between devices, along(): return lax.ppermute(x, 'rep', pairs)  178 us
    ppermute x63, waiting for transfers between devices, swap(): return lax.ppermute(x, PLANE, [(i, i ^ mask) for i in range(devices)])  155 us
    ppermute x30, starting transfers between devices, along(): return lax.ppermute(x, 'rep', pairs)  89.9 us
    ppermute x63, starting transfers between devices, swap(): return lax.ppermute(x, PLANE, [(i, i ^ mask) for i in range(devices)])  56.3 us
    dot_general x5, matrix products, outer(): lax.dot_general(left, right, (((0,), (0,)), ((), ())), preferred_element_...  39.8 us
    dot_general x6, matrix products, times_t(): lax.dot_general(left, right, (((1,), (1,)), ((), ())), preferred_element_...  34.3 us
    unnamed x149, local copies, waits for them, and re-layouts  27.7 us
    dot_general x6, matrix products, dot(): return jnp.dot(left, right, preferred_element_type=F32)  26.5 us
  transfers between devices with their start and end apart: 96, of which 40 were waited for; matrix products, arithmetic and copies ran while one was open for 29% of the time, Pallas kernels for 2%

profile of v5, /device:TPU:0, one launch (start us, length us, event | category | flops | bytes accessed | tf_op | source)
XLA Modules:
  0.0 854.2 jit_solution(8336599749745356630)
XLA Ops:
  79.3 11.9 %attend.1 = (bf16[1024,2048]{1,0:T(8,128)(2,1)}, bf16[1024,384]{1,0:T(8,128)(2,1)}, bf16[1024,256]{1,0:T(8,128)(2,1)}, f32[32,128]{1,0:T(8,128)}) custom-call(bf16[2,128,2048]{2,1,0:T(8,128)(2,1)} %copy-done.21, bf16[2,128,2048]{2,1,0:T(8,128)(2,1)} %collective-permute-done.1.refs_1_, bf16[2,128,2048]{2,1,0:T(8,128)(2,1)} %collective-permute-done.2.refs_2_, ...), custom_call_target="tpu_custom_call" | custom-call | flops 1610612736 | bytes 16777216 | tf_op jit(solution)/shard_map/attend/pallas_call | solution.py:157
  123.7 8.3 collective-permute-done.17
  141.2 13.2 %collective-permute-done.32 = bf16[2,128,2048]{2,1,0:T(8,128)(2,1)S(1)} collective-permute-done((bf16[2,128,2048]{2,1,0:T(8,128)(2,1)S(1)}, bf16[2,128,2048]{2,1,0:T(8,128)(2,1)S(1)}, u32[]{:S(2)}, u32[]{:S(2)}) %collective-permute-start.32) | collective-permute-done | bytes 1048608 | tf_op jit(solution)/shard_map/ppermute | solution.py:41
  165.7 10.4 %collective-permute-done.21 = bf16[128,2048]{1,0:T(8,128)(2,1)} collective-permute-done((bf16[128,2048]{1,0:T(8,128)(2,1)S(1)}, bf16[128,2048]{1,0:T(8,128)(2,1)}, u32[]{:S(2)}, u32[]{:S(2)}) %collective-permute-start.21) | collective-permute-done | bytes 524320 | tf_op jit(solution)/shard_map/ppermute | solution.py:41
  183.7 8.4 fusion.9
  196.0 13.6 %collective-permute-done.31 = bf16[2,128,2048]{2,1,0:T(8,128)(2,1)S(1)} collective-permute-done((bf16[2,128,2048]{2,1,0:T(8,128)(2,1)S(1)}, bf16[2,128,2048]{2,1,0:T(8,128)(2,1)S(1)}, u32[]{:S(2)}, u32[]{:S(2)}) %collective-permute-start.31) | collective-permute-done | bytes 1048608 | tf_op jit(solution)/shard_map/ppermute | solution.py:45
  228.8 15.1 %convolution_convert_fusion.2 = bf16[512,2048]{1,0:T(8,128)(2,1)} fusion(bf16[1024,1024]{1,0:T(8,128)(2,1)S(1)} %get-tuple-element.103, bf16[256,2048]{1,0:T(8,128)(2,1)S(1)} %bitcast.178, bf16[256,2048]{1,0:T(8,128)(2,1)S(1)} %bitcast.181, bf16[256,2048]{1,0:T(8,128)(2,1)S(1)} %bitcast.175, bf16[256,2048]{1,0:T(8,128)(2,1)S(1)} %bitcast.141), kind=kOutput, calls=%fused_computation.29 | convolution fusion | flops 2165309440 | bytes 7340032 | tf_op jit(solution)/shard_map/dot_general | solution.py:33
  258.8 8.4 fusion.88
  272.2 10.9 %convolution_convert_fusion = bf16[2048,2048]{1,0:T(8,128)(2,1)S(1)} fusion(bf16[1024,2048]{1,0:T(8,128)(2,1)} %constant_dynamic-update-slice_fusion, bf16[1024,2048]{1,0:T(8,128)(2,1)S(1)} %copy-done.24), kind=kOutput, calls=%fused_computation.3 | convolution fusion | flops 8594128896 | bytes 16777216 | tf_op jit(solution)/shard_map/dot_general | solution.py:33
  286.3 9.2 %collective-permute-done.38 = bf16[128,2048]{1,0:T(8,128)(2,1)} collective-permute-done((bf16[128,2048]{1,0:T(8,128)(2,1)S(1)}, bf16[128,2048]{1,0:T(8,128)(2,1)}, u32[]{:S(2)}, u32[]{:S(2)}) %collective-permute-start.38) | collective-permute-done | bytes 524320 | tf_op jit(solution)/shard_map/ppermute | solution.py:41
  333.6 23.9 %collective-permute-done.49 = bf16[512,2048]{1,0:T(8,128)(2,1)S(1)} collective-permute-done((bf16[512,2048]{1,0:T(8,128)(2,1)S(1)}, bf16[512,2048]{1,0:T(8,128)(2,1)S(1)}, u32[]{:S(2)}, u32[]{:S(2)}) %collective-permute-start.49) | collective-permute-done | bytes 2097184 | tf_op jit(solution)/shard_map/ppermute | solution.py:45
  360.9 12.2 %attend_back.1 = bf16[1024,384]{1,0:T(8,128)(2,1)} custom-call(bf16[1024,384]{1,0:T(8,128)(2,1)} %get-tuple-element.108.refs_0_, f32[1024,128]{1,0:T(8,128)} %get-tuple-element.265.refs_6_.refs_1_, f32[1024,128]{1,0:T(8,128)} %get-tuple-element.264.refs_7_.refs_2_, f32[1024,256]{1,0:T(8,128)} %fusion.42.refs_8_.refs_3_, ...), custom_call_target="tpu_custom_call" | custom-call | flops 805306368 | bytes 4718592 | tf_op jit(solution)/shard_map/attend_back/pallas_call | solution.py:211
  417.4 11.1 %collective-permute-done.55 = bf16[256,2048]{1,0:T(8,128)(2,1)S(1)} collective-permute-done((bf16[256,2048]{1,0:T(8,128)(2,1)}, bf16[256,2048]{1,0:T(8,128)(2,1)S(1)}, u32[]{:S(2)}, u32[]{:S(2)}) %collective-permute-start.55) | collective-permute-done | bytes 1048608 | tf_op jit(solution)/shard_map/ppermute | solution.py:41
  443.0 11.7 %collective-permute-start.63 = (bf16[2,256,2048]{2,1,0:T(8,128)(2,1)}, bf16[2,256,2048]{2,1,0:T(8,128)(2,1)}, u32[]{:S(2)}, u32[]{:S(2)}) collective-permute-start(bf16[2,256,2048]{2,1,0:T(8,128)(2,1)} %pad_maximum_fusion.5), channel_id=1, source_target_pairs={{0,1},{3,2},{4,5},{7,6},{8,9},{11,10},{12,13},{15,14},{16,17},{19,... | collective-permute-start | bytes 6291464 | tf_op jit(solution)/shard_map/ppermute | solution.py:45
  479.9 18.5 %collective-permute-done.61 = bf16[256,2048]{1,0:T(8,128)(2,1)} collective-permute-done((bf16[256,2048]{1,0:T(8,128)(2,1)}, bf16[256,2048]{1,0:T(8,128)(2,1)}, u32[]{:S(2)}, u32[]{:S(2)}) %collective-permute-start.61) | collective-permute-done | bytes 1048608 | tf_op jit(solution)/shard_map/ppermute | solution.py:41
  499.4 7.8 collective-permute-done.64
  513.8 9.5 %collective-permute-start.66 = (bf16[2,256,2048]{2,1,0:T(8,128)(2,1)S(1)}, bf16[2,256,2048]{2,1,0:T(8,128)(2,1)S(1)}, u32[]{:S(2)}, u32[]{:S(2)}) collective-permute-start(bf16[2,256,2048]{2,1,0:T(8,128)(2,1)S(1)} %add_select_fusion.1.sum_ref), channel_id=1, source_target_pairs={{0,1},{3,2},{1,0},{2,3},{4,5},{7,6},{5,4},{6,7},{8,9},{11,10},{9,8... | collective-permute-start | bytes 6291464 | tf_op jit(solution)/shard_map/ppermute | solution.py:45
  530.8 8.4 collective-permute-done.68
  557.1 14.9 %collective-permute-done.71 = bf16[256,2048]{1,0:T(8,128)(2,1)S(1)} collective-permute-done((bf16[256,2048]{1,0:T(8,128)(2,1)S(1)}, bf16[256,2048]{1,0:T(8,128)(2,1)S(1)}, u32[]{:S(2)}, u32[]{:S(2)}) %collective-permute-start.71) | collective-permute-done | bytes 1048608 | tf_op jit(solution)/shard_map/ppermute | solution.py:41
  617.1 17.1 %collective-permute-done.73 = bf16[256,2048]{1,0:T(8,128)(2,1)} collective-permute-done((bf16[256,2048]{1,0:T(8,128)(2,1)}, bf16[256,2048]{1,0:T(8,128)(2,1)}, u32[]{:S(2)}, u32[]{:S(2)}) %collective-permute-start.73) | collective-permute-done | bytes 1048608 | tf_op jit(solution)/shard_map/ppermute | solution.py:45
  666.8 24.7 %collective-permute-done.81.copy_ref = bf16[2,256,2048]{2,1,0:T(8,128)(2,1)} collective-permute-done((bf16[2,256,2048]{2,1,0:T(8,128)(2,1)}, bf16[2,256,2048]{2,1,0:T(8,128)(2,1)}, u32[]{:S(2)}, u32[]{:S(2)}) %collective-permute-start.81) | collective-permute-done | bytes 2097184 | tf_op jit(solution)/shard_map/ppermute | solution.py:45
  709.2 32.6 %collective-permute-done.85 = bf16[256,2048]{1,0:T(8,128)(2,1)} collective-permute-done((bf16[256,2048]{1,0:T(8,128)(2,1)}, bf16[256,2048]{1,0:T(8,128)(2,1)}, u32[]{:S(2)}, u32[]{:S(2)}) %collective-permute-start.85) | collective-permute-done | bytes 1048608 | tf_op jit(solution)/shard_map/ppermute | solution.py:45
  744.2 30.4 %collective-permute-done.86 = bf16[8,256,384]{2,1,0:T(8,128)(2,1)} collective-permute-done((bf16[8,256,384]{2,1,0:T(8,128)(2,1)}, bf16[8,256,384]{2,1,0:T(8,128)(2,1)}, u32[]{:S(2)}, u32[]{:S(2)}) %collective-permute-start.86) | collective-permute-done | bytes 1572896 | tf_op jit(solution)/shard_map/ppermute | solution.py:45
  834.9 13.4 %collective-permute-done.95.copy_ref = bf16[2,256,2048]{2,1,0:T(8,128)(2,1)} collective-permute-done((bf16[2,256,2048]{2,1,0:T(8,128)(2,1)}, bf16[2,256,2048]{2,1,0:T(8,128)(2,1)}, u32[]{:S(2)}, u32[]{:S(2)}) %collective-permute-start.95) | collective-permute-done | bytes 2097184 | tf_op jit(solution)/shard_map/ppermute | solution.py:45
  (504 shorter events, 506.2 us)
Async XLA Ops:
  139.9 41.5 %collective-permute-start.28 = (bf16[2,128,2048]{2,1,0:T(8,128)(2,1)}, bf16[2,128,2048]{2,1,0:T(8,128)(2,1)S(1)}, u32[]{:S(2)}, u32[]{:S(2)}) collective-permute-start(bf16[2,128,2048]{2,1,0:T(8,128)(2,1)} %collective-permute-done.27), channel_id=1, source_target_pairs={{1,0},{2,1},{5,4},{6,5},{9,8},{10,9},{13,12},{14,13},{17,16},{18,1... | collective-permute-start | bytes 3145736 | tf_op jit(solution)/shard_map/ppermute | solution.py:45
  250.0 52.7 %collective-permute-start.35 = (bf16[512,2048]{1,0:T(8,128)(2,1)}, bf16[512,2048]{1,0:T(8,128)(2,1)}, u32[]{:S(2)}, u32[]{:S(2)}) collective-permute-start(bf16[512,2048]{1,0:T(8,128)(2,1)} %convolution_convert_fusion.2), channel_id=1, source_target_pairs={{0,1},{3,2},{4,5},{7,6},{8,9},{11,10},{12,13},{15,14},{16,17},{19,... | collective-permute-start | bytes 6291464 | tf_op jit(solution)/shard_map/ppermute | solution.py:45
  313.1 44.4 %collective-permute-start.49 = (bf16[512,2048]{1,0:T(8,128)(2,1)S(1)}, bf16[512,2048]{1,0:T(8,128)(2,1)S(1)}, u32[]{:S(2)}, u32[]{:S(2)}) collective-permute-start(bf16[512,2048]{1,0:T(8,128)(2,1)S(1)} %convolution_convert_fusion.1), channel_id=1, source_target_pairs={{0,1},{3,2},{4,5},{7,6},{8,9},{11,10},{12,13},{15,14},{16,17},{19,... | collective-permute-start | bytes 6291464 | tf_op jit(solution)/shard_map/ppermute | solution.py:45
  315.7 41.9 %collective-permute-start.50 = (bf16[512,2048]{1,0:T(8,128)(2,1)S(1)}, bf16[512,2048]{1,0:T(8,128)(2,1)S(1)}, u32[]{:S(2)}, u32[]{:S(2)}) collective-permute-start(bf16[512,2048]{1,0:T(8,128)(2,1)S(1)} %add.585), channel_id=1, source_target_pairs={{1,2},{2,1},{5,6},{6,5},{9,10},{10,9},{13,14},{14,13},{17,18},{18,... | collective-permute-start | bytes 6291464 | tf_op jit(solution)/shard_map/ppermute | solution.py:45
  379.0 50.5 %collective-permute-start.51 = (bf16[2,256,2048]{2,1,0:T(8,128)(2,1)}, bf16[2,256,2048]{2,1,0:T(8,128)(2,1)}, u32[]{:S(2)}, u32[]{:S(2)}) collective-permute-start(bf16[2,256,2048]{2,1,0:T(8,128)(2,1)} %pad_maximum_fusion.3), channel_id=1, source_target_pairs={{0,1},{3,2},{4,5},{7,6},{8,9},{11,10},{12,13},{15,14},{16,17},{19,... | collective-permute-start | bytes 6291464 | tf_op jit(solution)/shard_map/ppermute | solution.py:45
  385.8 50.0 %collective-permute-start.52 = (bf16[512,2048]{1,0:T(8,128)(2,1)S(1)}, bf16[512,2048]{1,0:T(8,128)(2,1)}, u32[]{:S(2)}, u32[]{:S(2)}) collective-permute-start(bf16[512,2048]{1,0:T(8,128)(2,1)S(1)} %add.587), channel_id=1, source_target_pairs={{1,0},{2,3},{5,4},{6,7},{9,8},{10,11},{13,12},{14,15},{17,16},{18,... | collective-permute-start | bytes 6291464 | tf_op jit(solution)/shard_map/ppermute | solution.py:45
  389.5 46.3 %collective-permute-start.53 = (bf16[512,2048]{1,0:T(8,128)(2,1)}, bf16[512,2048]{1,0:T(8,128)(2,1)}, u32[]{:S(2)}, u32[]{:S(2)}) collective-permute-start(bf16[512,2048]{1,0:T(8,128)(2,1)} %add.588), channel_id=1, source_target_pairs={{1,2},{2,1},{5,6},{6,5},{9,10},{10,9},{13,14},{14,13},{17,18},{18,... | collective-permute-start | bytes 6291464 | tf_op jit(solution)/shard_map/ppermute | solution.py:45
  443.0 56.4 %collective-permute-start.63 = (bf16[2,256,2048]{2,1,0:T(8,128)(2,1)}, bf16[2,256,2048]{2,1,0:T(8,128)(2,1)}, u32[]{:S(2)}, u32[]{:S(2)}) collective-permute-start(bf16[2,256,2048]{2,1,0:T(8,128)(2,1)} %pad_maximum_fusion.5), channel_id=1, source_target_pairs={{0,1},{3,2},{4,5},{7,6},{8,9},{11,10},{12,13},{15,14},{16,17},{19,... | collective-permute-start | bytes 6291464 | tf_op jit(solution)/shard_map/ppermute | solution.py:45
  459.2 48.1 %collective-permute-start.64 = (bf16[512,2048]{1,0:T(8,128)(2,1)}, bf16[512,2048]{1,0:T(8,128)(2,1)}, u32[]{:S(2)}, u32[]{:S(2)}) collective-permute-start(bf16[512,2048]{1,0:T(8,128)(2,1)} %add.594), channel_id=1, source_target_pairs={{1,0},{2,3},{5,4},{6,7},{9,8},{10,11},{13,12},{14,15},{17,16},{18,... | collective-permute-start | bytes 6291464 | tf_op jit(solution)/shard_map/ppermute | solution.py:45
  465.0 42.2 %collective-permute-start.57 = (bf16[2,256,2048]{2,1,0:T(8,128)(2,1)}, bf16[2,256,2048]{2,1,0:T(8,128)(2,1)}, u32[]{:S(2)}, u32[]{:S(2)}) collective-permute-start(bf16[2,256,2048]{2,1,0:T(8,128)(2,1)} %add.586), channel_id=1, source_target_pairs={{1,2},{2,1},{5,6},{6,5},{9,10},{10,9},{13,14},{14,13},{17,18},{18,... | collective-permute-start | bytes 6291464 | tf_op jit(solution)/shard_map/ppermute | solution.py:45
  513.8 58.2 %collective-permute-start.66 = (bf16[2,256,2048]{2,1,0:T(8,128)(2,1)S(1)}, bf16[2,256,2048]{2,1,0:T(8,128)(2,1)S(1)}, u32[]{:S(2)}, u32[]{:S(2)}) collective-permute-start(bf16[2,256,2048]{2,1,0:T(8,128)(2,1)S(1)} %add_select_fusion.1.sum_ref), channel_id=1, source_target_pairs={{0,1},{3,2},{1,0},{2,3},{4,5},{7,6},{5,4},{6,7},{8,9},{11,10},{9,8... | collective-permute-start | bytes 6291464 | tf_op jit(solution)/shard_map/ppermute | solution.py:45
  526.3 45.6 %collective-permute-start.67 = (bf16[2,256,2048]{2,1,0:T(8,128)(2,1)S(1)}, bf16[2,256,2048]{2,1,0:T(8,128)(2,1)S(1)}, u32[]{:S(2)}, u32[]{:S(2)}) collective-permute-start(bf16[2,256,2048]{2,1,0:T(8,128)(2,1)S(1)} %add.595), channel_id=1, source_target_pairs={{1,2},{2,1},{5,6},{6,5},{9,10},{10,9},{13,14},{14,13},{17,18},{18,... | collective-permute-start | bytes 6291464 | tf_op jit(solution)/shard_map/ppermute | solution.py:45
  549.4 48.8 %collective-permute-start.84 = (f32[3,2048]{1,0:T(4,128)S(1)}, f32[3,2048]{1,0:T(4,128)S(1)}, u32[]{:S(2)}, u32[]{:S(2)}) collective-permute-start(f32[3,2048]{1,0:T(4,128)S(1)} %pad_maximum_fusion.21), channel_id=1, source_target_pairs={{0,1},{3,2},{4,5},{7,6},{8,9},{11,10},{12,13},{15,14},{16,17},{19,... | collective-permute-start | bytes 73736 | tf_op jit(solution)/shard_map/ppermute | solution.py:45
  572.0 41.7 %collective-permute-start.74 = (bf16[8,256,384]{2,1,0:T(8,128)(2,1)}, bf16[8,256,384]{2,1,0:T(8,128)(2,1)}, u32[]{:S(2)}, u32[]{:S(2)}) collective-permute-start(bf16[8,256,384]{2,1,0:T(8,128)(2,1)} %constant_dynamic-update-slice_fusion.16), channel_id=1, source_target_pairs={{0,1},{3,2},{4,5},{7,6},{8,9},{11,10},{12,13},{15,14},{16,17},{19,... | collective-permute-start | bytes 4718600 | tf_op jit(solution)/shard_map/ppermute | solution.py:45
  581.8 52.3 %collective-permute-start.75 = (bf16[2,256,2048]{2,1,0:T(8,128)(2,1)}, bf16[2,256,2048]{2,1,0:T(8,128)(2,1)}, u32[]{:S(2)}, u32[]{:S(2)}) collective-permute-start(bf16[2,256,2048]{2,1,0:T(8,128)(2,1)} %add.600.sum_ref), channel_id=1, source_target_pairs={{1,0},{2,3},{5,4},{6,7},{9,8},{10,11},{13,12},{14,15},{17,16},{18,... | collective-permute-start | bytes 6291464 | tf_op jit(solution)/shard_map/ppermute | solution.py:45
  586.4 47.8 %collective-permute-start.76 = (bf16[2,256,2048]{2,1,0:T(8,128)(2,1)}, bf16[2,256,2048]{2,1,0:T(8,128)(2,1)}, u32[]{:S(2)}, u32[]{:S(2)}) collective-permute-start(bf16[2,256,2048]{2,1,0:T(8,128)(2,1)} %fusion.22), channel_id=1, source_target_pairs={{1,2},{2,1},{5,6},{6,5},{9,10},{10,9},{13,14},{14,13},{17,18},{18,... | collective-permute-start | bytes 6291464 | tf_op jit(solution)/shard_map/ppermute | solution.py:45
  591.5 42.7 %collective-permute-start.73 = (bf16[256,2048]{1,0:T(8,128)(2,1)}, bf16[256,2048]{1,0:T(8,128)(2,1)}, u32[]{:S(2)}, u32[]{:S(2)}) collective-permute-start(bf16[256,2048]{1,0:T(8,128)(2,1)} %convolution_convert_fusion.7), channel_id=1, source_target_pairs={{0,1},{3,2},{4,5},{7,6},{8,9},{11,10},{12,13},{15,14},{16,17},{19,... | collective-permute-start | bytes 3145736 | tf_op jit(solution)/shard_map/ppermute | solution.py:45
  640.4 51.1 %collective-permute-start.81 = (bf16[2,256,2048]{2,1,0:T(8,128)(2,1)}, bf16[2,256,2048]{2,1,0:T(8,128)(2,1)}, u32[]{:S(2)}, u32[]{:S(2)}) collective-permute-start(bf16[2,256,2048]{2,1,0:T(8,128)(2,1)} %add_select_fusion.sum_ref), channel_id=1, source_target_pairs={{0,1},{3,2},{1,0},{2,3},{4,5},{7,6},{5,4},{6,7},{8,9},{11,10},{9,8... | collective-permute-start | bytes 6291464 | tf_op jit(solution)/shard_map/ppermute | solution.py:45
  650.9 43.2 %collective-permute-start.90 = (f32[3,2048]{1,0:T(4,128)S(1)}, f32[3,2048]{1,0:T(4,128)S(1)}, u32[]{:S(2)}, u32[]{:S(2)}) collective-permute-start(f32[3,2048]{1,0:T(4,128)S(1)} %pad_maximum_fusion.22), channel_id=1, source_target_pairs={{1,0},{2,3},{5,4},{6,7},{9,8},{10,11},{13,12},{14,15},{17,16},{18,... | collective-permute-start | bytes 73736 | tf_op jit(solution)/shard_map/ppermute | solution.py:45
  691.5 50.3 %collective-permute-start.85 = (bf16[256,2048]{1,0:T(8,128)(2,1)}, bf16[256,2048]{1,0:T(8,128)(2,1)}, u32[]{:S(2)}, u32[]{:S(2)}) collective-permute-start(bf16[256,2048]{1,0:T(8,128)(2,1)} %add.610), channel_id=1, source_target_pairs={{1,0},{2,3},{5,4},{6,7},{9,8},{10,11},{13,12},{14,15},{17,16},{18,... | collective-permute-start | bytes 3145736 | tf_op jit(solution)/shard_map/ppermute | solution.py:45
  692.8 81.7 %collective-permute-start.86 = (bf16[8,256,384]{2,1,0:T(8,128)(2,1)}, bf16[8,256,384]{2,1,0:T(8,128)(2,1)}, u32[]{:S(2)}, u32[]{:S(2)}) collective-permute-start(bf16[8,256,384]{2,1,0:T(8,128)(2,1)} %add.620), channel_id=1, source_target_pairs={{1,0},{2,3},{5,4},{6,7},{9,8},{10,11},{13,12},{14,15},{17,16},{18,... | collective-permute-start | bytes 4718600 | tf_op jit(solution)/shard_map/ppermute | solution.py:45
  696.5 95.2 %collective-permute-start.88 = (bf16[512,2048]{1,0:T(8,128)(2,1)}, bf16[512,2048]{1,0:T(8,128)(2,1)}, u32[]{:S(2)}, u32[]{:S(2)}) collective-permute-start(bf16[512,2048]{1,0:T(8,128)(2,1)} %broadcast_select_fusion), channel_id=1, source_target_pairs={{4,8},{8,16},{12,24},{16,4},{20,12},{24,20},{5,9},{9,17},{13,25},{... | collective-permute-start | bytes 6291464 | tf_op jit(solution)/shard_map/ppermute | solution.py:458
  701.9 91.4 %collective-permute-start.87 = (bf16[2,256,2048]{2,1,0:T(8,128)(2,1)}, bf16[2,256,2048]{2,1,0:T(8,128)(2,1)}, u32[]{:S(2)}, u32[]{:S(2)}) collective-permute-start(bf16[2,256,2048]{2,1,0:T(8,128)(2,1)} %fusion.21), channel_id=1, source_target_pairs={{1,2},{2,1},{5,6},{6,5},{9,10},{10,9},{13,14},{14,13},{17,18},{18,... | collective-permute-start | bytes 6291464 | tf_op jit(solution)/shard_map/ppermute | solution.py:45
  797.9 50.4 %collective-permute-start.95 = (bf16[2,256,2048]{2,1,0:T(8,128)(2,1)}, bf16[2,256,2048]{2,1,0:T(8,128)(2,1)}, u32[]{:S(2)}, u32[]{:S(2)}) collective-permute-start(bf16[2,256,2048]{2,1,0:T(8,128)(2,1)} %add.644.sum_ref), channel_id=1, source_target_pairs={{1,0},{2,3},{5,4},{6,7},{9,8},{10,11},{13,12},{14,15},{17,16},{18,... | collective-permute-start | bytes 6291464 | tf_op jit(solution)/shard_map/ppermute | solution.py:45
  (137 other events, 2280.4 us)
